TPU v7x, 32 devices: a whole 2x2x4 slice. The times are simulated.
32 devices in a mesh: ha: 8 (over z, core), wa: 4 (over y, x).
Axes of the slice: x: 2, y: 2, z: 4, core: 2. Of those that a mesh axis runs over, the one named last changes fastest.
Arguments:
- inputs: bfloat16 [32, 256, 512], P('ha', 'wa'), may hold values from -6 to 6
- grad_out: bfloat16 [32, 256, 512], P('ha', 'wa'), may hold values from -6 to 6
- kernel_one: bfloat16 [27, 64, 64], replicated, may hold values from -0.15625 to 0.15625
- kernel_two: bfloat16 [27, 64, 64], replicated, may hold values from -0.15625 to 0.15625
Outputs:
- grad_inputs: bfloat16 [32, 256, 512], P('ha', 'wa')
- grad_kernel_one: float32 [110592], P(('ha', 'wa'))
- grad_kernel_two: float32 [110592], P(('ha', 'wa'))
All inputs are finite; a program needn't handle non-finite values.
Results may differ from a plain program's by a relative error of at most 0.0049.
Values may be sent and summed in bfloat16 or wider, within the bound.
No kernel may reach another device: no remote copies, remote signals or barrier semaphores. Data moves between devices by JAX's collectives and lax.ppermute only.
A program may use at most 64 MiB of HBM per device.

v0:
```python
import jax
import jax.numpy as jnp
from jax import lax
from jax.sharding import PartitionSpec as P

CH = 64


root_half = 0.7071067811865476
inv_root_two_pi = 0.3989422804014327


def extended_2(block, sides, width):
    for axis, dim in sides:
        count = lax.axis_size(axis)
        forward = [(i, i + 1) for i in range(count - 1)]
        backward = [(target, source) for source, target in forward]
        low = lax.ppermute(
            lax.slice_in_dim(block, block.shape[dim] - width, None, axis=dim), axis, forward
        )
        high = lax.ppermute(lax.slice_in_dim(block, 0, width, axis=dim), axis, backward)
        block = jnp.concatenate([low, block, high], axis=dim)
    return block


def gelu_value(values):
    return 0.5 * values * (1.0 + jax.scipy.special.erf(values * root_half))


def gelu_slope(values):
    return 0.5 * (
        1.0 + jax.scipy.special.erf(values * root_half)
    ) + values * inv_root_two_pi * jnp.exp(-0.5 * values * values)


def flip_kernel(kernel):
    return jnp.swapaxes(kernel[::-1], 1, 2)


def correlate(extended, kernel):
    chans_in = kernel.shape[1]
    chans_out = kernel.shape[2]
    taps = kernel.reshape(3, 3, 3, chans_in, chans_out)
    result = lax.conv_general_dilated(
        extended[None],
        taps,
        (1, 1, 1),
        ((0, 0), (0, 0), (1, 1)),
        dimension_numbers=("NDHWC", "DHWIO", "NDHWC"),
        preferred_element_type=jnp.float32,
    )
    return result[0]


def kernel_grad(extended, cotangent):
    chans_in = extended.shape[-1]
    chans_out = cotangent.shape[-1]
    result = lax.conv_general_dilated(
        extended[None],
        cotangent[:, :, :, None, :],
        (1, 1, 1),
        ((0, 0), (0, 0), (1, 1)),
        dimension_numbers=("CDHWN", "DHWIO", "NDHWC"),
        preferred_element_type=jnp.float32,
    )
    return jnp.transpose(result, (1, 2, 3, 0, 4)).reshape(27, chans_in, chans_out)


def shards(inputs, grad_out, kernel_one, kernel_two):
    rows_here, cols_here, merged = inputs.shape
    depth_cells = merged // CH
    volume = inputs.reshape(rows_here, cols_here, depth_cells, CH)
    cotangent = grad_out.reshape(rows_here, cols_here, depth_cells, CH)
    both_fields = jnp.concatenate([volume, cotangent], axis=-1)
    both_ext = extended_2(both_fields, (("ha", 0), ("wa", 1)), 1)
    input_ext = both_ext[..., :CH]
    cot_ext = both_ext[..., CH:]
    pre_active = correlate(input_ext, kernel_one)
    active = gelu_value(pre_active).astype(jnp.bfloat16)
    active_ext = extended_2(active, (("ha", 0), ("wa", 1)), 1)
    grad_active = correlate(cot_ext, flip_kernel(kernel_two))
    grad_pre = (grad_active * gelu_slope(pre_active)).astype(jnp.bfloat16)
    grad_ext = extended_2(grad_pre, (("ha", 0), ("wa", 1)), 1)
    kernel_two_part = kernel_grad(active_ext, cotangent)
    kernel_one_part = kernel_grad(input_ext, grad_pre)
    grad_inputs = (
        correlate(grad_ext, flip_kernel(kernel_one))
        .astype(jnp.bfloat16)
        .reshape(rows_here, cols_here, merged)
    )
    height_count = lax.axis_size("ha")
    width_count = lax.axis_size("wa")
    first_part = kernel_one_part.reshape(height_count, width_count, -1)
    second_part = kernel_two_part.reshape(height_count, width_count, -1)
    first_part, second_part = (
        lax.psum_scatter(first_part, "wa", scatter_dimension=1, tiled=True),
        lax.psum_scatter(second_part, "wa", scatter_dimension=1, tiled=True),
    )
    first_part, second_part = (
        lax.psum_scatter(first_part, "ha", scatter_dimension=0, tiled=True),
        lax.psum_scatter(second_part, "ha", scatter_dimension=0, tiled=True),
    )
    grad_kernel_one = first_part.reshape(-1)
    grad_kernel_two = second_part.reshape(-1)
    return (grad_inputs, grad_kernel_one, grad_kernel_two)


def solution(mesh):
    return jax.shard_map(
        shards,
        mesh=mesh,
        in_specs=(P("ha", "wa", None), P("ha", "wa", None), P(), P()),
        out_specs=(P("ha", "wa", None), P(("ha", "wa")), P(("ha", "wa"))),
        check_vma=False,
    )
```

profile of v0, /device:TPU:0, one launch (start us, length us, event | category | flops | bytes accessed | tf_op | source)
XLA Modules:
  0.0 224.8 jit_solution(2507443990350639203)
XLA Ops:
  7.2 0.0 reduce-scatter.7.cloned.1.call-start
  7.2 1.2 copy.29
  8.4 1.2 copy.28
  9.7 0.1 pad_maximum_fusion.3
  9.8 1.3 collective-permute-start.1
  11.1 3.0 %collective-permute-start = (bf16[1,64,8,128]{1,3,2,0:T(8,128)(2,1)S(1)}, bf16[1,64,8,128]{1,3,2,0:T(8,128)(2,1)S(1)}, u32[]{:S(2)}, u32[]{:S(2)}) collective-permute-start(bf16[1,64,8,128]{1,3,2,0:T(8,128)(2,1)S(1)} %get-tuple-element.11), channel_id=1, source_target_pairs={{0,4},{4,8},{8,12},{12,16},{16,20},{20,24},{24,28},{1,5},{5,9},{9,... | collective-permute-start | bytes 393224 | tf_op jit(solution)/shard_map/ppermute | solution.py:18
  14.2 1.1 collective-permute-done
  15.3 0.4 pad_maximum_fusion
  15.7 1.9 fusion.22
  17.6 1.8 copy.31
  19.4 1.3 collective-permute-start.3
  20.7 0.7 copy.30
  21.4 6.0 %collective-permute-start.2 = (bf16[6,1,8,128]{3,2,1,0:T(8,128)(2,1)S(1)}, bf16[6,1,8,128]{3,2,1,0:T(8,128)(2,1)S(1)}, u32[]{:S(2)}, u32[]{:S(2)}) collective-permute-start(bf16[6,1,8,128]{3,2,1,0:T(8,128)(2,1)S(1)} %copy.30), channel_id=1, source_target_pairs={{0,1},{1,2},{2,3},{4,5},{5,6},{6,7},{8,9},{9,10},{10,11},{12,13},{... | collective-permute-start | bytes 36872 | tf_op jit(solution)/shard_map/ppermute | solution.py:18
  27.4 1.9 broadcast_in_dim_reshape.4
  29.4 1.8 rev.6
  31.2 1.0 copy.33
  32.1 1.6 copy.32
  33.8 2.8 %pad_maximum_fusion.1 = bf16[6,66,8,128]{1,3,2,0:T(8,128)(2,1)S(1)} fusion(bf16[6,1,8,128]{1,3,2,0:T(8,128)(2,1)S(1)} %copy.33, bf16[1,64,8,128]{1,3,2,0:T(8,128)(2,1)S(1)} %collective-permute-done.1, bf16[4,64,8,64]{1,3,2,0:T(8,128)(2,1)S(1)} %bitcast.38, bf16[4,64,8,64]{1,3,2,0:T(8,128)(2,1)S(1)} %bitcast.41, ...), kind=kLoop, calls=%fused_computation.5 | loop fusion | flops 4866048 | bytes 1622016 | tf_op jit(solution)/shard_map/concatenate | solution.py:22
  36.6 0.2 slice_bitcast_fusion
  36.8 1.7 copy.35
  38.5 0.0 copy-start.10
  38.5 3.3 %copy.34 = bf16[1,6,66,8,64]{4,0,3,2,1:T(2,128)(2,1)} copy(bf16[1,6,66,8,64]{2,4,3,1,0:T(8,128)(2,1)S(1)} %get-tuple-element.6) | data formatting | bytes 811008 | tf_op jit(solution)/shard_map/broadcast_in_dim | solution.py:45
  41.8 7.8 %fusion.26 = f32[1,4,64,8,64]{4,0,3,2,1:T(1,128)S(1)} fusion(bf16[1,6,66,8,64]{4,0,3,2,1:T(2,128)(2,1)S(1)} %copy.35, bf16[3,3,3,64,64]{4,3,2,1,0:T(8,128)(2,1)S(1)} %bitcast.46), kind=kOutput, calls=%fused_computation.42 | convolution fusion | flops 415236096 | bytes 1150976 | tf_op jit(solution)/shard_map/conv_general_dilated | solution.py:44
  49.7 21.7 %fusion.25 = f32[1,4,64,8,64]{4,0,3,2,1:T(1,128)S(1)} fusion(bf16[1,6,66,8,64]{4,0,3,2,1:T(2,128)(2,1)S(1)} %copy-done.3, bf16[3,3,3,64,64]{3,4,2,1,0:T(8,128)(2,1)S(1)} %bitcast.48), kind=kOutput, calls=%fused_computation.41 | convolution fusion | flops 415236096 | bytes 1150976 | tf_op jit(solution)/shard_map/conv_general_dilated | solution.py:44
  71.4 1.4 multiply_convert_fusion
  72.7 1.3 collective-permute-start.9
  74.0 5.9 %collective-permute-start.8 = (bf16[1,64,8,64]{3,2,1,0:T(8,128)(2,1)S(1)}, bf16[1,64,8,64]{3,2,1,0:T(8,128)(2,1)S(1)}, u32[]{:S(2)}, u32[]{:S(2)}) collective-permute-start(bf16[1,64,8,64]{3,2,1,0:T(8,128)(2,1)S(1)} %get-tuple-element.17), channel_id=1, source_target_pairs={{0,4},{4,8},{8,12},{12,16},{16,20},{20,24},{24,28},{1,5},{5,9},{9,... | collective-permute-start | bytes 196616 | tf_op jit(solution)/shard_map/ppermute | solution.py:18
  79.9 0.4 fusion.19
  80.4 0.0 copy-start.6
  80.4 0.5 collective-permute-done.8
  80.9 0.6 pad_maximum_fusion.6
  81.5 1.3 collective-permute-start.11
  82.8 5.9 %collective-permute-start.10 = (bf16[6,1,8,64]{3,2,1,0:T(8,128)(2,1)}, bf16[6,1,8,64]{3,2,1,0:T(8,128)(2,1)}, u32[]{:S(2)}, u32[]{:S(2)}) collective-permute-start(bf16[6,1,8,64]{3,2,1,0:T(8,128)(2,1)} %get-tuple-element.13), channel_id=1, source_target_pairs={{0,1},{1,2},{2,3},{4,5},{5,6},{6,7},{8,9},{9,10},{10,11},{12,13},{... | collective-permute-start | bytes 18440 | tf_op jit(solution)/shard_map/ppermute | solution.py:18
  88.7 12.8 %fusion.20 = f32[3,3,3,64,64]{4,3,2,1,0:T(8,128)S(1)} fusion(bf16[1,6,66,8,64]{4,0,3,2,1:T(2,128)(2,1)S(1)} %copy.35, bf16[4,64,8,1,64]{4,2,1,0,3:T(8,128)(2,1)S(1)} %fusion.19), kind=kOutput, calls=%fused_computation.22 | convolution fusion | flops 415236096 | bytes 1110016 | tf_op jit(solution)/shard_map/transpose | solution.py:66
  101.6 0.0 copy-start.7
  101.6 0.3 reshape_reshape.6
  101.9 0.8 copy.39
  102.7 0.0 reduce-scatter.7.cloned.1.call-update
  102.7 0.2 reduce-scatter.9.cloned.1.call-start
  103.0 1.0 maximum_bitcast_fusion.1
  104.0 12.6 %fusion = f32[3,3,3,64,64]{4,3,2,1,0:T(8,128)S(1)} fusion(bf16[4,64,8,1,64]{4,3,2,1,0:T(2,128)(2,1)S(1)} %copy-done.5, bf16[1,6,66,8,64]{4,3,2,1,0:T(8,128)(2,1)S(1)} %maximum_bitcast_fusion.1), kind=kOutput, calls=%fused_computation | convolution fusion | flops 415236096 | bytes 1110016 | tf_op jit(solution)/shard_map/transpose | solution.py:66
  116.6 0.3 reshape_reshape.7
  117.0 0.0 copy-start.11
  117.0 0.0 copy-start.13
  117.0 0.8 copy.43
  117.8 0.0 reduce-scatter.9.cloned.1.call-update
  117.8 0.3 all-reduce.7.cloned.1.call-start
  118.1 1.3 collective-permute-start.5
  119.4 6.3 %collective-permute-start.4 = (bf16[1,64,8,64]{3,2,1,0:T(8,128)(2,1)S(1)}, bf16[1,64,8,64]{3,2,1,0:T(8,128)(2,1)S(1)}, u32[]{:S(2)}, u32[]{:S(2)}) collective-permute-start(bf16[1,64,8,64]{3,2,1,0:T(8,128)(2,1)S(1)} %get-tuple-element.19), channel_id=1, source_target_pairs={{0,4},{4,8},{8,12},{12,16},{16,20},{20,24},{24,28},{1,5},{5,9},{9,... | collective-permute-start | bytes 196616 | tf_op jit(solution)/shard_map/ppermute | solution.py:18
  125.7 1.0 collective-permute-done.4
  126.6 1.3 collective-permute-start.7
  127.9 4.6 %collective-permute-start.6 = (bf16[6,1,8,64]{3,2,1,0:T(8,128)(2,1)S(1)}, bf16[6,1,8,64]{3,2,1,0:T(8,128)(2,1)S(1)}, u32[]{:S(2)}, u32[]{:S(2)}) collective-permute-start(bf16[6,1,8,64]{3,2,1,0:T(8,128)(2,1)S(1)} %get-tuple-element.15), channel_id=1, source_target_pairs={{0,1},{1,2},{2,3},{4,5},{5,6},{6,7},{8,9},{9,10},{10,11},{12,13},{... | collective-permute-start | bytes 18440 | tf_op jit(solution)/shard_map/ppermute | solution.py:18
  132.6 0.6 dynamic-slice.2
  133.3 0.7 collective-permute-done.6
  133.9 0.3 maximum_bitcast_fusion
  134.2 0.0 reduce-scatter.7.cloned.1.call-done
  134.2 1.7 copy.40
  135.9 24.7 %reduce-scatter.9.cloned.1.call-done = f32[8,1,3456]{2,0,1:T(8,128)} async-done(((f32[8,4,3456]{2,0,1:T(8,128)}), f32[8,1,3456]{2,0,1:T(8,128)}) %reduce-scatter.9.cloned.1.call-update) | async-done | bytes 110608
  160.6 1.7 copy.44
  162.3 0.0 all-reduce.7.cloned.1.call-update
  162.3 23.8 %fusion.7 = bf16[4,64,8,64]{3,2,1,0:T(8,128)(2,1)S(1)} fusion(bf16[3,3,3,64,64]{3,4,2,1,0:T(8,128)(2,1)S(1)} %bitcast.47, bf16[1,6,66,8,64]{4,3,2,1,0:T(8,128)(2,1)S(1)} %maximum_bitcast_fusion), kind=kOutput, calls=%fused_computation.9 | convolution fusion | flops 415367168 | bytes 888832 | tf_op jit(solution)/shard_map/conv_general_dilated | solution.py:44
  186.1 1.0 convert_element_type.24
  187.2 28.8 %all-reduce.7.cloned.1.call-done = (f32[8,1,3456]{2,1,0:T(1,128)}, f32[8,1,3456]{2,1,0:T(1,128)}) async-done(((f32[8,1,3456]{2,1,0:T(1,128)}, f32[8,1,3456]{2,1,0:T(1,128)}), (f32[8,1,3456]{2,1,0:T(1,128)}, f32[8,1,3456]{2,1,0:T(1,128)})) %all-reduce.7.cloned.1.call-update) | async-done | bytes 221200
  216.0 2.1 dynamic-slice_reduce_fusion
  (35 shorter events, 0.1 us)
Async XLA Ops:
  7.2 127.1 %reduce-scatter.7.cloned.1.call-start = ((), (), s32[]{:S(2)}) async-start(), calls=%async_computation.2 | async-start | bytes 552960
  9.8 4.4 %collective-permute-start.1 = (bf16[1,64,8,128]{1,3,2,0:T(8,128)(2,1)S(1)}, bf16[1,64,8,128]{1,3,2,0:T(8,128)(2,1)S(1)}, u32[]{:S(2)}, u32[]{:S(2)}) collective-permute-start(bf16[1,64,8,128]{1,3,2,0:T(8,128)(2,1)S(1)} %get-tuple-element.12), channel_id=1, source_target_pairs={{4,0},{8,4},{12,8},{16,12},{20,16},{24,20},{28,24},{5,1},{9,5},{13... | collective-permute-start | bytes 393224 | tf_op jit(solution)/shard_map/ppermute | solution.py:21
  11.1 4.2 %collective-permute-start = (bf16[1,64,8,128]{1,3,2,0:T(8,128)(2,1)S(1)}, bf16[1,64,8,128]{1,3,2,0:T(8,128)(2,1)S(1)}, u32[]{:S(2)}, u32[]{:S(2)}) collective-permute-start(bf16[1,64,8,128]{1,3,2,0:T(8,128)(2,1)S(1)} %get-tuple-element.11), channel_id=1, source_target_pairs={{0,4},{4,8},{8,12},{12,16},{16,20},{20,24},{24,28},{1,5},{5,9},{9,... | collective-permute-start | bytes 393224 | tf_op jit(solution)/shard_map/ppermute | solution.py:18
  17.6 9.8 %copy-start.4 = (bf16[4,64,512]{2,1,0:T(8,128)(2,1)S(1)}, bf16[4,64,512]{2,1,0:T(8,128)(2,1)}, u32[]{:S(2)}) copy-start(bf16[4,64,512]{2,1,0:T(8,128)(2,1)} %param.5) | copy-start | bytes 786436
  19.4 11.8 %collective-permute-start.3 = (bf16[6,1,8,128]{3,2,1,0:T(8,128)(2,1)S(1)}, bf16[6,1,8,128]{3,2,1,0:T(8,128)(2,1)S(1)}, u32[]{:S(2)}, u32[]{:S(2)}) collective-permute-start(bf16[6,1,8,128]{3,2,1,0:T(8,128)(2,1)S(1)} %copy.31), channel_id=1, source_target_pairs={{1,0},{2,1},{3,2},{5,4},{6,5},{7,6},{9,8},{10,9},{11,10},{13,12},{... | collective-permute-start | bytes 36872 | tf_op jit(solution)/shard_map/ppermute | solution.py:21
  21.4 10.7 %collective-permute-start.2 = (bf16[6,1,8,128]{3,2,1,0:T(8,128)(2,1)S(1)}, bf16[6,1,8,128]{3,2,1,0:T(8,128)(2,1)S(1)}, u32[]{:S(2)}, u32[]{:S(2)}) collective-permute-start(bf16[6,1,8,128]{3,2,1,0:T(8,128)(2,1)S(1)} %copy.30), channel_id=1, source_target_pairs={{0,1},{1,2},{2,3},{4,5},{5,6},{6,7},{8,9},{9,10},{10,11},{12,13},{... | collective-permute-start | bytes 36872 | tf_op jit(solution)/shard_map/ppermute | solution.py:18
  38.5 3.3 %copy-start.10 = (bf16[27,64,64]{2,1,0:T(8,128)(2,1)S(1)}, bf16[27,64,64]{2,1,0:T(8,128)(2,1)}, u32[]{:S(2)}) copy-start(bf16[27,64,64]{2,1,0:T(8,128)(2,1)} %param.6) | copy-start | bytes 663556
  41.8 7.8 %copy-start.3 = (bf16[1,6,66,8,64]{4,0,3,2,1:T(2,128)(2,1)S(1)}, bf16[1,6,66,8,64]{4,0,3,2,1:T(2,128)(2,1)}, u32[]{:S(2)}) copy-start(bf16[1,6,66,8,64]{4,0,3,2,1:T(2,128)(2,1)} %copy.34) | copy-start | bytes 1216516
  41.8 7.9 %copy-start.12 = (bf16[27,64,64]{2,1,0:T(8,128)(2,1)S(1)}, bf16[27,64,64]{2,1,0:T(8,128)(2,1)}, u32[]{:S(2)}) copy-start(bf16[27,64,64]{2,1,0:T(8,128)(2,1)} %rev.6) | copy-start | bytes 663556
  72.7 8.8 %copy-start.1 = (bf16[4,64,8,64]{3,2,1,0:T(8,128)(2,1)}, bf16[4,64,8,64]{3,2,1,0:T(8,128)(2,1)S(1)}, u32[]{:S(2)}) copy-start(bf16[4,64,8,64]{3,2,1,0:T(8,128)(2,1)S(1)} %get-tuple-element.9) | copy-start | bytes 786436
  72.7 7.6 %collective-permute-start.9 = (bf16[1,64,8,64]{3,2,1,0:T(8,128)(2,1)S(1)}, bf16[1,64,8,64]{3,2,1,0:T(8,128)(2,1)S(1)}, u32[]{:S(2)}, u32[]{:S(2)}) collective-permute-start(bf16[1,64,8,64]{3,2,1,0:T(8,128)(2,1)S(1)} %get-tuple-element.18), channel_id=1, source_target_pairs={{4,0},{8,4},{12,8},{16,12},{20,16},{24,20},{28,24},{5,1},{9,5},{13... | collective-permute-start | bytes 196616 | tf_op jit(solution)/shard_map/ppermute | solution.py:21
  74.0 6.8 %collective-permute-start.8 = (bf16[1,64,8,64]{3,2,1,0:T(8,128)(2,1)S(1)}, bf16[1,64,8,64]{3,2,1,0:T(8,128)(2,1)S(1)}, u32[]{:S(2)}, u32[]{:S(2)}) collective-permute-start(bf16[1,64,8,64]{3,2,1,0:T(8,128)(2,1)S(1)} %get-tuple-element.17), channel_id=1, source_target_pairs={{0,4},{4,8},{8,12},{12,16},{16,20},{20,24},{24,28},{1,5},{5,9},{9,... | collective-permute-start | bytes 196616 | tf_op jit(solution)/shard_map/ppermute | solution.py:18
  80.4 2.4 %copy-start.6 = (bf16[1,64,8,64]{3,2,1,0:T(8,128)(2,1)}, bf16[1,64,8,64]{3,2,1,0:T(8,128)(2,1)S(1)}, u32[]{:S(2)}) copy-start(bf16[1,64,8,64]{3,2,1,0:T(8,128)(2,1)S(1)} %collective-permute-done.9) | copy-start | bytes 196612
  80.9 1.9 copy-start.8
  81.5 21.4 %collective-permute-start.11 = (bf16[6,1,8,64]{3,2,1,0:T(8,128)(2,1)}, bf16[6,1,8,64]{3,2,1,0:T(8,128)(2,1)}, u32[]{:S(2)}, u32[]{:S(2)}) collective-permute-start(bf16[6,1,8,64]{3,2,1,0:T(8,128)(2,1)} %get-tuple-element.14), channel_id=1, source_target_pairs={{1,0},{2,1},{3,2},{5,4},{6,5},{7,6},{9,8},{10,9},{11,10},{13,12},{... | collective-permute-start | bytes 18440 | tf_op jit(solution)/shard_map/ppermute | solution.py:21
  82.8 20.1 %collective-permute-start.10 = (bf16[6,1,8,64]{3,2,1,0:T(8,128)(2,1)}, bf16[6,1,8,64]{3,2,1,0:T(8,128)(2,1)}, u32[]{:S(2)}, u32[]{:S(2)}) collective-permute-start(bf16[6,1,8,64]{3,2,1,0:T(8,128)(2,1)} %get-tuple-element.13), channel_id=1, source_target_pairs={{0,1},{1,2},{2,3},{4,5},{5,6},{6,7},{8,9},{9,10},{10,11},{12,13},{... | collective-permute-start | bytes 18440 | tf_op jit(solution)/shard_map/ppermute | solution.py:18
  101.5 1.4 copy-start.2
  101.6 1.4 copy-start.7
  101.6 1.4 copy-start.9
  101.9 2.1 copy-start.5
  102.7 57.9 %reduce-scatter.9.cloned.1.call-start = ((), (), s32[]{:S(2)}) async-start(), calls=%async_computation.3 | async-start | bytes 552960
  116.6 1.4 copy-start
  117.0 15.6 %copy-start.11 = (bf16[27,64,64]{2,1,0:T(8,128)(2,1)S(1)}, bf16[27,64,64]{2,1,0:T(8,128)(2,1)}, u32[]{:S(2)}) copy-start(bf16[27,64,64]{2,1,0:T(8,128)(2,1)} %param.6) | copy-start | bytes 663556
  117.0 15.6 %copy-start.13 = (u32[32]{0:T(128)S(1)}, u32[32]{0:T(128)}, u32[]{:S(2)}) copy-start(u32[32]{0:T(128)} %constant.18) | copy-start | bytes 388
  117.8 98.2 %all-reduce.7.cloned.1.call-start = ((), (), s32[]{:S(2)}) async-start(), calls=%async_computation.4 | async-start | bytes 442368
  118.1 7.6 %collective-permute-start.5 = (bf16[1,64,8,64]{3,2,1,0:T(8,128)(2,1)S(1)}, bf16[1,64,8,64]{3,2,1,0:T(8,128)(2,1)S(1)}, u32[]{:S(2)}, u32[]{:S(2)}) collective-permute-start(bf16[1,64,8,64]{3,2,1,0:T(8,128)(2,1)S(1)} %get-tuple-element.20), channel_id=1, source_target_pairs={{4,0},{8,4},{12,8},{16,12},{20,16},{24,20},{28,24},{5,1},{9,5},{13... | collective-permute-start | bytes 196616 | tf_op jit(solution)/shard_map/ppermute | solution.py:21
  119.4 7.2 %collective-permute-start.4 = (bf16[1,64,8,64]{3,2,1,0:T(8,128)(2,1)S(1)}, bf16[1,64,8,64]{3,2,1,0:T(8,128)(2,1)S(1)}, u32[]{:S(2)}, u32[]{:S(2)}) collective-permute-start(bf16[1,64,8,64]{3,2,1,0:T(8,128)(2,1)S(1)} %get-tuple-element.19), channel_id=1, source_target_pairs={{0,4},{4,8},{8,12},{12,16},{16,20},{20,24},{24,28},{1,5},{5,9},{9,... | collective-permute-start | bytes 196616 | tf_op jit(solution)/shard_map/ppermute | solution.py:18
  126.6 6.6 %collective-permute-start.7 = (bf16[6,1,8,64]{3,2,1,0:T(8,128)(2,1)S(1)}, bf16[6,1,8,64]{3,2,1,0:T(8,128)(2,1)S(1)}, u32[]{:S(2)}, u32[]{:S(2)}) collective-permute-start(bf16[6,1,8,64]{3,2,1,0:T(8,128)(2,1)S(1)} %get-tuple-element.16), channel_id=1, source_target_pairs={{1,0},{2,1},{3,2},{5,4},{6,5},{7,6},{9,8},{10,9},{11,10},{13,12},{... | collective-permute-start | bytes 18440 | tf_op jit(solution)/shard_map/ppermute | solution.py:21
  127.9 6.0 %collective-permute-start.6 = (bf16[6,1,8,64]{3,2,1,0:T(8,128)(2,1)S(1)}, bf16[6,1,8,64]{3,2,1,0:T(8,128)(2,1)S(1)}, u32[]{:S(2)}, u32[]{:S(2)}) collective-permute-start(bf16[6,1,8,64]{3,2,1,0:T(8,128)(2,1)S(1)} %get-tuple-element.15), channel_id=1, source_target_pairs={{0,1},{1,2},{2,3},{4,5},{5,6},{6,7},{8,9},{9,10},{10,11},{12,13},{... | collective-permute-start | bytes 18440 | tf_op jit(solution)/shard_map/ppermute | solution.py:18
Sparse Core Ops, SparseCore 0:
  102.8 30.3 reduce-scatter.6
  136.1 24.4 reduce-scatter.8
  163.0 52.8 all-reduce.6
where the time goes:
time: 228 us; the launch traced here: 225 us
  matrix products  78.8 us (35%)
  waiting for transfers between devices  56.9 us (25%)
  starting transfers between devices  39.9 us (18%)
  local copies, waits for them, and re-layouts  27.7 us (12%)
  between operations  14.4 us (6%)
  other arithmetic  7.07 us (3%)
    unnamed x6, waiting for transfers between devices  53.6 us
    conv_general_dilated x3, matrix products, correlate(): lax.conv_general_dilated(extended[None], taps, (1, 1, 1), ((0, 0), (0, 0)...  53.3 us
    ppermute x6, starting transfers between devices, extended_2(): lax.ppermute(lax.slice_in_dim(block, block.shape[dim] - width, None, axis...  31.7 us
    transpose x2, matrix products, kernel_grad(): jnp.transpose(result, (1, 2, 3, 0, 4)).reshape(27, chans_in, chans_out)  25.5 us
    ppermute x6, starting transfers between devices, extended_2(): lax.ppermute(lax.slice_in_dim(block, 0, width, axis=dim), axis, backward)  7.74 us
    broadcast_in_dim x3, local copies, waits for them, and re-layouts, correlate(): extended[None]  5.15 us
  transfers between devices with their start and end apart: 15, of which 6 were waited for; matrix products, arithmetic and copies ran while one was open for 28% of the time, Pallas kernels for 0%

commit v1 on v0

v1 whole, which is shorter than its diff:
```python
import functools

import jax
import jax.numpy as jnp
from jax import lax
from jax.experimental import pallas as pl
from jax.experimental.pallas import tpu as pltpu
from jax.sharding import PartitionSpec as P

CH = 64
PAD = 16

root_half = 0.7071067811865476
inv_root_two_pi = 0.3989422804014327


def pair_exchange(block, axis, first):
    count = lax.axis_size(axis)
    pairs = []
    for low in range(first, count - 1, 2):
        pairs += [(low, low + 1), (low + 1, low)]
    return lax.ppermute(block, axis, pairs)


def prepare_kernel(one_ref, two_ref, one_out, two_flip_out, one_flip_out):
    zero = jnp.zeros((CH, CH), jnp.bfloat16)

    def banded(tiles):
        padded = [zero] + tiles + [zero]
        return [jnp.concatenate([padded[c + 1], padded[c]], axis=1) for c in range(4)]

    def flipped(ref, tap):
        return jnp.transpose(ref[26 - tap].astype(jnp.float32)).astype(jnp.bfloat16)

    for ab in range(9):
        taps = [3 * ab + c for c in range(3)]
        for c, tile in enumerate(banded([one_ref[t] for t in taps])):
            one_out[ab, c] = tile
        for c, tile in enumerate(banded([flipped(two_ref, t) for t in taps])):
            two_flip_out[ab, c] = tile
        for c, tile in enumerate(banded([flipped(one_ref, t) for t in taps])):
            one_flip_out[ab, c] = tile


def prepare(kernel_one, kernel_two):
    shape = jax.ShapeDtypeStruct((9, 4, CH, 2 * CH), jnp.bfloat16)
    vmem = pl.BlockSpec(memory_space=pltpu.VMEM)
    return pl.pallas_call(
        prepare_kernel,
        out_shape=(shape, shape, shape),
        in_specs=[vmem, vmem],
        out_specs=(vmem, vmem, vmem),
        compiler_params=pltpu.CompilerParams(vmem_limit_bytes=16 << 20),
        cost_estimate=pl.CostEstimate(
            flops=4_000_000, bytes_accessed=4_000_000, transcendentals=0
        ),
    )(kernel_one, kernel_two)


def banded_weights(band_ref, group):
    zero = jnp.zeros((CH, 2 * CH), jnp.bfloat16)
    lift = 1 if group == 0 else -1
    rows = []
    for ab in range(9):
        for i in range(6):
            halves = []
            for m in range(2):
                c = i - 2 * m + lift
                halves.append(band_ref[ab, c] if 0 <= c < 4 else zero)
            rows.append(jnp.concatenate(halves, axis=1))
    return jnp.concatenate(rows, axis=0)


def main_kernel(
    rows,
    cols,
    x_ref,
    g_ref,
    ra_ref,
    rb_ref,
    ca_ref,
    cb_ref,
    one_ref,
    two_flip_ref,
    one_flip_ref,
    gi_ref,
    kg_ref,
    wide,
    xs,
    gs,
    ps,
    sums,
    acc_ref,
):
    f32, bf16 = jnp.float32, jnp.bfloat16
    stride = cols + PAD
    lines = rows + 4
    span = lines * stride + PAD
    lanes = x_ref.shape[2]
    base = 8
    ha = lax.axis_index("ha")
    wa = lax.axis_index("wa")
    ha_odd = lax.rem(ha, 2)
    wa_odd = lax.rem(wa, 2)

    halo = 2 * lines
    gap_rows = (lines + 1) * PAD
    q = lax.broadcasted_iota(jnp.int32, (gap_rows, 2 * halo), 0)
    col = lax.broadcasted_iota(jnp.int32, (gap_rows, 2 * halo), 1)
    gap = lax.div(q, PAD)
    w = lax.rem(q, PAD)

    def order(line):
        swapped = jnp.where(
            line < 2, line + lines - 2, jnp.where(line >= lines - 2, line - lines + 2, line)
        )
        return jnp.where(ha_odd == 0, swapped, line)

    left_base = jnp.where(wa_odd == 0, halo, 0)
    right_base = jnp.where(wa_odd == 0, 0, halo)
    left_hit = (w >= PAD - 2) & (gap < lines) & (col == left_base + 2 * order(gap) + w - (PAD - 2))
    right_hit = (w < 2) & (gap >= 1) & (col == right_base + 2 * order(gap - 1) + w)
    select = jnp.where(left_hit | right_hit, 1.0, 0.0).astype(bf16)

    def spread(which, own_ref, out):
        columns = jnp.concatenate([ca_ref[which], cb_ref[which]], axis=0)
        gaps = jnp.dot(select, columns, preferred_element_type=f32)
        for k in range(lines + 1):
            wide[base + k * stride : base + k * stride + PAD, :] = gaps[k * PAD : (k + 1) * PAD]
        for r in range(rows):
            start = base + PAD + (r + 2) * stride
            wide[start : start + cols, :] = own_ref[r].astype(f32)
        above = base + PAD
        below = base + PAD + (rows + 2) * stride
        a_start = jnp.where(ha_odd == 0, below, above)
        b_start = jnp.where(ha_odd == 0, above, below)
        for r in range(2):
            wide[pl.ds(pl.multiple_of(a_start + r * stride, 8), cols), :] = ra_ref[which, r].astype(f32)
            wide[pl.ds(pl.multiple_of(b_start + r * stride, 8), cols), :] = rb_ref[which, r].astype(f32)
        for b in range(3):
            out[b] = wide[base + b - 1 : base + b - 1 + span, :].astype(bf16)

    spread(0, x_ref, xs)
    spread(1, g_ref, gs)

    def correlate(src, band_ref, start, count):
        outs = []
        for group in range(2):
            lane = 128 * group
            left = jnp.concatenate(
                [
                    src[ab % 3, start + (ab // 3 - 1) * stride : start + (ab // 3 - 1) * stride + count, lane : lane + 6 * CH]
                    for ab in range(9)
                ],
                axis=1,
            )
            outs.append(jnp.dot(left, banded_weights(band_ref, group), preferred_element_type=f32))
        return outs

    first = stride
    count = (rows + 2) * stride + PAD
    pre = correlate(xs, one_ref, first, count)
    grad_active = correlate(gs, two_flip_ref, first, count)

    position = first + lax.broadcasted_iota(jnp.int32, (count, 256), 0)
    line = lax.div(position, stride)
    w = lax.rem(position, stride)
    ha_last = lax.axis_size("ha") - 1
    wa_last = lax.axis_size("wa") - 1
    owner = jnp.where(w < PAD // 2, line - 1, line)
    dead = ((owner < 2) & (ha == 0)) | ((owner >= rows + 2) & (ha == ha_last))
    dead = dead | ((w >= PAD // 2) & (w < PAD) & (wa == 0)) | ((w < PAD // 2) & (wa == wa_last))

    own_line = [PAD + (r + 1) * stride for r in range(rows)]
    active_t = []
    for group in range(2):
        value = pre[group]
        cdf = 0.5 * (1.0 + lax.erf(value * root_half))
        slope = cdf + value * inv_root_two_pi * jnp.exp(-0.5 * value * value)
        grad_pre = jnp.where(dead, 0.0, grad_active[group] * slope)
        wide[base + first : base + first + count, 256 * group : 256 * group + 256] = (
            grad_pre.astype(bf16).astype(f32)
        )
        active = value * cdf
        active = jnp.concatenate([active[s : s + cols] for s in own_line], axis=0)
        active_t.append(jnp.transpose(active).astype(bf16))
    for b in range(3):
        ps[b, first : first + count, :] = wide[
            base + first + b - 1 : base + first + b - 1 + count, :
        ].astype(bf16)

    x_own = jnp.concatenate([x_ref[r] for r in range(rows)], axis=0).astype(f32)
    x_t = [jnp.transpose(x_own[:, 256 * group : 256 * group + 256]).astype(bf16) for group in range(2)]

    def kernel_grad(fixed, src, a):
        parts = [[[None] * 4 for _ in range(3)] for _ in range(1)][0]
        for group in range(2):
            lane = 128 * group
            windows = []
            for b in range(3):
                shift = (1 - a) * stride
                windows.append(
                    jnp.concatenate(
                        [
                            src[2 - b, PAD + (r + 2) * stride + shift : PAD + (r + 2) * stride + shift + cols, lane : lane + 6 * CH]
                            for r in range(rows)
                        ],
                        axis=0,
                    )
                )
            acc_ref[...] = jnp.dot(
                fixed[group], jnp.concatenate(windows, axis=1), preferred_element_type=f32
            )
            lift = 1 if group == 0 else 3
            for b in range(3):
                for j in range(4):
                    for m in range(3):
                        e = j - 2 * m + lift
                        if 0 <= e < 4:
                            tile = acc_ref[64 * j : 64 * j + 64, 384 * b + 128 * m : 384 * b + 128 * m + 128]
                            old = parts[b][e]
                            parts[b][e] = tile if old is None else old + tile
        return parts

    low = lax.broadcasted_iota(jnp.int32, (CH, 2 * CH), 1) < CH
    for a in range(3):
        one = kernel_grad(x_t, ps, a)
        two = kernel_grad(active_t, gs, a)
        for b in range(3):
            for c in range(3):
                k_one = one[b][c] + pltpu.roll(one[b][c + 1], CH, 1)
                k_two = pltpu.roll(two[b][c], CH, 1) + two[b][c + 1]
                tap = 9 * a + 3 * b + c
                sums[CH * tap : CH * tap + CH, :] = jnp.where(low, k_one, k_two)
    share = kg_ref.shape[1]
    take = 27 * CH // kg_ref.shape[0]
    for d in range(kg_ref.shape[0]):
        kg_ref[d] = sums[take * d : take * d + share, :].astype(bf16)

    start = PAD + 2 * stride
    grad_inputs = correlate(ps, one_flip_ref, start, (rows - 1) * stride + cols)
    for group in range(2):
        for r in range(rows):
            gi_ref[r, :, 256 * group : 256 * group + 256] = grad_inputs[group][
                r * stride : r * stride + cols
            ].astype(bf16)


def main(x, g, ra, rb, ca, cb, one, two_flip, one_flip, devices):
    rows, cols, lanes = x.shape
    stride = cols + PAD
    span = (rows + 4) * stride + PAD
    take = 27 * CH // devices
    share = -(-take // 8) * 8
    vmem = pl.BlockSpec(memory_space=pltpu.VMEM)
    moving = pltpu.VMEM((3, span, lanes), jnp.bfloat16)
    return pl.pallas_call(
        functools.partial(main_kernel, rows, cols),
        out_shape=(
            jax.ShapeDtypeStruct(x.shape, jnp.bfloat16),
            jax.ShapeDtypeStruct((devices, share, 2 * CH), jnp.bfloat16),
        ),
        in_specs=[vmem] * 9,
        out_specs=(vmem, vmem),
        scratch_shapes=[
            pltpu.VMEM((span + 16, lanes), jnp.float32),
            moving,
            moving,
            moving,
            pltpu.VMEM((27 * CH + 8, 2 * CH), jnp.float32),
            pltpu.VMEM((256, 1152), jnp.float32),
        ],
        compiler_params=pltpu.CompilerParams(vmem_limit_bytes=48 << 20),
        cost_estimate=pl.CostEstimate(
            flops=20_000_000_000, bytes_accessed=8_000_000, transcendentals=1_000_000
        ),
    )(x, g, ra, rb, ca, cb, one, two_flip, one_flip)


def shards(inputs, grad_out, kernel_one, kernel_two):
    rows, cols, lanes = inputs.shape
    height_count = lax.axis_size("ha")
    width_count = lax.axis_size("wa")
    devices = height_count * width_count
    ha_even = lax.rem(lax.axis_index("ha"), 2) == 0
    wa_even = lax.rem(lax.axis_index("wa"), 2) == 0
    both = jnp.stack([inputs, grad_out])
    low, high = both[:, :2], both[:, rows - 2 :]
    ra = pair_exchange(jnp.where(ha_even, high, low), "ha", 0)
    rb = pair_exchange(jnp.where(ha_even, low, high), "ha", 1)
    one, two_flip, one_flip = prepare(kernel_one, kernel_two)

    def edge(start):
        pieces = [part[:, :, start : start + 2] for part in (ra, both, rb)]
        return jnp.concatenate(pieces, axis=1).reshape(2, 2 * (rows + 4), lanes)

    left, right = edge(0), edge(cols - 2)
    ca = pair_exchange(jnp.where(wa_even, right, left), "wa", 0)
    cb = pair_exchange(jnp.where(wa_even, left, right), "wa", 1)
    units = devices if (27 * CH) % devices == 0 else 1
    grad_inputs, partial = main(
        inputs, grad_out, ra, rb, ca, cb, one, two_flip, one_flip, units
    )
    if units == devices:
        take = 27 * CH // devices
        pieces = lax.all_to_all(partial, ("ha", "wa"), 0, 0, tiled=True)
        total = pieces.astype(jnp.float32).sum(0)[:take]
        return (
            grad_inputs,
            total[:, :CH].reshape(-1),
            total[:, CH:].reshape(-1),
        )
    partial = partial[0].astype(jnp.float32)
    outs = [partial[:, :CH].reshape(devices, -1), partial[:, CH:].reshape(devices, -1)]
    outs = [lax.psum_scatter(v, ("ha", "wa"), scatter_dimension=0, tiled=True) for v in outs]
    return (grad_inputs, outs[0].reshape(-1), outs[1].reshape(-1))


def solution(mesh):
    return jax.shard_map(
        shards,
        mesh=mesh,
        in_specs=(P("ha", "wa", None), P("ha", "wa", None), P(), P()),
        out_specs=(P("ha", "wa", None), P(("ha", "wa")), P(("ha", "wa"))),
        check_vma=False,
    )
```

time: 228 us -> 49.8 us (0.22); the launches traced: 225 us -> 49.7 us
  matrix products: 78.8 us -> 0 us
  waiting for transfers between devices: 56.9 us -> 2.1 us
  starting transfers between devices: 39.9 us -> 7.35 us
  blocking collectives: 0 us -> 26.8 us
  local copies, waits for them, and re-layouts: 27.7 us -> 1.53 us
  between operations: 14.4 us -> 0.76 us
  Pallas kernels: 0 us -> 9.45 us
  other arithmetic: 7.07 us -> 1.65 us
    unnamed x6 -> x0, waiting for transfers between devices: 53.6 us -> none
    conv_general_dilated x3 -> x0, matrix products: 53.3 us -> none  [correlate(): lax.conv_general_dilated(extended[None], taps, (1, 1, 1), ((0, 0), (0, 0)...]
    ppermute x12 -> x4, starting transfers between devices: 39.4 us -> 7.35 us  [pair_exchange(): return lax.ppermute(block, axis, pairs)]
    all_to_all x0 -> x1, blocking collectives: none -> 26.8 us  [shards(): pieces = lax.all_to_all(partial, ('ha', 'wa'), 0, 0, tiled=True)]
    transpose x2 -> x0, matrix products: 25.5 us -> none  [kernel_grad(): jnp.transpose(result, (1, 2, 3, 0, 4)).reshape(27, chans_in, chans_out)]
    pallas_call x0 -> x2, Pallas kernels: none -> 9.45 us  [the longest x1 8.72 us: main(): pl.pallas_call(functools.partial(main_kernel, rows, cols), out_shape=(jax...]
    broadcast_in_dim x3 -> x0, local copies, waits for them, and re-layouts: 5.15 us -> none  [correlate(): extended[None]]
    slice x5 -> x3, local copies, waits for them, and re-layouts: 4.42 us -> 0.11 us  [the longest x1 0.08 us: shards(): return (grad_inputs, total[:, :CH].reshape(-1), total[:, CH:].reshape(-1))]
  transfers between devices with their start and end apart: 15 -> 4, of which waited for: 6 -> 2; matrix products, arithmetic and copies ran while one was open for 28% -> 0% of each run, Pallas kernels for 0% -> 1%
where the time goes in v1:
time: 49.8 us; the launch traced here: 49.7 us
  blocking collectives  26.8 us (54%)
  Pallas kernels  9.45 us (19%)
  starting transfers between devices  7.35 us (15%)
  waiting for transfers between devices  2.1 us (4%)
  other arithmetic  1.65 us (3%)
  local copies, waits for them, and re-layouts  1.53 us (3%)
  between operations  0.76 us (2%)
    all_to_all x1, blocking collectives, shards(): pieces = lax.all_to_all(partial, ('ha', 'wa'), 0, 0, tiled=True)  26.8 us
    pallas_call x1, Pallas kernels, main(): pl.pallas_call(functools.partial(main_kernel, rows, cols), out_shape=(jax...  8.72 us
    ppermute x4, starting transfers between devices, pair_exchange(): return lax.ppermute(block, axis, pairs)  7.35 us
    ppermute x4, waiting for transfers between devices, pair_exchange(): return lax.ppermute(block, axis, pairs)  2.1 us
    select_n x1, other arithmetic, shards(): rb = pair_exchange(jnp.where(ha_even, low, high), 'ha', 1)  1.42 us
    reshape x2, local copies, waits for them, and re-layouts, shards(): return (grad_inputs, total[:, :CH].reshape(-1), total[:, CH:].reshape(-1))  1.36 us
  transfers between devices with their start and end apart: 4, of which 2 were waited for; matrix products, arithmetic and copies ran while one was open for 0% of the time, Pallas kernels for 1%

profile of v1, /device:TPU:0, one launch (start us, length us, event | category | flops | bytes accessed | tf_op | source)
XLA Modules:
  0.0 49.7 jit_solution(11433032646494290460)
XLA Ops:
  0.6 0.0 copy-start
  0.6 0.0 copy-start.1
  0.7 1.4 %broadcast_select_fusion = (bf16[2,2,64,512]{3,2,1,0:T(8,128)(2,1)S(1)}, bf16[2,2,64,512]{3,2,1,0:T(8,128)(2,1)S(1)}) fusion(pred[]{:T(512)S(6)} %eq.6, bf16[1,4,64,512]{3,2,1,0:T(8,128)(2,1)} %bitcast.5, bf16[1,4,64,512]{3,2,1,0:T(8,128)(2,1)} %bitcast.2), kind=kLoop, calls=%fused_computation.9 | loop fusion | flops 786432 | bytes 1048577 | tf_op jit(solution)/shard_map/jit(_where)/select_n | solution.py:290
  2.1 0.7 %collective-permute-start.1 = (bf16[2,2,64,512]{3,2,1,0:T(8,128)(2,1)S(1)}, bf16[2,2,64,512]{3,2,1,0:T(8,128)(2,1)S(1)}, u32[]{:S(2)}, u32[]{:S(2)}) collective-permute-start(bf16[2,2,64,512]{3,2,1,0:T(8,128)(2,1)S(1)} %get-tuple-element.15), channel_id=1, source_target_pairs={{4,8},{8,4},{12,16},{16,12},{20,24},{24,20},{5,9},{9,5},{13,17},{1... | collective-permute-start | bytes 786440 | tf_op jit(solution)/shard_map/ppermute | solution.py:22
  2.8 4.5 %collective-permute-start = (bf16[2,2,64,512]{3,2,1,0:T(8,128)(2,1)S(1)}, bf16[2,2,64,512]{3,2,1,0:T(8,128)(2,1)S(1)}, u32[]{:S(2)}, u32[]{:S(2)}) collective-permute-start(bf16[2,2,64,512]{3,2,1,0:T(8,128)(2,1)S(1)} %get-tuple-element.16), channel_id=1, source_target_pairs={{0,4},{4,0},{8,12},{12,8},{16,20},{20,16},{24,28},{28,24},{1,5},{5... | collective-permute-start | bytes 786440 | tf_op jit(solution)/shard_map/ppermute | solution.py:22
  7.2 0.0 copy-done
  7.2 0.0 copy-done.1
  7.3 0.0 collective-permute-done.1.rb_ref
  7.3 1.1 %collective-permute-done.ra_ref = bf16[2,2,64,512]{3,2,1,0:T(8,128)(2,1)S(1)} collective-permute-done((bf16[2,2,64,512]{3,2,1,0:T(8,128)(2,1)S(1)}, bf16[2,2,64,512]{3,2,1,0:T(8,128)(2,1)S(1)}, u32[]{:S(2)}, u32[]{:S(2)}) %collective-permute-start) | collective-permute-done | bytes 262176 | tf_op jit(solution)/shard_map/ppermute | solution.py:22
  8.4 0.0 copy-start.3
  8.4 0.0 copy-start.2
  8.4 0.1 broadcast_select_fusion.2
  8.5 0.1 broadcast_select_fusion.3
  8.6 1.6 %collective-permute-start.2 = (bf16[2,16,512]{2,1,0:T(8,128)(2,1)S(1)}, bf16[2,16,512]{2,1,0:T(8,128)(2,1)S(1)}, u32[]{:S(2)}, u32[]{:S(2)}) collective-permute-start(bf16[2,16,512]{2,1,0:T(8,128)(2,1)S(1)} %select_n.35), channel_id=1, source_target_pairs={{0,1},{1,0},{2,3},{3,2},{4,5},{5,4},{6,7},{7,6},{8,9},{9,8},{10,11... | collective-permute-start | bytes 98312 | tf_op jit(solution)/shard_map/ppermute | solution.py:22
  10.2 0.7 %collective-permute-start.3 = (bf16[2,16,512]{2,1,0:T(8,128)(2,1)S(1)}, bf16[2,16,512]{2,1,0:T(8,128)(2,1)S(1)}, u32[]{:S(2)}, u32[]{:S(2)}) collective-permute-start(bf16[2,16,512]{2,1,0:T(8,128)(2,1)S(1)} %select_n.37), channel_id=1, source_target_pairs={{1,2},{2,1},{5,6},{6,5},{9,10},{10,9},{13,14},{14,13},{17,18},{18,... | collective-permute-start | bytes 98312 | tf_op jit(solution)/shard_map/ppermute | solution.py:22
  10.8 0.0 copy-done.3
  10.8 0.0 copy-done.2
  10.8 0.7 %shard_map.67 = (bf16[9,4,64,128]{3,2,1,0:T(8,128)(2,1)S(1)}, bf16[9,4,64,128]{3,2,1,0:T(8,128)(2,1)S(1)}, bf16[9,4,64,128]{3,2,1,0:T(8,128)(2,1)S(1)}) custom-call(bf16[27,64,64]{2,1,0:T(8,128)(2,1)S(1)} %copy-done.2, bf16[27,64,64]{2,1,0:T(8,128)(2,1)S(1)} %copy-done.3), custom_call_target="tpu_custom_call" | custom-call | flops 4000000 | bytes 4000000 | tf_op jit(solution)/shard_map/pallas_call | solution.py:48
  11.6 1.0 %collective-permute-done.2.ca_ref = bf16[2,16,512]{2,1,0:T(8,128)(2,1)S(1)} collective-permute-done((bf16[2,16,512]{2,1,0:T(8,128)(2,1)S(1)}, bf16[2,16,512]{2,1,0:T(8,128)(2,1)S(1)}, u32[]{:S(2)}, u32[]{:S(2)}) %collective-permute-start.2) | collective-permute-done | bytes 32800 | tf_op jit(solution)/shard_map/ppermute | solution.py:22
  12.6 0.0 collective-permute-done.3.cb_ref
  12.6 8.7 %shard_map.68 = (bf16[4,64,512]{2,1,0:T(8,128)(2,1)}, bf16[32,56,128]{2,1,0:T(8,128)(2,1)S(1)}) custom-call(bf16[4,64,512]{2,1,0:T(8,128)(2,1)S(1)} %copy-done, bf16[4,64,512]{2,1,0:T(8,128)(2,1)S(1)} %copy-done.1, bf16[2,2,64,512]{3,2,1,0:T(8,128)(2,1)S(1)} %collective-permute-done.ra_ref, bf16[2,2,64,512]{3,2,1,0:T(8,128)(2,1)S(1)} %collective-permute-done.1.rb_ref, ...), custom_call_target="tpu_custom_call" | custom-call | flops 20000000000 | bytes 8000000 | tf_op jit(solution)/shard_map/pallas_call | solution.py:257
  21.3 26.8 %all_to_all.5 = bf16[32,56,128]{2,1,0:T(8,128)(2,1)S(1)} all-to-all(bf16[32,56,128]{2,1,0:T(8,128)(2,1)S(1)} %get-tuple-element.12), channel_id=1, replica_groups=mesh['ha'=8,'wa'=4] {'ha','wa'}, dimensions={0} | all-to-all | bytes 917504 | tf_op jit(solution)/shard_map/all_to_all | solution.py:306
  48.1 0.1 convert_reduce_fusion
  48.2 0.1 fusion.8
  48.3 0.7 %reshape.19 = f32[3456]{0:T(1024)} reshape(f32[54,64]{1,0:T(8,128)S(1)} %get-tuple-element.21) | data formatting | bytes 27648 | tf_op jit(solution)/shard_map/reshape | solution.py:311
  49.0 0.7 %reshape.18 = f32[3456]{0:T(1024)} reshape(f32[54,64]{1,0:T(8,128)S(1)} %get-tuple-element.22) | data formatting | bytes 27648 | tf_op jit(solution)/shard_map/reshape | solution.py:310
  (5 shorter events, 0.1 us)
Async XLA Ops:
  0.6 6.6 %copy-start = (bf16[4,64,512]{2,1,0:T(8,128)(2,1)S(1)}, bf16[4,64,512]{2,1,0:T(8,128)(2,1)}, u32[]{:S(2)}) copy-start(bf16[4,64,512]{2,1,0:T(8,128)(2,1)} %x_ref.1) | copy-start | bytes 786436
  0.6 6.6 %copy-start.1 = (bf16[4,64,512]{2,1,0:T(8,128)(2,1)S(1)}, bf16[4,64,512]{2,1,0:T(8,128)(2,1)}, u32[]{:S(2)}) copy-start(bf16[4,64,512]{2,1,0:T(8,128)(2,1)} %g_ref.1) | copy-start | bytes 786436
  2.1 5.2 %collective-permute-start.1 = (bf16[2,2,64,512]{3,2,1,0:T(8,128)(2,1)S(1)}, bf16[2,2,64,512]{3,2,1,0:T(8,128)(2,1)S(1)}, u32[]{:S(2)}, u32[]{:S(2)}) collective-permute-start(bf16[2,2,64,512]{3,2,1,0:T(8,128)(2,1)S(1)} %get-tuple-element.15), channel_id=1, source_target_pairs={{4,8},{8,4},{12,16},{16,12},{20,24},{24,20},{5,9},{9,5},{13,17},{1... | collective-permute-start | bytes 786440 | tf_op jit(solution)/shard_map/ppermute | solution.py:22
  2.8 5.6 %collective-permute-start = (bf16[2,2,64,512]{3,2,1,0:T(8,128)(2,1)S(1)}, bf16[2,2,64,512]{3,2,1,0:T(8,128)(2,1)S(1)}, u32[]{:S(2)}, u32[]{:S(2)}) collective-permute-start(bf16[2,2,64,512]{3,2,1,0:T(8,128)(2,1)S(1)} %get-tuple-element.16), channel_id=1, source_target_pairs={{0,4},{4,0},{8,12},{12,8},{16,20},{20,16},{24,28},{28,24},{1,5},{5... | collective-permute-start | bytes 786440 | tf_op jit(solution)/shard_map/ppermute | solution.py:22
  8.4 2.4 %copy-start.3 = (bf16[27,64,64]{2,1,0:T(8,128)(2,1)S(1)}, bf16[27,64,64]{2,1,0:T(8,128)(2,1)}, u32[]{:S(2)}) copy-start(bf16[27,64,64]{2,1,0:T(8,128)(2,1)} %two_ref.1) | copy-start | bytes 663556
  8.4 2.4 %copy-start.2 = (bf16[27,64,64]{2,1,0:T(8,128)(2,1)S(1)}, bf16[27,64,64]{2,1,0:T(8,128)(2,1)}, u32[]{:S(2)}) copy-start(bf16[27,64,64]{2,1,0:T(8,128)(2,1)} %one_ref.1) | copy-start | bytes 663556
  8.6 4.0 %collective-permute-start.2 = (bf16[2,16,512]{2,1,0:T(8,128)(2,1)S(1)}, bf16[2,16,512]{2,1,0:T(8,128)(2,1)S(1)}, u32[]{:S(2)}, u32[]{:S(2)}) collective-permute-start(bf16[2,16,512]{2,1,0:T(8,128)(2,1)S(1)} %select_n.35), channel_id=1, source_target_pairs={{0,1},{1,0},{2,3},{3,2},{4,5},{5,4},{6,7},{7,6},{8,9},{9,8},{10,11... | collective-permute-start | bytes 98312 | tf_op jit(solution)/shard_map/ppermute | solution.py:22
  10.2 2.4 %collective-permute-start.3 = (bf16[2,16,512]{2,1,0:T(8,128)(2,1)S(1)}, bf16[2,16,512]{2,1,0:T(8,128)(2,1)S(1)}, u32[]{:S(2)}, u32[]{:S(2)}) collective-permute-start(bf16[2,16,512]{2,1,0:T(8,128)(2,1)S(1)} %select_n.37), channel_id=1, source_target_pairs={{1,2},{2,1},{5,6},{6,5},{9,10},{10,9},{13,14},{14,13},{17,18},{18,... | collective-permute-start | bytes 98312 | tf_op jit(solution)/shard_map/ppermute | solution.py:22

commit v2 on v1

v2 whole, which is shorter than its diff:
```python
import functools

import jax
import jax.numpy as jnp
from jax import lax
from jax.experimental import pallas as pl
from jax.experimental.pallas import tpu as pltpu
from jax.sharding import PartitionSpec as P


CH = 64
PAD = 16

root_half = 0.7071067811865476
inv_root_two_pi = 0.3989422804014327


def pair_exchange(block, axis, first):
    count = lax.axis_size(axis)
    pairs = []
    for low in range(first, count - 1, 2):
        pairs += [(low, low + 1), (low + 1, low)]
    return lax.ppermute(block, axis, pairs)


def in_hbm(block):
    return pltpu.with_memory_space_constraint(block, pltpu.HBM)


def pack_kernel(x_hbm, g_hbm, x_ref, g_ref, to_a, to_b, own_a, own_b, sems):
    rows, cols, _ = x_ref.shape
    pairs = ((x_hbm, x_ref), (g_hbm, g_ref))
    copies = [
        pltpu.make_async_copy(source, target, sems.at[k])
        for k, (source, target) in enumerate(pairs)
    ]
    for copy in copies:
        copy.start()
    ha_even = lax.rem(lax.axis_index("ha"), 2) == 0
    wa_even = lax.rem(lax.axis_index("wa"), 2) == 0
    a_start = jnp.where(ha_even, rows - 2, 0)
    b_start = jnp.where(ha_even, 0, rows - 2)
    for which, ref in enumerate((x_ref, g_ref)):
        copies[which].wait()
        to_a[which] = ref[pl.ds(a_start, 2)]
        to_b[which] = ref[pl.ds(b_start, 2)]
        for r in range(rows):
            left, right = ref[r, 0:2, :], ref[r, cols - 2 : cols, :]
            own_a[which, r] = jnp.where(wa_even, right, left)
            own_b[which, r] = jnp.where(wa_even, left, right)


def pack(x, g):
    rows, cols, lanes = x.shape
    vmem = pl.BlockSpec(memory_space=pltpu.VMEM)
    hbm = pl.BlockSpec(memory_space=pltpu.HBM)
    shapes = [x.shape] * 2 + [(2, 2, cols, lanes)] * 2 + [(2, rows, 2, lanes)] * 2
    return pl.pallas_call(
        pack_kernel,
        out_shape=tuple(jax.ShapeDtypeStruct(shape, x.dtype) for shape in shapes),
        in_specs=[hbm, hbm],
        out_specs=(vmem,) * 6,
        scratch_shapes=[pltpu.SemaphoreType.DMA((2,))],
        compiler_params=pltpu.CompilerParams(vmem_limit_bytes=4 << 20),
        cost_estimate=pl.CostEstimate(flops=0, bytes_accessed=1_100_000, transcendentals=0),
    )(in_hbm(x), in_hbm(g))


def corners_kernel(wa_ref, wb_ref, to_a, to_b):
    rows = wa_ref.shape[1]
    ha_even = lax.rem(lax.axis_index("ha"), 2) == 0
    a_start = jnp.where(ha_even, rows - 2, 0)
    b_start = jnp.where(ha_even, 0, rows - 2)
    for side, ref in enumerate((wa_ref, wb_ref)):
        for which in range(2):
            for r in range(2):
                to_a[side, which, r] = ref[which, a_start + r]
                to_b[side, which, r] = ref[which, b_start + r]


def small_call(kernel, out_shape, *operands):
    vmem = pl.BlockSpec(memory_space=pltpu.VMEM)
    return pl.pallas_call(
        kernel,
        out_shape=out_shape,
        in_specs=[vmem] * len(operands),
        out_specs=(vmem,) * len(out_shape),
        compiler_params=pltpu.CompilerParams(vmem_limit_bytes=2 << 20),
        cost_estimate=pl.CostEstimate(flops=0, bytes_accessed=300_000, transcendentals=0),
    )(*operands)


def corners(wa, wb):
    shape = jax.ShapeDtypeStruct((2, 2, 2) + wa.shape[2:], wa.dtype)
    return small_call(corners_kernel, (shape, shape), wa, wb)


def prepare_kernel(
    one_hbm, two_hbm, one_out, two_flip_out, one_flip_out, one_ref, two_ref, sems
):
    copies = [
        pltpu.make_async_copy(one_hbm, one_ref, sems.at[0]),
        pltpu.make_async_copy(two_hbm, two_ref, sems.at[1]),
    ]
    for copy in copies:
        copy.start()
    for copy in copies:
        copy.wait()
    zero = jnp.zeros((CH, CH), jnp.bfloat16)

    def banded(tiles):
        padded = [zero] + tiles + [zero]
        return [jnp.concatenate([padded[c + 1], padded[c]], axis=1) for c in range(4)]

    def flipped(ref, tap):
        return jnp.transpose(ref[26 - tap].astype(jnp.float32)).astype(jnp.bfloat16)

    for ab in range(9):
        taps = [3 * ab + c for c in range(3)]
        for c, tile in enumerate(banded([one_ref[t] for t in taps])):
            one_out[ab, c] = tile
        for c, tile in enumerate(banded([flipped(two_ref, t) for t in taps])):
            two_flip_out[ab, c] = tile
        for c, tile in enumerate(banded([flipped(one_ref, t) for t in taps])):
            one_flip_out[ab, c] = tile


def prepare(kernel_one, kernel_two):
    shape = jax.ShapeDtypeStruct((9, 4, CH, 2 * CH), jnp.bfloat16)
    vmem = pl.BlockSpec(memory_space=pltpu.VMEM)
    hbm = pl.BlockSpec(memory_space=pltpu.HBM)
    return pl.pallas_call(
        prepare_kernel,
        out_shape=(shape, shape, shape),
        in_specs=[hbm, hbm],
        out_specs=(vmem, vmem, vmem),
        scratch_shapes=[pltpu.VMEM(kernel_one.shape, kernel_one.dtype)] * 2
        + [pltpu.SemaphoreType.DMA((2,))],
        compiler_params=pltpu.CompilerParams(vmem_limit_bytes=8 << 20),
        cost_estimate=pl.CostEstimate(
            flops=4_000_000, bytes_accessed=4_000_000, transcendentals=0
        ),
    )(in_hbm(kernel_one), in_hbm(kernel_two))


def banded_weights(band_ref, group):
    zero = jnp.zeros((CH, 2 * CH), jnp.bfloat16)
    lift = 1 if group == 0 else -1
    rows = []
    for ab in range(9):
        for i in range(6):
            halves = []
            for m in range(2):
                c = i - 2 * m + lift
                halves.append(band_ref[ab, c] if 0 <= c < 4 else zero)
            rows.append(jnp.concatenate(halves, axis=1))
    return jnp.concatenate(rows, axis=0)


def correlate(src, band_ref, start, count, stride):
    outs = []
    for group in range(2):
        lane = 128 * group
        windows = []
        for ab in range(9):
            top = start + (ab // 3 - 1) * stride
            windows.append(src[ab % 3, top : top + count, lane : lane + 6 * CH])
        outs.append(
            jnp.dot(
                jnp.concatenate(windows, axis=1),
                banded_weights(band_ref, group),
                preferred_element_type=jnp.float32,
            )
        )
    return outs


def input_grad_kernel(rows, cols, ps, band_ref, out_ref):
    stride = cols + PAD
    result = correlate(ps, band_ref, PAD + 2 * stride, (rows - 1) * stride + cols, stride)
    for group in range(2):
        for r in range(rows):
            out_ref[r, :, 256 * group : 256 * group + 256] = result[group][
                r * stride : r * stride + cols
            ].astype(out_ref.dtype)


def main_kernel(
    rows,
    cols,
    x_ref,
    g_ref,
    ra_ref,
    rb_ref,
    wa_ref,
    wb_ref,
    corner_a_ref,
    corner_b_ref,
    one_ref,
    two_flip_ref,
    ps,
    *rest,
):
    kg_refs, (wide, xs, gs, sums, acc_ref, turned, edges) = rest[:-7], rest[-7:]
    f32, bf16 = jnp.float32, jnp.bfloat16
    stride = cols + PAD
    lines = rows + 4
    span = lines * stride + PAD
    base = 8
    ha = lax.axis_index("ha")
    wa = lax.axis_index("wa")
    ha_odd = lax.rem(ha, 2)
    wa_odd = lax.rem(wa, 2)

    halo = 2 * lines
    gap_rows = (lines + 1) * PAD
    q = lax.broadcasted_iota(jnp.int32, (gap_rows, 2 * halo), 0)
    col = lax.broadcasted_iota(jnp.int32, (gap_rows, 2 * halo), 1)
    gap = lax.div(q, PAD)
    w = lax.rem(q, PAD)

    def order(line):
        swapped = jnp.where(
            line < 2, line + lines - 2, jnp.where(line >= lines - 2, line - lines + 2, line)
        )
        return jnp.where(ha_odd == 0, swapped, line)

    left_base = jnp.where(wa_odd == 0, halo, 0)
    right_base = jnp.where(wa_odd == 0, 0, halo)
    left_hit = (w >= PAD - 2) & (gap < lines) & (col == left_base + 2 * order(gap) + w - (PAD - 2))
    right_hit = (w < 2) & (gap >= 1) & (col == right_base + 2 * order(gap - 1) + w)
    select = jnp.where(left_hit | right_hit, 1.0, 0.0).astype(bf16)

    def spread(which, own_ref, out):
        for side, ref in enumerate((wa_ref, wb_ref)):
            pieces = (
                [corner_a_ref[side, which, r] for r in range(2)]
                + [ref[which, r] for r in range(rows)]
                + [corner_b_ref[side, which, r] for r in range(2)]
            )
            for k, piece in enumerate(pieces):
                at = side * halo + 2 * k
                edges[at : at + 2, :] = piece.astype(f32)
        gaps = jnp.dot(select, edges[...].astype(bf16), preferred_element_type=f32)
        for k in range(lines + 1):
            wide[base + k * stride : base + k * stride + PAD, :] = gaps[k * PAD : (k + 1) * PAD]
        for r in range(rows):
            start = base + PAD + (r + 2) * stride
            wide[start : start + cols, :] = own_ref[r].astype(f32)
        above = base + PAD
        below = base + PAD + (rows + 2) * stride
        a_start = jnp.where(ha_odd == 0, below, above)
        b_start = jnp.where(ha_odd == 0, above, below)
        for r in range(2):
            wide[pl.ds(pl.multiple_of(a_start + r * stride, 8), cols), :] = ra_ref[which, r].astype(f32)
            wide[pl.ds(pl.multiple_of(b_start + r * stride, 8), cols), :] = rb_ref[which, r].astype(f32)
        for b in range(3):
            out[b] = wide[base + b - 1 : base + b - 1 + span, :].astype(bf16)

    spread(0, x_ref, xs)
    spread(1, g_ref, gs)

    first = stride
    count = (rows + 2) * stride + PAD
    pre = correlate(xs, one_ref, first, count, stride)
    grad_active = correlate(gs, two_flip_ref, first, count, stride)

    position = first + lax.broadcasted_iota(jnp.int32, (count, 256), 0)
    line = lax.div(position, stride)
    w = lax.rem(position, stride)
    ha_last = lax.axis_size("ha") - 1
    wa_last = lax.axis_size("wa") - 1
    owner = jnp.where(w < PAD // 2, line - 1, line)
    dead = ((owner < 2) & (ha == 0)) | ((owner >= rows + 2) & (ha == ha_last))
    dead = dead | ((w >= PAD // 2) & (w < PAD) & (wa == 0)) | ((w < PAD // 2) & (wa == wa_last))

    def transposed(value):
        flat = jnp.transpose(value)
        halves = []
        for side in range(flat.shape[1] // 128):
            turned[side] = flat[:, 128 * side : 128 * side + 128]
            pieces = [
                turned[side, pl.ds(64 * j + odd, 32, stride=2), :]
                for j in range(4)
                for odd in range(2)
            ]
            halves.append(jnp.concatenate(pieces, axis=0))
        return jnp.concatenate(halves, axis=1).astype(bf16)

    own_line = [PAD + (r + 1) * stride for r in range(rows)]
    active_t = []
    for group in range(2):
        value = pre[group]
        cdf = 0.5 * (1.0 + lax.erf(value * root_half))
        slope = cdf + value * inv_root_two_pi * jnp.exp(-0.5 * value * value)
        grad_pre = jnp.where(dead, 0.0, grad_active[group] * slope)
        wide[base + first : base + first + count, 256 * group : 256 * group + 256] = (
            grad_pre.astype(bf16).astype(f32)
        )
        active = value * cdf
        active = jnp.concatenate([active[s : s + cols] for s in own_line], axis=0)
        active_t.append(transposed(active))
    for b in range(3):
        ps[b, first : first + count, :] = wide[
            base + first + b - 1 : base + first + b - 1 + count, :
        ].astype(bf16)

    x_own = jnp.concatenate([x_ref[r] for r in range(rows)], axis=0).astype(f32)
    x_t = [transposed(x_own[:, 256 * group : 256 * group + 256]) for group in range(2)]

    def kernel_grad(fixed, src, a):
        parts = [[[None] * 4 for _ in range(3)] for _ in range(1)][0]
        for group in range(2):
            lane = 128 * group
            windows = []
            for b in range(3):
                shift = (1 - a) * stride
                windows.append(
                    jnp.concatenate(
                        [
                            src[2 - b, PAD + (r + 2) * stride + shift : PAD + (r + 2) * stride + shift + cols, lane : lane + 6 * CH]
                            for r in range(rows)
                        ],
                        axis=0,
                    )
                )
            acc_ref[...] = jnp.dot(
                fixed[group], jnp.concatenate(windows, axis=1), preferred_element_type=f32
            )
            lift = 1 if group == 0 else 3
            for b in range(3):
                for j in range(4):
                    for m in range(3):
                        e = j - 2 * m + lift
                        if 0 <= e < 4:
                            tile = acc_ref[64 * j : 64 * j + 64, 384 * b + 128 * m : 384 * b + 128 * m + 128]
                            old = parts[b][e]
                            parts[b][e] = tile if old is None else old + tile
        return parts

    half = CH // 2
    low = lax.broadcasted_iota(jnp.int32, (half, 2 * CH), 1) < CH
    for a in range(3):
        for k, parts in enumerate((kernel_grad(x_t, ps, a), kernel_grad(active_t, gs, a))):
            for b in range(3):
                for c in range(3):
                    left, right = parts[b][c], parts[b][c + 1]
                    tile = jnp.where(
                        low,
                        left[:half] + pltpu.roll(right[:half], CH, 1),
                        pltpu.roll(left[half:], CH, 1) + right[half:],
                    )
                    tap = 9 * a + 3 * b + c
                    sums[k, half * tap : half * tap + half, :] = tile
    if len(kg_refs) == 1:
        for k in range(2):
            kg_refs[0][k] = sums[k, : 27 * half, :]
        return
    keep_ref, send_ref = kg_refs
    slabs, width, _, share, _ = keep_ref.shape
    take = 27 * half // (2 * slabs * width)
    for z in range(slabs):
        for w in range(width):
            for k in range(2):
                at = [take * ((2 * z + c) * width + w) for c in range(2)]
                even, odd = (sums[k, r : r + share, :] for r in at)
                keep_ref[z, w, k] = jnp.where(ha_odd == 0, even, odd)
                send_ref[z, w, k] = jnp.where(ha_odd == 0, odd, even).astype(bf16)


def main(x, g, ra, rb, wa, wb, corner_a, corner_b, one, two_flip, split):
    rows, cols, lanes = x.shape
    stride = cols + PAD
    span = (rows + 4) * stride + PAD
    if split:
        slabs, width = split
        take = 27 * CH // 2 // (2 * slabs * width)
        share = -(-take // 8) * 8
        grads = tuple(
            jax.ShapeDtypeStruct((slabs, width, 2, share, 2 * CH), dtype)
            for dtype in (jnp.float32, jnp.bfloat16)
        )
    else:
        grads = (jax.ShapeDtypeStruct((2, 27 * CH // 2, 2 * CH), jnp.float32),)
    vmem = pl.BlockSpec(memory_space=pltpu.VMEM)
    moving = pltpu.VMEM((3, span, lanes), jnp.bfloat16)
    return pl.pallas_call(
        functools.partial(main_kernel, rows, cols),
        out_shape=(
            jax.ShapeDtypeStruct((3, span, lanes), jnp.bfloat16),
            *grads,
        ),
        in_specs=[vmem] * 10,
        out_specs=(vmem,) * (1 + len(grads)),
        scratch_shapes=[
            pltpu.VMEM((span + 16, lanes), jnp.float32),
            moving,
            moving,
            pltpu.VMEM((2, 27 * CH // 2 + 8, 2 * CH), jnp.float32),
            pltpu.VMEM((256, 1152), jnp.float32),
            pltpu.VMEM((rows * cols // 128, 256, 128), jnp.float32),
            pltpu.VMEM((4 * (rows + 4), lanes), jnp.float32),
        ],
        compiler_params=pltpu.CompilerParams(vmem_limit_bytes=16 << 20),
        cost_estimate=pl.CostEstimate(
            flops=14_000_000_000, bytes_accessed=8_000_000, transcendentals=1_000_000
        ),
    )(x, g, ra, rb, wa, wb, corner_a, corner_b, one, two_flip)


def input_grad(ps, band, shape):
    rows, cols, _ = shape
    vmem = pl.BlockSpec(memory_space=pltpu.VMEM)
    return pl.pallas_call(
        functools.partial(input_grad_kernel, rows, cols),
        out_shape=jax.ShapeDtypeStruct(shape, jnp.bfloat16),
        in_specs=[vmem, vmem],
        out_specs=vmem,
        compiler_params=pltpu.CompilerParams(vmem_limit_bytes=8 << 20),
        cost_estimate=pl.CostEstimate(
            flops=2_000_000_000, bytes_accessed=4_000_000, transcendentals=0
        ),
    )(ps, band)


def xor_exchange(block, axis, mask):
    count = lax.axis_size(axis)
    return lax.ppermute(block, axis, [(i, i ^ mask) for i in range(count)])


def total_of(refs):
    total = refs[0].astype(jnp.float32)
    for ref in refs[1:]:
        total = total + ref.astype(jnp.float32)
    return total


def sum_chip_kernel(keep_ref, got_ref, own_ref, *send_refs):
    wa = lax.axis_index("wa")
    for z in range(keep_ref.shape[0]):
        own_ref[z] = total_of([keep_ref[z, wa], got_ref[z, wa]])
        for k, ref in enumerate(send_refs, 1):
            ref[z] = total_of([keep_ref[z, wa ^ k], got_ref[z, wa ^ k]]).astype(ref.dtype)


def sum_wa_kernel(*refs):
    slabs = refs[0].shape[0]
    got_refs, (own_ref, *send_refs) = refs[:-slabs], refs[-slabs:]
    z = lax.div(lax.axis_index("ha"), 2)
    own_ref[...] = total_of([ref[z] for ref in got_refs])
    for k, ref in enumerate(send_refs, 1):
        ref[...] = total_of([got[z ^ k] for got in got_refs])


def sum_z_kernel(*refs):
    total = total_of([ref[...] for ref in refs[:-2]])
    take = refs[-1].shape[0]
    for k, ref in enumerate(refs[-2:]):
        ref[...] = total[k, :take]


def reduce_chunks(keep, send, take):
    slabs, width = keep.shape[:2]
    f32, bf16 = jnp.float32, jnp.bfloat16
    unit = keep.shape[2:]
    got = xor_exchange(send, "ha", 1)
    shapes = [jax.ShapeDtypeStruct((slabs,) + unit, f32)]
    shapes += [jax.ShapeDtypeStruct((slabs,) + unit, bf16)] * (width - 1)
    own, *sends = small_call(sum_chip_kernel, tuple(shapes), keep, got)
    got = [xor_exchange(block, "wa", k) for k, block in enumerate(sends, 1)]
    shapes = [jax.ShapeDtypeStruct(unit, f32)] * slabs
    own, *sends = small_call(sum_wa_kernel, tuple(shapes), own, *got)
    got = [xor_exchange(block, "ha", 2 * k) for k, block in enumerate(sends, 1)]
    shapes = (jax.ShapeDtypeStruct((take, 2 * CH), f32),) * 2
    return small_call(sum_z_kernel, shapes, own, *got)


def shards(inputs, grad_out, kernel_one, kernel_two):
    height_count = lax.axis_size("ha")
    width_count = lax.axis_size("wa")
    devices = height_count * width_count
    x, g, to_a, to_b, own_a, own_b = pack(inputs, grad_out)
    wb = pair_exchange(own_b, "wa", 1)
    wa = pair_exchange(own_a, "wa", 0)
    ra = pair_exchange(to_a, "ha", 0)
    rb = pair_exchange(to_b, "ha", 1)
    one, two_flip, one_flip = prepare(kernel_one, kernel_two)
    corner_to_a, corner_to_b = corners(wa, wb)
    corner_b = pair_exchange(corner_to_b, "ha", 1)
    corner_a = pair_exchange(corner_to_a, "ha", 0)

    split = None
    if (
        (27 * CH // 2) % devices == 0
        and height_count & (height_count - 1) == 0
        and width_count & (width_count - 1) == 0
        and height_count > 1
    ):
        split = (height_count // 2, width_count)
    ps, *grads = main(x, g, ra, rb, wa, wb, corner_a, corner_b, one, two_flip, split)
    grad_inputs = input_grad(ps, one_flip, inputs.shape)
    if split:
        grads = reduce_chunks(*grads, 27 * CH // 2 // devices)
    else:
        grads = [
            lax.psum_scatter(
                grads[0][k].reshape(devices, -1), ("ha", "wa"), scatter_dimension=0, tiled=True
            )
            for k in range(2)
        ]
    return (grad_inputs, grads[0].reshape(-1), grads[1].reshape(-1))


def solution(mesh):
    return jax.shard_map(
        shards,
        mesh=mesh,
        in_specs=(P("ha", "wa", None), P("ha", "wa", None), P(), P()),
        out_specs=(P("ha", "wa", None), P(("ha", "wa")), P(("ha", "wa"))),
        check_vma=False,
    )
```

time: 49.8 us -> 45.2 us (0.908)
  blocking collectives: 26.8 us -> 0 us
  starting transfers between devices: 7.35 us -> 22.2 us
  waiting for transfers between devices: 2.1 us -> 9.31 us
  Pallas kernels: 9.45 us -> 12.8 us
  other arithmetic: 1.65 us -> 0 us
  local copies, waits for them, and re-layouts: 1.53 us -> 0 us
    all_to_all x1 -> x0, blocking collectives: 26.8 us -> none  [shards(): pieces = lax.all_to_all(partial, ('ha', 'wa'), 0, 0, tiled=True)]
    ppermute x0 -> x7, starting transfers between devices: none -> 14.8 us  [xor_exchange(): return lax.ppermute(block, axis, [(i, i ^ mask) for i in range(count)])]
    ppermute x0 -> x7, waiting for transfers between devices: none -> 8.23 us  [xor_exchange(): return lax.ppermute(block, axis, [(i, i ^ mask) for i in range(count)])]
    pallas_call x0 -> x6, Pallas kernels: none -> 3.78 us  [the longest x1 2 us: input_grad(): pl.pallas_call(functools.partial(input_grad_kernel, rows, cols), out_shap...]
    pallas_call x1, Pallas kernels: 8.72 us -> 7.09 us  [main(): pl.pallas_call(functools.partial(main_kernel, rows, cols), out_shape=(jax...]
    select_n x3 -> x0, other arithmetic: 1.54 us -> none  [the longest x1 1.42 us: shards(): rb = pair_exchange(jnp.where(ha_even, low, high), 'ha', 1)]
    reshape x2 -> x0, local copies, waits for them, and re-layouts: 1.36 us -> none  [shards(): return (grad_inputs, total[:, :CH].reshape(-1), total[:, CH:].reshape(-1))]
    pallas_call x1, Pallas kernels: 0.73 us -> 1.9 us  [prepare(): pl.pallas_call(prepare_kernel, out_shape=(shape, shape, shape), in_specs=...]
  transfers between devices with their start and end apart: 4 -> 13, of which waited for: 2 -> 6; matrix products, arithmetic and copies ran while one was open for 0% -> 0% of each run, Pallas kernels for 1% -> 9%
where the time goes in v2:
time: 45.2 us; the launch traced here: 45 us
  starting transfers between devices  22.2 us (49%)
  Pallas kernels  12.8 us (28%)
  waiting for transfers between devices  9.31 us (21%)
  between operations  0.72 us (2%)
    ppermute x7, starting transfers between devices, xor_exchange(): return lax.ppermute(block, axis, [(i, i ^ mask) for i in range(count)])  14.8 us
    ppermute x7, waiting for transfers between devices, xor_exchange(): return lax.ppermute(block, axis, [(i, i ^ mask) for i in range(count)])  8.23 us
    ppermute x6, starting transfers between devices, pair_exchange(): return lax.ppermute(block, axis, pairs)  7.45 us
    pallas_call x1, Pallas kernels, main(): pl.pallas_call(functools.partial(main_kernel, rows, cols), out_shape=(jax...  7.09 us
    pallas_call x1, Pallas kernels, input_grad(): pl.pallas_call(functools.partial(input_grad_kernel, rows, cols), out_shap...  2 us
    pallas_call x1, Pallas kernels, prepare(): pl.pallas_call(prepare_kernel, out_shape=(shape, shape, shape), in_specs=...  1.9 us
    pallas_call x1, Pallas kernels, pack(): pl.pallas_call(pack_kernel, out_shape=tuple((jax.ShapeDtypeStruct(shape,...  1.08 us
    ppermute x6, waiting for transfers between devices, pair_exchange(): return lax.ppermute(block, axis, pairs)  1.07 us
  transfers between devices with their start and end apart: 13, of which 6 were waited for; matrix products, arithmetic and copies ran while one was open for 0% of the time, Pallas kernels for 9%

profile of v2, /device:TPU:0, one launch (start us, length us, event | category | flops | bytes accessed | tf_op | source)
XLA Modules:
  0.0 45.0 jit_solution(15578471378782429829)
XLA Ops:
  0.6 1.1 %shard_map.67 = (bf16[4,64,512]{2,1,0:T(8,128)(2,1)S(1)}, bf16[4,64,512]{2,1,0:T(8,128)(2,1)S(1)}, bf16[2,2,64,512]{3,2,1,0:T(8,128)(2,1)S(1)}, bf16[2,2,64,512]...) custom-call(bf16[4,64,512]{2,1,0:T(8,128)(2,1)} %x_hbm.1, ...), custom_call_target="tpu_custom_call" | custom-call | bytes 1100000 | tf_op jit(solution)/shard_map/pallas_call | solution.py:58
  1.7 0.6 %collective-permute-start = (bf16[2,2,64,512]{3,2,1,0:T(8,128)(2,1)S(1)}, bf16[2,2,64,512]{3,2,1,0:T(8,128)(2,1)S(1)}, u32[]{:S(2)}, u32[]{:S(2)}) collective-permute-start(bf16[2,2,64,512]{3,2,1,0:T(8,128)(2,1)S(1)} %get-tuple-element.29), channel_id=1, source_target_pairs={{0,4},{4,0},{8,12},{12,8},{16,20},{20,16},{24,28},{28,24},{1,5},{5... | collective-permute-start | bytes 786440 | tf_op jit(solution)/shard_map/ppermute | solution.py:23
  2.3 0.7 %collective-permute-start.1 = (bf16[2,2,64,512]{3,2,1,0:T(8,128)(2,1)S(1)}, bf16[2,2,64,512]{3,2,1,0:T(8,128)(2,1)S(1)}, u32[]{:S(2)}, u32[]{:S(2)}) collective-permute-start(bf16[2,2,64,512]{3,2,1,0:T(8,128)(2,1)S(1)} %get-tuple-element.30), channel_id=1, source_target_pairs={{4,8},{8,4},{12,16},{16,12},{20,24},{24,20},{5,9},{9,5},{13,17},{1... | collective-permute-start | bytes 786440 | tf_op jit(solution)/shard_map/ppermute | solution.py:23
  2.9 2.6 %collective-permute-start.2 = (bf16[2,4,2,512]{3,2,1,0:T(2,128)(2,1)S(1)}, bf16[2,4,2,512]{3,2,1,0:T(2,128)(2,1)S(1)}, u32[]{:S(2)}, u32[]{:S(2)}) collective-permute-start(bf16[2,4,2,512]{3,2,1,0:T(2,128)(2,1)S(1)} %get-tuple-element.31), channel_id=1, source_target_pairs={{0,1},{1,0},{2,3},{3,2},{4,5},{5,4},{6,7},{7,6},{8,9},{9,8},{10,11... | collective-permute-start | bytes 49160 | tf_op jit(solution)/shard_map/ppermute | solution.py:23
  5.5 0.7 %collective-permute-start.3 = (bf16[2,4,2,512]{3,2,1,0:T(2,128)(2,1)S(1)}, bf16[2,4,2,512]{3,2,1,0:T(2,128)(2,1)S(1)}, u32[]{:S(2)}, u32[]{:S(2)}) collective-permute-start(bf16[2,4,2,512]{3,2,1,0:T(2,128)(2,1)S(1)} %get-tuple-element.32), channel_id=1, source_target_pairs={{1,2},{2,1},{5,6},{6,5},{9,10},{10,9},{13,14},{14,13},{17,18},{18,... | collective-permute-start | bytes 49160 | tf_op jit(solution)/shard_map/ppermute | solution.py:23
  6.2 1.1 %collective-permute-done.2.wa_ref = bf16[2,4,2,512]{3,2,1,0:T(2,128)(2,1)S(1)} collective-permute-done((bf16[2,4,2,512]{3,2,1,0:T(2,128)(2,1)S(1)}, bf16[2,4,2,512]{3,2,1,0:T(2,128)(2,1)S(1)}, u32[]{:S(2)}, u32[]{:S(2)}) %collective-permute-start.2) | collective-permute-done | bytes 16416 | tf_op jit(solution)/shard_map/ppermute | solution.py:23
  7.2 0.0 collective-permute-done.3.wb_ref
  7.2 2.4 %collective-permute-start.4 = (bf16[2,2,2,2,512]{4,3,2,1,0:T(2,128)(2,1)S(1)}, bf16[2,2,2,2,512]{4,3,2,1,0:T(2,128)(2,1)S(1)}, u32[]{:S(2)}, u32[]{:S(2)}) collective-permute-start(bf16[2,2,2,2,512]{4,3,2,1,0:T(2,128)(2,1)S(1)} %get-tuple-element.33), channel_id=1, source_target_pairs={{0,4},{4,0},{8,12},{12,8},{16,20},{20,16},{24,28},{28,24},{1,5},{5... | collective-permute-start | bytes 49160 | tf_op jit(solution)/shard_map/ppermute | solution.py:23
  9.6 0.7 %collective-permute-start.5 = (bf16[2,2,2,2,512]{4,3,2,1,0:T(2,128)(2,1)S(1)}, bf16[2,2,2,2,512]{4,3,2,1,0:T(2,128)(2,1)S(1)}, u32[]{:S(2)}, u32[]{:S(2)}) collective-permute-start(bf16[2,2,2,2,512]{4,3,2,1,0:T(2,128)(2,1)S(1)} %get-tuple-element.34), channel_id=1, source_target_pairs={{4,8},{8,4},{12,16},{16,12},{20,24},{24,20},{5,9},{9,5},{13,17},{1... | collective-permute-start | bytes 49160 | tf_op jit(solution)/shard_map/ppermute | solution.py:23
  10.3 1.9 %shard_map.69 = (bf16[9,4,64,128]{3,2,1,0:T(8,128)(2,1)S(1)}, bf16[9,4,64,128]{3,2,1,0:T(8,128)(2,1)S(1)}, bf16[9,4,64,128]{3,2,1,0:T(8,128)(2,1)S(1)}) custom-call(bf16[27,64,64]{2,1,0:T(8,128)(2,1)} %one_hbm.1, bf16[27,64,64]{2,1,0:T(8,128)(2,1)} %two_hbm.1), custom_call_target="tpu_custom_call" | custom-call | flops 4000000 | bytes 4000000 | tf_op jit(solution)/shard_map/pallas_call | solution.py:132
  12.2 0.0 collective-permute-done.4.corner_a_ref
  12.2 0.0 collective-permute-done.5.corner_b_ref
  12.2 0.0 collective-permute-done.ra_ref
  12.2 0.0 collective-permute-done.1.rb_ref
  12.2 7.1 %shard_map.70 = (bf16[3,656,512]{2,1,0:T(8,128)(2,1)S(1)}, f32[4,4,2,32,128]{4,3,2,1,0:T(8,128)S(1)}, bf16[4,4,2,32,128]{4,3,2,1,0:T(8,128)(2,1)S(1)}) custom-call(bf16[4,64,512]{2,1,0:T(8,128)(2,1)S(1)} %get-tuple-element.27.x_ref, bf16[4,64,512]{2,1,0:T(8,128)(2,1)S(1)} %get-tuple-element.28.g_ref, ...), custom_call_target="tpu_custom_call" | custom-call | flops 14000000000 | bytes 8000000 | tf_op jit(solution)/shard_map/pallas_call | solution.py:387
  19.3 3.3 %collective-permute-start.6 = (bf16[4,4,2,32,128]{4,3,2,1,0:T(8,128)(2,1)S(1)}, bf16[4,4,2,32,128]{4,3,2,1,0:T(8,128)(2,1)S(1)}, u32[]{:S(2)}, u32[]{:S(2)}) collective-permute-start(bf16[4,4,2,32,128]{4,3,2,1,0:T(8,128)(2,1)S(1)} %get-tuple-element.40), channel_id=1, source_target_pairs={{0,4},{4,0},{8,12},{12,8},{16,20},{20,16},{24,28},{28,24},{1,5},{5... | collective-permute-start | bytes 786440 | tf_op jit(solution)/shard_map/ppermute | solution.py:428
  22.6 1.2 %collective-permute-done.6.got_ref = bf16[4,4,2,32,128]{4,3,2,1,0:T(8,128)(2,1)S(1)} collective-permute-done((bf16[4,4,2,32,128]{4,3,2,1,0:T(8,128)(2,1)S(1)}, bf16[4,4,2,32,128]{4,3,2,1,0:T(8,128)(2,1)S(1)}, u32[]{:S(2)}, u32[]{:S(2)}) %collective-permute-start.6) | collective-permute-done | bytes 262176 | tf_op jit(solution)/shard_map/ppermute | solution.py:428
  23.8 4.2 %collective-permute-start.7 = (bf16[4,2,32,128]{3,2,1,0:T(8,128)(2,1)S(1)}, bf16[4,2,32,128]{3,2,1,0:T(8,128)(2,1)S(1)}, u32[]{:S(2)}, u32[]{:S(2)}) collective-permute-start(bf16[4,2,32,128]{3,2,1,0:T(8,128)(2,1)S(1)} %get-tuple-element.42), channel_id=1, source_target_pairs={{0,1},{1,0},{2,3},{3,2},{4,5},{5,4},{6,7},{7,6},{8,9},{9,8},{10,11... | collective-permute-start | bytes 196616 | tf_op jit(solution)/shard_map/ppermute | solution.py:428
  28.0 1.4 %collective-permute-start.8 = (bf16[4,2,32,128]{3,2,1,0:T(8,128)(2,1)S(1)}, bf16[4,2,32,128]{3,2,1,0:T(8,128)(2,1)S(1)}, u32[]{:S(2)}, u32[]{:S(2)}) collective-permute-start(bf16[4,2,32,128]{3,2,1,0:T(8,128)(2,1)S(1)} %get-tuple-element.43), channel_id=1, source_target_pairs={{0,2},{1,3},{2,0},{3,1},{4,6},{5,7},{6,4},{7,5},{8,10},{9,11},{10,... | collective-permute-start | bytes 196616 | tf_op jit(solution)/shard_map/ppermute | solution.py:428
  29.5 1.4 %collective-permute-start.9 = (bf16[4,2,32,128]{3,2,1,0:T(8,128)(2,1)S(1)}, bf16[4,2,32,128]{3,2,1,0:T(8,128)(2,1)S(1)}, u32[]{:S(2)}, u32[]{:S(2)}) collective-permute-start(bf16[4,2,32,128]{3,2,1,0:T(8,128)(2,1)S(1)} %get-tuple-element.44), channel_id=1, source_target_pairs={{0,3},{1,2},{2,1},{3,0},{4,7},{5,6},{6,5},{7,4},{8,11},{9,10},{10,... | collective-permute-start | bytes 196616 | tf_op jit(solution)/shard_map/ppermute | solution.py:428
  30.9 0.0 collective-permute-done.7.refs_1_
  30.9 1.4 %collective-permute-done.8.refs_2_ = bf16[4,2,32,128]{3,2,1,0:T(8,128)(2,1)S(1)} collective-permute-done((bf16[4,2,32,128]{3,2,1,0:T(8,128)(2,1)S(1)}, bf16[4,2,32,128]{3,2,1,0:T(8,128)(2,1)S(1)}, u32[]{:S(2)}, u32[]{:S(2)}) %collective-permute-start.8) | collective-permute-done | bytes 65568 | tf_op jit(solution)/shard_map/ppermute | solution.py:428
  32.3 2.3 %collective-permute-done.9.refs_3_ = bf16[4,2,32,128]{3,2,1,0:T(8,128)(2,1)S(1)} collective-permute-done((bf16[4,2,32,128]{3,2,1,0:T(8,128)(2,1)S(1)}, bf16[4,2,32,128]{3,2,1,0:T(8,128)(2,1)S(1)}, u32[]{:S(2)}, u32[]{:S(2)}) %collective-permute-start.9) | collective-permute-done | bytes 65568 | tf_op jit(solution)/shard_map/ppermute | solution.py:428
  34.7 1.6 %collective-permute-start.10 = (f32[2,32,128]{2,1,0:T(8,128)S(1)}, f32[2,32,128]{2,1,0:T(8,128)S(1)}, u32[]{:S(2)}, u32[]{:S(2)}) collective-permute-start(f32[2,32,128]{2,1,0:T(8,128)S(1)} %get-tuple-element.46), channel_id=1, source_target_pairs={{0,8},{4,12},{8,0},{12,4},{16,24},{20,28},{24,16},{28,20},{1,9},{5... | collective-permute-start | bytes 98312 | tf_op jit(solution)/shard_map/ppermute | solution.py:428
  36.3 2.4 %collective-permute-start.11 = (f32[2,32,128]{2,1,0:T(8,128)S(1)}, f32[2,32,128]{2,1,0:T(8,128)S(1)}, u32[]{:S(2)}, u32[]{:S(2)}) collective-permute-start(f32[2,32,128]{2,1,0:T(8,128)S(1)} %get-tuple-element.47), channel_id=1, source_target_pairs={{0,16},{4,20},{8,24},{12,28},{16,0},{20,4},{24,8},{28,12},{1,17},{... | collective-permute-start | bytes 98312 | tf_op jit(solution)/shard_map/ppermute | solution.py:428
  38.7 0.4 collective-permute-start.12
  39.1 2.0 %shard_map.71 = bf16[4,64,512]{2,1,0:T(8,128)(2,1)} custom-call(bf16[3,656,512]{2,1,0:T(8,128)(2,1)S(1)} %get-tuple-element.37.ps, bf16[9,4,64,128]{3,2,1,0:T(8,128)(2,1)S(1)} %get-tuple-element.38.band_ref), custom_call_target="tpu_custom_call" | custom-call | flops 2000000000 | bytes 4000000 | tf_op jit(solution)/shard_map/pallas_call | solution.py:414
  41.1 0.0 collective-permute-done.10.refs_1_
  41.1 0.3 collective-permute-done.11.refs_2_
  41.4 3.0 %collective-permute-done.12.refs_3_ = f32[2,32,128]{2,1,0:T(8,128)S(1)} collective-permute-done((f32[2,32,128]{2,1,0:T(8,128)S(1)}, f32[2,32,128]{2,1,0:T(8,128)S(1)}, u32[]{:S(2)}, u32[]{:S(2)}) %collective-permute-start.12) | collective-permute-done | bytes 32800 | tf_op jit(solution)/shard_map/ppermute | solution.py:428
  44.4 0.6 %shard_map.74 = (f32[27,128]{1,0:T(8,128)}, f32[27,128]{1,0:T(8,128)}) custom-call(f32[2,32,128]{2,1,0:T(8,128)S(1)} %get-tuple-element.45.refs_0_, f32[2,32,128]{2,1,0:T(8,128)S(1)} %collective-permute-done.10.refs_1_, f32[2,32,128]{2,1,0:T(8,128)S(1)} %collective-permute-done.11.refs_2_, f32[2,32,128]{2,1,0:T(8,128)S(1)} %collective-permute-done.12.refs_3_), custom_call_target="tpu_custom_call" | custom-call | bytes 300000 | tf_op jit(solution)/shard_map/pallas_call | solution.py:83
  (3 shorter events, 0.1 us)
Async XLA Ops:
  1.7 10.5 %collective-permute-start = (bf16[2,2,64,512]{3,2,1,0:T(8,128)(2,1)S(1)}, bf16[2,2,64,512]{3,2,1,0:T(8,128)(2,1)S(1)}, u32[]{:S(2)}, u32[]{:S(2)}) collective-permute-start(bf16[2,2,64,512]{3,2,1,0:T(8,128)(2,1)S(1)} %get-tuple-element.29), channel_id=1, source_target_pairs={{0,4},{4,0},{8,12},{12,8},{16,20},{20,16},{24,28},{28,24},{1,5},{5... | collective-permute-start | bytes 786440 | tf_op jit(solution)/shard_map/ppermute | solution.py:23
  2.3 9.9 %collective-permute-start.1 = (bf16[2,2,64,512]{3,2,1,0:T(8,128)(2,1)S(1)}, bf16[2,2,64,512]{3,2,1,0:T(8,128)(2,1)S(1)}, u32[]{:S(2)}, u32[]{:S(2)}) collective-permute-start(bf16[2,2,64,512]{3,2,1,0:T(8,128)(2,1)S(1)} %get-tuple-element.30), channel_id=1, source_target_pairs={{4,8},{8,4},{12,16},{16,12},{20,24},{24,20},{5,9},{9,5},{13,17},{1... | collective-permute-start | bytes 786440 | tf_op jit(solution)/shard_map/ppermute | solution.py:23
  2.9 4.3 %collective-permute-start.2 = (bf16[2,4,2,512]{3,2,1,0:T(2,128)(2,1)S(1)}, bf16[2,4,2,512]{3,2,1,0:T(2,128)(2,1)S(1)}, u32[]{:S(2)}, u32[]{:S(2)}) collective-permute-start(bf16[2,4,2,512]{3,2,1,0:T(2,128)(2,1)S(1)} %get-tuple-element.31), channel_id=1, source_target_pairs={{0,1},{1,0},{2,3},{3,2},{4,5},{5,4},{6,7},{7,6},{8,9},{9,8},{10,11... | collective-permute-start | bytes 49160 | tf_op jit(solution)/shard_map/ppermute | solution.py:23
  5.5 1.7 %collective-permute-start.3 = (bf16[2,4,2,512]{3,2,1,0:T(2,128)(2,1)S(1)}, bf16[2,4,2,512]{3,2,1,0:T(2,128)(2,1)S(1)}, u32[]{:S(2)}, u32[]{:S(2)}) collective-permute-start(bf16[2,4,2,512]{3,2,1,0:T(2,128)(2,1)S(1)} %get-tuple-element.32), channel_id=1, source_target_pairs={{1,2},{2,1},{5,6},{6,5},{9,10},{10,9},{13,14},{14,13},{17,18},{18,... | collective-permute-start | bytes 49160 | tf_op jit(solution)/shard_map/ppermute | solution.py:23
  7.2 4.9 %collective-permute-start.4 = (bf16[2,2,2,2,512]{4,3,2,1,0:T(2,128)(2,1)S(1)}, bf16[2,2,2,2,512]{4,3,2,1,0:T(2,128)(2,1)S(1)}, u32[]{:S(2)}, u32[]{:S(2)}) collective-permute-start(bf16[2,2,2,2,512]{4,3,2,1,0:T(2,128)(2,1)S(1)} %get-tuple-element.33), channel_id=1, source_target_pairs={{0,4},{4,0},{8,12},{12,8},{16,20},{20,16},{24,28},{28,24},{1,5},{5... | collective-permute-start | bytes 49160 | tf_op jit(solution)/shard_map/ppermute | solution.py:23
  9.6 2.6 %collective-permute-start.5 = (bf16[2,2,2,2,512]{4,3,2,1,0:T(2,128)(2,1)S(1)}, bf16[2,2,2,2,512]{4,3,2,1,0:T(2,128)(2,1)S(1)}, u32[]{:S(2)}, u32[]{:S(2)}) collective-permute-start(bf16[2,2,2,2,512]{4,3,2,1,0:T(2,128)(2,1)S(1)} %get-tuple-element.34), channel_id=1, source_target_pairs={{4,8},{8,4},{12,16},{16,12},{20,24},{24,20},{5,9},{9,5},{13,17},{1... | collective-permute-start | bytes 49160 | tf_op jit(solution)/shard_map/ppermute | solution.py:23
  19.3 4.5 %collective-permute-start.6 = (bf16[4,4,2,32,128]{4,3,2,1,0:T(8,128)(2,1)S(1)}, bf16[4,4,2,32,128]{4,3,2,1,0:T(8,128)(2,1)S(1)}, u32[]{:S(2)}, u32[]{:S(2)}) collective-permute-start(bf16[4,4,2,32,128]{4,3,2,1,0:T(8,128)(2,1)S(1)} %get-tuple-element.40), channel_id=1, source_target_pairs={{0,4},{4,0},{8,12},{12,8},{16,20},{20,16},{24,28},{28,24},{1,5},{5... | collective-permute-start | bytes 786440 | tf_op jit(solution)/shard_map/ppermute | solution.py:428
  23.8 7.1 %collective-permute-start.7 = (bf16[4,2,32,128]{3,2,1,0:T(8,128)(2,1)S(1)}, bf16[4,2,32,128]{3,2,1,0:T(8,128)(2,1)S(1)}, u32[]{:S(2)}, u32[]{:S(2)}) collective-permute-start(bf16[4,2,32,128]{3,2,1,0:T(8,128)(2,1)S(1)} %get-tuple-element.42), channel_id=1, source_target_pairs={{0,1},{1,0},{2,3},{3,2},{4,5},{5,4},{6,7},{7,6},{8,9},{9,8},{10,11... | collective-permute-start | bytes 196616 | tf_op jit(solution)/shard_map/ppermute | solution.py:428
  28.0 4.3 %collective-permute-start.8 = (bf16[4,2,32,128]{3,2,1,0:T(8,128)(2,1)S(1)}, bf16[4,2,32,128]{3,2,1,0:T(8,128)(2,1)S(1)}, u32[]{:S(2)}, u32[]{:S(2)}) collective-permute-start(bf16[4,2,32,128]{3,2,1,0:T(8,128)(2,1)S(1)} %get-tuple-element.43), channel_id=1, source_target_pairs={{0,2},{1,3},{2,0},{3,1},{4,6},{5,7},{6,4},{7,5},{8,10},{9,11},{10,... | collective-permute-start | bytes 196616 | tf_op jit(solution)/shard_map/ppermute | solution.py:428
  29.5 5.2 %collective-permute-start.9 = (bf16[4,2,32,128]{3,2,1,0:T(8,128)(2,1)S(1)}, bf16[4,2,32,128]{3,2,1,0:T(8,128)(2,1)S(1)}, u32[]{:S(2)}, u32[]{:S(2)}) collective-permute-start(bf16[4,2,32,128]{3,2,1,0:T(8,128)(2,1)S(1)} %get-tuple-element.44), channel_id=1, source_target_pairs={{0,3},{1,2},{2,1},{3,0},{4,7},{5,6},{6,5},{7,4},{8,11},{9,10},{10,... | collective-permute-start | bytes 196616 | tf_op jit(solution)/shard_map/ppermute | solution.py:428
  34.7 6.5 %collective-permute-start.10 = (f32[2,32,128]{2,1,0:T(8,128)S(1)}, f32[2,32,128]{2,1,0:T(8,128)S(1)}, u32[]{:S(2)}, u32[]{:S(2)}) collective-permute-start(f32[2,32,128]{2,1,0:T(8,128)S(1)} %get-tuple-element.46), channel_id=1, source_target_pairs={{0,8},{4,12},{8,0},{12,4},{16,24},{20,28},{24,16},{28,20},{1,9},{5... | collective-permute-start | bytes 98312 | tf_op jit(solution)/shard_map/ppermute | solution.py:428
  36.3 5.1 %collective-permute-start.11 = (f32[2,32,128]{2,1,0:T(8,128)S(1)}, f32[2,32,128]{2,1,0:T(8,128)S(1)}, u32[]{:S(2)}, u32[]{:S(2)}) collective-permute-start(f32[2,32,128]{2,1,0:T(8,128)S(1)} %get-tuple-element.47), channel_id=1, source_target_pairs={{0,16},{4,20},{8,24},{12,28},{16,0},{20,4},{24,8},{28,12},{1,17},{... | collective-permute-start | bytes 98312 | tf_op jit(solution)/shard_map/ppermute | solution.py:428
  38.7 5.7 %collective-permute-start.12 = (f32[2,32,128]{2,1,0:T(8,128)S(1)}, f32[2,32,128]{2,1,0:T(8,128)S(1)}, u32[]{:S(2)}, u32[]{:S(2)}) collective-permute-start(f32[2,32,128]{2,1,0:T(8,128)S(1)} %get-tuple-element.48), channel_id=1, source_target_pairs={{0,24},{4,28},{8,16},{12,20},{16,8},{20,12},{24,0},{28,4},{1,25},{... | collective-permute-start | bytes 98312 | tf_op jit(solution)/shard_map/ppermute | solution.py:428

commit v3 on v2

--- a/solution.py
+++ b/solution.py
@@ -27,9 +27,11 @@
     return pltpu.with_memory_space_constraint(block, pltpu.HBM)
 
 
-def pack_kernel(x_hbm, g_hbm, x_ref, g_ref, to_a, to_b, own_a, own_b, sems):
+def pack_kernel(
+    x_hbm, g_hbm, one_hbm, two_hbm, x_ref, g_ref, one_ref, two_ref, to_a, to_b, own_a, own_b, sems
+):
     rows, cols, _ = x_ref.shape
-    pairs = ((x_hbm, x_ref), (g_hbm, g_ref))
+    pairs = ((x_hbm, x_ref), (g_hbm, g_ref), (one_hbm, one_ref), (two_hbm, two_ref))
     copies = [
         pltpu.make_async_copy(source, target, sems.at[k])
         for k, (source, target) in enumerate(pairs)
@@ -48,22 +50,25 @@
             left, right = ref[r, 0:2, :], ref[r, cols - 2 : cols, :]
             own_a[which, r] = jnp.where(wa_even, right, left)
             own_b[which, r] = jnp.where(wa_even, left, right)
-
-
-def pack(x, g):
+    for copy in copies[2:]:
+        copy.wait()
+
+
+def pack(x, g, one, two):
     rows, cols, lanes = x.shape
     vmem = pl.BlockSpec(memory_space=pltpu.VMEM)
     hbm = pl.BlockSpec(memory_space=pltpu.HBM)
-    shapes = [x.shape] * 2 + [(2, 2, cols, lanes)] * 2 + [(2, rows, 2, lanes)] * 2
+    shapes = [x.shape] * 2 + [one.shape] * 2
+    shapes += [(2, 2, cols, lanes)] * 2 + [(2, rows, 2, lanes)] * 2
     return pl.pallas_call(
         pack_kernel,
         out_shape=tuple(jax.ShapeDtypeStruct(shape, x.dtype) for shape in shapes),
-        in_specs=[hbm, hbm],
-        out_specs=(vmem,) * 6,
-        scratch_shapes=[pltpu.SemaphoreType.DMA((2,))],
+        in_specs=[hbm] * 4,
+        out_specs=(vmem,) * 8,
+        scratch_shapes=[pltpu.SemaphoreType.DMA((4,))],
         compiler_params=pltpu.CompilerParams(vmem_limit_bytes=4 << 20),
         cost_estimate=pl.CostEstimate(flops=0, bytes_accessed=1_100_000, transcendentals=0),
-    )(in_hbm(x), in_hbm(g))
+    )(*(in_hbm(block) for block in (x, g, one, two)))
 
 
 def corners_kernel(wa_ref, wb_ref, to_a, to_b):
@@ -95,17 +100,7 @@
     return small_call(corners_kernel, (shape, shape), wa, wb)
 
 
-def prepare_kernel(
-    one_hbm, two_hbm, one_out, two_flip_out, one_flip_out, one_ref, two_ref, sems
-):
-    copies = [
-        pltpu.make_async_copy(one_hbm, one_ref, sems.at[0]),
-        pltpu.make_async_copy(two_hbm, two_ref, sems.at[1]),
-    ]
-    for copy in copies:
-        copy.start()
-    for copy in copies:
-        copy.wait()
+def prepare_kernel(one_ref, two_ref, one_out, two_flip_out, one_flip_out):
     zero = jnp.zeros((CH, CH), jnp.bfloat16)
 
     def banded(tiles):
@@ -128,19 +123,16 @@
 def prepare(kernel_one, kernel_two):
     shape = jax.ShapeDtypeStruct((9, 4, CH, 2 * CH), jnp.bfloat16)
     vmem = pl.BlockSpec(memory_space=pltpu.VMEM)
-    hbm = pl.BlockSpec(memory_space=pltpu.HBM)
     return pl.pallas_call(
         prepare_kernel,
         out_shape=(shape, shape, shape),
-        in_specs=[hbm, hbm],
+        in_specs=[vmem, vmem],
         out_specs=(vmem, vmem, vmem),
-        scratch_shapes=[pltpu.VMEM(kernel_one.shape, kernel_one.dtype)] * 2
-        + [pltpu.SemaphoreType.DMA((2,))],
         compiler_params=pltpu.CompilerParams(vmem_limit_bytes=8 << 20),
         cost_estimate=pl.CostEstimate(
             flops=4_000_000, bytes_accessed=4_000_000, transcendentals=0
         ),
-    )(in_hbm(kernel_one), in_hbm(kernel_two))
+    )(kernel_one, kernel_two)
 
 
 def banded_weights(band_ref, group):
@@ -467,10 +459,14 @@
     shapes = [jax.ShapeDtypeStruct((slabs,) + unit, f32)]
     shapes += [jax.ShapeDtypeStruct((slabs,) + unit, bf16)] * (width - 1)
     own, *sends = small_call(sum_chip_kernel, tuple(shapes), keep, got)
-    got = [xor_exchange(block, "wa", k) for k, block in enumerate(sends, 1)]
+    got = []
+    for k, block in enumerate(sends, 1):
+        got.append(xor_exchange(block, "wa", k))
     shapes = [jax.ShapeDtypeStruct(unit, f32)] * slabs
     own, *sends = small_call(sum_wa_kernel, tuple(shapes), own, *got)
-    got = [xor_exchange(block, "ha", 2 * k) for k, block in enumerate(sends, 1)]
+    got = []
+    for k, block in enumerate(sends, 1):
+        got.append(xor_exchange(block, "ha", 2 * k))
     shapes = (jax.ShapeDtypeStruct((take, 2 * CH), f32),) * 2
     return small_call(sum_z_kernel, shapes, own, *got)
 
@@ -479,7 +475,9 @@
     height_count = lax.axis_size("ha")
     width_count = lax.axis_size("wa")
     devices = height_count * width_count
-    x, g, to_a, to_b, own_a, own_b = pack(inputs, grad_out)
+    x, g, kernel_one, kernel_two, to_a, to_b, own_a, own_b = pack(
+        inputs, grad_out, kernel_one, kernel_two
+    )
     wb = pair_exchange(own_b, "wa", 1)
     wa = pair_exchange(own_a, "wa", 0)
     ra = pair_exchange(to_a, "ha", 0)

time: 45.2 us -> 45.5 us (level)
  Pallas kernels: 12.8 us -> 11.8 us
  starting transfers between devices: 22.2 us -> 23.1 us
    pallas_call x1, Pallas kernels: 1.9 us -> 0.73 us  [prepare(): pl.pallas_call(prepare_kernel, out_shape=(shape, shape, shape), in_specs=...]
    ppermute x7, starting transfers between devices: 14.8 us -> 15.7 us  [xor_exchange(): return lax.ppermute(block, axis, [(i, i ^ mask) for i in range(count)])]
  transfers between devices with their start and end apart: 13 -> 13, of which waited for: 6 -> 6; matrix products, arithmetic and copies ran while one was open for 0% -> 0% of each run, Pallas kernels for 9% -> 6%
where the time goes in v3:
time: 45.5 us; the launch traced here: 45.3 us
  starting transfers between devices  23.1 us (51%)
  Pallas kernels  11.8 us (26%)
  waiting for transfers between devices  9.62 us (21%)
  between operations  0.72 us (2%)
    ppermute x7, starting transfers between devices, xor_exchange(): return lax.ppermute(block, axis, [(i, i ^ mask) for i in range(count)])  15.7 us
    ppermute x7, waiting for transfers between devices, xor_exchange(): return lax.ppermute(block, axis, [(i, i ^ mask) for i in range(count)])  8.55 us
    ppermute x6, starting transfers between devices, pair_exchange(): return lax.ppermute(block, axis, pairs)  7.45 us
    pallas_call x1, Pallas kernels, main(): pl.pallas_call(functools.partial(main_kernel, rows, cols), out_shape=(jax...  7.08 us
    pallas_call x1, Pallas kernels, input_grad(): pl.pallas_call(functools.partial(input_grad_kernel, rows, cols), out_shap...  2 us
    pallas_call x1, Pallas kernels, pack(): pl.pallas_call(pack_kernel, out_shape=tuple((jax.ShapeDtypeStruct(shape,...  1.34 us
    ppermute x6, waiting for transfers between devices, pair_exchange(): return lax.ppermute(block, axis, pairs)  1.07 us
  transfers between devices with their start and end apart: 13, of which 6 were waited for; matrix products, arithmetic and copies ran while one was open for 0% of the time, Pallas kernels for 6%

profile of v3, /device:TPU:0, one launch (start us, length us, event | category | flops | bytes accessed | tf_op | source)
XLA Modules:
  0.0 45.3 jit_solution(7965903546544914772)
XLA Ops:
  0.6 1.3 %shard_map.67 = (bf16[4,64,512]{2,1,0:T(8,128)(2,1)S(1)}, bf16[4,64,512]{2,1,0:T(8,128)(2,1)S(1)}, bf16[27,64,64]{2,1,0:T(8,128)(2,1)S(1)}, bf16[27,64,64]{2,1,0...) custom-call(bf16[4,64,512]{2,1,0:T(8,128)(2,1)} %x_hbm.1, ...), custom_call_target="tpu_custom_call" | custom-call | bytes 1100000 | tf_op jit(solution)/shard_map/pallas_call | solution.py:63
  2.0 0.6 %collective-permute-start = (bf16[2,2,64,512]{3,2,1,0:T(8,128)(2,1)S(1)}, bf16[2,2,64,512]{3,2,1,0:T(8,128)(2,1)S(1)}, u32[]{:S(2)}, u32[]{:S(2)}) collective-permute-start(bf16[2,2,64,512]{3,2,1,0:T(8,128)(2,1)S(1)} %get-tuple-element.31), channel_id=1, source_target_pairs={{0,4},{4,0},{8,12},{12,8},{16,20},{20,16},{24,28},{28,24},{1,5},{5... | collective-permute-start | bytes 786440 | tf_op jit(solution)/shard_map/ppermute | solution.py:23
  2.5 0.7 %collective-permute-start.1 = (bf16[2,2,64,512]{3,2,1,0:T(8,128)(2,1)S(1)}, bf16[2,2,64,512]{3,2,1,0:T(8,128)(2,1)S(1)}, u32[]{:S(2)}, u32[]{:S(2)}) collective-permute-start(bf16[2,2,64,512]{3,2,1,0:T(8,128)(2,1)S(1)} %get-tuple-element.32), channel_id=1, source_target_pairs={{4,8},{8,4},{12,16},{16,12},{20,24},{24,20},{5,9},{9,5},{13,17},{1... | collective-permute-start | bytes 786440 | tf_op jit(solution)/shard_map/ppermute | solution.py:23
  3.2 2.6 %collective-permute-start.2 = (bf16[2,4,2,512]{3,2,1,0:T(2,128)(2,1)S(1)}, bf16[2,4,2,512]{3,2,1,0:T(2,128)(2,1)S(1)}, u32[]{:S(2)}, u32[]{:S(2)}) collective-permute-start(bf16[2,4,2,512]{3,2,1,0:T(2,128)(2,1)S(1)} %get-tuple-element.33), channel_id=1, source_target_pairs={{0,1},{1,0},{2,3},{3,2},{4,5},{5,4},{6,7},{7,6},{8,9},{9,8},{10,11... | collective-permute-start | bytes 49160 | tf_op jit(solution)/shard_map/ppermute | solution.py:23
  5.8 0.7 %collective-permute-start.3 = (bf16[2,4,2,512]{3,2,1,0:T(2,128)(2,1)S(1)}, bf16[2,4,2,512]{3,2,1,0:T(2,128)(2,1)S(1)}, u32[]{:S(2)}, u32[]{:S(2)}) collective-permute-start(bf16[2,4,2,512]{3,2,1,0:T(2,128)(2,1)S(1)} %get-tuple-element.34), channel_id=1, source_target_pairs={{1,2},{2,1},{5,6},{6,5},{9,10},{10,9},{13,14},{14,13},{17,18},{18,... | collective-permute-start | bytes 49160 | tf_op jit(solution)/shard_map/ppermute | solution.py:23
  6.4 1.1 %collective-permute-done.2.wa_ref = bf16[2,4,2,512]{3,2,1,0:T(2,128)(2,1)S(1)} collective-permute-done((bf16[2,4,2,512]{3,2,1,0:T(2,128)(2,1)S(1)}, bf16[2,4,2,512]{3,2,1,0:T(2,128)(2,1)S(1)}, u32[]{:S(2)}, u32[]{:S(2)}) %collective-permute-start.2) | collective-permute-done | bytes 16416 | tf_op jit(solution)/shard_map/ppermute | solution.py:23
  7.5 0.0 collective-permute-done.3.wb_ref
  7.5 2.4 %collective-permute-start.4 = (bf16[2,2,2,2,512]{4,3,2,1,0:T(2,128)(2,1)S(1)}, bf16[2,2,2,2,512]{4,3,2,1,0:T(2,128)(2,1)S(1)}, u32[]{:S(2)}, u32[]{:S(2)}) collective-permute-start(bf16[2,2,2,2,512]{4,3,2,1,0:T(2,128)(2,1)S(1)} %get-tuple-element.35), channel_id=1, source_target_pairs={{0,4},{4,0},{8,12},{12,8},{16,20},{20,16},{24,28},{28,24},{1,5},{5... | collective-permute-start | bytes 49160 | tf_op jit(solution)/shard_map/ppermute | solution.py:23
  9.9 0.7 %collective-permute-start.5 = (bf16[2,2,2,2,512]{4,3,2,1,0:T(2,128)(2,1)S(1)}, bf16[2,2,2,2,512]{4,3,2,1,0:T(2,128)(2,1)S(1)}, u32[]{:S(2)}, u32[]{:S(2)}) collective-permute-start(bf16[2,2,2,2,512]{4,3,2,1,0:T(2,128)(2,1)S(1)} %get-tuple-element.36), channel_id=1, source_target_pairs={{4,8},{8,4},{12,16},{16,12},{20,24},{24,20},{5,9},{9,5},{13,17},{1... | collective-permute-start | bytes 49160 | tf_op jit(solution)/shard_map/ppermute | solution.py:23
  10.5 0.7 %shard_map.69 = (bf16[9,4,64,128]{3,2,1,0:T(8,128)(2,1)S(1)}, bf16[9,4,64,128]{3,2,1,0:T(8,128)(2,1)S(1)}, bf16[9,4,64,128]{3,2,1,0:T(8,128)(2,1)S(1)}) custom-call(bf16[27,64,64]{2,1,0:T(8,128)(2,1)S(1)} %get-tuple-element.37.one_ref, bf16[27,64,64]{2,1,0:T(8,128)(2,1)S(1)} %get-tuple-element.38.two_ref), custom_call_target="tpu_custom_call" | custom-call | flops 4000000 | bytes 4000000 | tf_op jit(solution)/shard_map/pallas_call | solution.py:126
  11.3 0.0 collective-permute-done.4.corner_a_ref
  11.3 0.0 collective-permute-done.5.corner_b_ref
  11.3 0.0 collective-permute-done.ra_ref
  11.3 0.0 collective-permute-done.1.rb_ref
  11.3 7.1 %shard_map.70 = (bf16[3,656,512]{2,1,0:T(8,128)(2,1)S(1)}, f32[4,4,2,32,128]{4,3,2,1,0:T(8,128)S(1)}, bf16[4,4,2,32,128]{4,3,2,1,0:T(8,128)(2,1)S(1)}) custom-call(bf16[4,64,512]{2,1,0:T(8,128)(2,1)S(1)} %get-tuple-element.29.x_ref, bf16[4,64,512]{2,1,0:T(8,128)(2,1)S(1)} %get-tuple-element.30.g_ref, ...), custom_call_target="tpu_custom_call" | custom-call | flops 14000000000 | bytes 8000000 | tf_op jit(solution)/shard_map/pallas_call | solution.py:379
  18.4 3.9 %collective-permute-start.6 = (bf16[4,4,2,32,128]{4,3,2,1,0:T(8,128)(2,1)S(1)}, bf16[4,4,2,32,128]{4,3,2,1,0:T(8,128)(2,1)S(1)}, u32[]{:S(2)}, u32[]{:S(2)}) collective-permute-start(bf16[4,4,2,32,128]{4,3,2,1,0:T(8,128)(2,1)S(1)} %get-tuple-element.44), channel_id=1, source_target_pairs={{0,4},{4,0},{8,12},{12,8},{16,20},{20,16},{24,28},{28,24},{1,5},{5... | collective-permute-start | bytes 786440 | tf_op jit(solution)/shard_map/ppermute | solution.py:420
  22.3 1.2 %collective-permute-done.6.got_ref = bf16[4,4,2,32,128]{4,3,2,1,0:T(8,128)(2,1)S(1)} collective-permute-done((bf16[4,4,2,32,128]{4,3,2,1,0:T(8,128)(2,1)S(1)}, bf16[4,4,2,32,128]{4,3,2,1,0:T(8,128)(2,1)S(1)}, u32[]{:S(2)}, u32[]{:S(2)}) %collective-permute-start.6) | collective-permute-done | bytes 262176 | tf_op jit(solution)/shard_map/ppermute | solution.py:420
  23.5 4.3 %collective-permute-start.7 = (bf16[4,2,32,128]{3,2,1,0:T(8,128)(2,1)S(1)}, bf16[4,2,32,128]{3,2,1,0:T(8,128)(2,1)S(1)}, u32[]{:S(2)}, u32[]{:S(2)}) collective-permute-start(bf16[4,2,32,128]{3,2,1,0:T(8,128)(2,1)S(1)} %get-tuple-element.46), channel_id=1, source_target_pairs={{0,1},{1,0},{2,3},{3,2},{4,5},{5,4},{6,7},{7,6},{8,9},{9,8},{10,11... | collective-permute-start | bytes 196616 | tf_op jit(solution)/shard_map/ppermute | solution.py:420
  27.8 1.4 %collective-permute-start.8 = (bf16[4,2,32,128]{3,2,1,0:T(8,128)(2,1)S(1)}, bf16[4,2,32,128]{3,2,1,0:T(8,128)(2,1)S(1)}, u32[]{:S(2)}, u32[]{:S(2)}) collective-permute-start(bf16[4,2,32,128]{3,2,1,0:T(8,128)(2,1)S(1)} %get-tuple-element.47), channel_id=1, source_target_pairs={{0,2},{1,3},{2,0},{3,1},{4,6},{5,7},{6,4},{7,5},{8,10},{9,11},{10,... | collective-permute-start | bytes 196616 | tf_op jit(solution)/shard_map/ppermute | solution.py:420
  29.2 1.4 %collective-permute-start.9 = (bf16[4,2,32,128]{3,2,1,0:T(8,128)(2,1)S(1)}, bf16[4,2,32,128]{3,2,1,0:T(8,128)(2,1)S(1)}, u32[]{:S(2)}, u32[]{:S(2)}) collective-permute-start(bf16[4,2,32,128]{3,2,1,0:T(8,128)(2,1)S(1)} %get-tuple-element.48), channel_id=1, source_target_pairs={{0,3},{1,2},{2,1},{3,0},{4,7},{5,6},{6,5},{7,4},{8,11},{9,10},{10,... | collective-permute-start | bytes 196616 | tf_op jit(solution)/shard_map/ppermute | solution.py:420
  30.6 0.0 collective-permute-done.7.refs_1_
  30.6 1.5 %collective-permute-done.8.refs_2_ = bf16[4,2,32,128]{3,2,1,0:T(8,128)(2,1)S(1)} collective-permute-done((bf16[4,2,32,128]{3,2,1,0:T(8,128)(2,1)S(1)}, bf16[4,2,32,128]{3,2,1,0:T(8,128)(2,1)S(1)}, u32[]{:S(2)}, u32[]{:S(2)}) %collective-permute-start.8) | collective-permute-done | bytes 65568 | tf_op jit(solution)/shard_map/ppermute | solution.py:420
  32.1 2.3 %collective-permute-done.9.refs_3_ = bf16[4,2,32,128]{3,2,1,0:T(8,128)(2,1)S(1)} collective-permute-done((bf16[4,2,32,128]{3,2,1,0:T(8,128)(2,1)S(1)}, bf16[4,2,32,128]{3,2,1,0:T(8,128)(2,1)S(1)}, u32[]{:S(2)}, u32[]{:S(2)}) %collective-permute-start.9) | collective-permute-done | bytes 65568 | tf_op jit(solution)/shard_map/ppermute | solution.py:420
  34.4 2.2 %collective-permute-start.10 = (f32[2,32,128]{2,1,0:T(8,128)S(1)}, f32[2,32,128]{2,1,0:T(8,128)S(1)}, u32[]{:S(2)}, u32[]{:S(2)}) collective-permute-start(f32[2,32,128]{2,1,0:T(8,128)S(1)} %get-tuple-element.50), channel_id=1, source_target_pairs={{0,8},{4,12},{8,0},{12,4},{16,24},{20,28},{24,16},{28,20},{1,9},{5... | collective-permute-start | bytes 98312 | tf_op jit(solution)/shard_map/ppermute | solution.py:420
  36.6 2.4 %collective-permute-start.11 = (f32[2,32,128]{2,1,0:T(8,128)S(1)}, f32[2,32,128]{2,1,0:T(8,128)S(1)}, u32[]{:S(2)}, u32[]{:S(2)}) collective-permute-start(f32[2,32,128]{2,1,0:T(8,128)S(1)} %get-tuple-element.51), channel_id=1, source_target_pairs={{0,16},{4,20},{8,24},{12,28},{16,0},{20,4},{24,8},{28,12},{1,17},{... | collective-permute-start | bytes 98312 | tf_op jit(solution)/shard_map/ppermute | solution.py:420
  39.0 0.1 collective-permute-start.12
  39.1 2.0 %shard_map.71 = bf16[4,64,512]{2,1,0:T(8,128)(2,1)} custom-call(bf16[3,656,512]{2,1,0:T(8,128)(2,1)S(1)} %get-tuple-element.41.ps, bf16[9,4,64,128]{3,2,1,0:T(8,128)(2,1)S(1)} %get-tuple-element.42.band_ref), custom_call_target="tpu_custom_call" | custom-call | flops 2000000000 | bytes 4000000 | tf_op jit(solution)/shard_map/pallas_call | solution.py:406
  41.1 0.0 collective-permute-done.10.refs_1_
  41.1 0.6 %collective-permute-done.11.refs_2_ = f32[2,32,128]{2,1,0:T(8,128)S(1)} collective-permute-done((f32[2,32,128]{2,1,0:T(8,128)S(1)}, f32[2,32,128]{2,1,0:T(8,128)S(1)}, u32[]{:S(2)}, u32[]{:S(2)}) %collective-permute-start.11) | collective-permute-done | bytes 32800 | tf_op jit(solution)/shard_map/ppermute | solution.py:420
  41.6 3.0 %collective-permute-done.12.refs_3_ = f32[2,32,128]{2,1,0:T(8,128)S(1)} collective-permute-done((f32[2,32,128]{2,1,0:T(8,128)S(1)}, f32[2,32,128]{2,1,0:T(8,128)S(1)}, u32[]{:S(2)}, u32[]{:S(2)}) %collective-permute-start.12) | collective-permute-done | bytes 32800 | tf_op jit(solution)/shard_map/ppermute | solution.py:420
  44.7 0.6 %shard_map.74 = (f32[27,128]{1,0:T(8,128)}, f32[27,128]{1,0:T(8,128)}) custom-call(f32[2,32,128]{2,1,0:T(8,128)S(1)} %get-tuple-element.49.refs_0_, f32[2,32,128]{2,1,0:T(8,128)S(1)} %collective-permute-done.10.refs_1_, f32[2,32,128]{2,1,0:T(8,128)S(1)} %collective-permute-done.11.refs_2_, f32[2,32,128]{2,1,0:T(8,128)S(1)} %collective-permute-done.12.refs_3_), custom_call_target="tpu_custom_call" | custom-call | bytes 300000 | tf_op jit(solution)/shard_map/pallas_call | solution.py:88
  (3 shorter events, 0.1 us)
Async XLA Ops:
  2.0 9.3 %collective-permute-start = (bf16[2,2,64,512]{3,2,1,0:T(8,128)(2,1)S(1)}, bf16[2,2,64,512]{3,2,1,0:T(8,128)(2,1)S(1)}, u32[]{:S(2)}, u32[]{:S(2)}) collective-permute-start(bf16[2,2,64,512]{3,2,1,0:T(8,128)(2,1)S(1)} %get-tuple-element.31), channel_id=1, source_target_pairs={{0,4},{4,0},{8,12},{12,8},{16,20},{20,16},{24,28},{28,24},{1,5},{5... | collective-permute-start | bytes 786440 | tf_op jit(solution)/shard_map/ppermute | solution.py:23
  2.5 8.8 %collective-permute-start.1 = (bf16[2,2,64,512]{3,2,1,0:T(8,128)(2,1)S(1)}, bf16[2,2,64,512]{3,2,1,0:T(8,128)(2,1)S(1)}, u32[]{:S(2)}, u32[]{:S(2)}) collective-permute-start(bf16[2,2,64,512]{3,2,1,0:T(8,128)(2,1)S(1)} %get-tuple-element.32), channel_id=1, source_target_pairs={{4,8},{8,4},{12,16},{16,12},{20,24},{24,20},{5,9},{9,5},{13,17},{1... | collective-permute-start | bytes 786440 | tf_op jit(solution)/shard_map/ppermute | solution.py:23
  3.2 4.3 %collective-permute-start.2 = (bf16[2,4,2,512]{3,2,1,0:T(2,128)(2,1)S(1)}, bf16[2,4,2,512]{3,2,1,0:T(2,128)(2,1)S(1)}, u32[]{:S(2)}, u32[]{:S(2)}) collective-permute-start(bf16[2,4,2,512]{3,2,1,0:T(2,128)(2,1)S(1)} %get-tuple-element.33), channel_id=1, source_target_pairs={{0,1},{1,0},{2,3},{3,2},{4,5},{5,4},{6,7},{7,6},{8,9},{9,8},{10,11... | collective-permute-start | bytes 49160 | tf_op jit(solution)/shard_map/ppermute | solution.py:23
  5.8 1.7 %collective-permute-start.3 = (bf16[2,4,2,512]{3,2,1,0:T(2,128)(2,1)S(1)}, bf16[2,4,2,512]{3,2,1,0:T(2,128)(2,1)S(1)}, u32[]{:S(2)}, u32[]{:S(2)}) collective-permute-start(bf16[2,4,2,512]{3,2,1,0:T(2,128)(2,1)S(1)} %get-tuple-element.34), channel_id=1, source_target_pairs={{1,2},{2,1},{5,6},{6,5},{9,10},{10,9},{13,14},{14,13},{17,18},{18,... | collective-permute-start | bytes 49160 | tf_op jit(solution)/shard_map/ppermute | solution.py:23
  7.5 3.8 %collective-permute-start.4 = (bf16[2,2,2,2,512]{4,3,2,1,0:T(2,128)(2,1)S(1)}, bf16[2,2,2,2,512]{4,3,2,1,0:T(2,128)(2,1)S(1)}, u32[]{:S(2)}, u32[]{:S(2)}) collective-permute-start(bf16[2,2,2,2,512]{4,3,2,1,0:T(2,128)(2,1)S(1)} %get-tuple-element.35), channel_id=1, source_target_pairs={{0,4},{4,0},{8,12},{12,8},{16,20},{20,16},{24,28},{28,24},{1,5},{5... | collective-permute-start | bytes 49160 | tf_op jit(solution)/shard_map/ppermute | solution.py:23
  9.9 1.4 %collective-permute-start.5 = (bf16[2,2,2,2,512]{4,3,2,1,0:T(2,128)(2,1)S(1)}, bf16[2,2,2,2,512]{4,3,2,1,0:T(2,128)(2,1)S(1)}, u32[]{:S(2)}, u32[]{:S(2)}) collective-permute-start(bf16[2,2,2,2,512]{4,3,2,1,0:T(2,128)(2,1)S(1)} %get-tuple-element.36), channel_id=1, source_target_pairs={{4,8},{8,4},{12,16},{16,12},{20,24},{24,20},{5,9},{9,5},{13,17},{1... | collective-permute-start | bytes 49160 | tf_op jit(solution)/shard_map/ppermute | solution.py:23
  18.4 5.1 %collective-permute-start.6 = (bf16[4,4,2,32,128]{4,3,2,1,0:T(8,128)(2,1)S(1)}, bf16[4,4,2,32,128]{4,3,2,1,0:T(8,128)(2,1)S(1)}, u32[]{:S(2)}, u32[]{:S(2)}) collective-permute-start(bf16[4,4,2,32,128]{4,3,2,1,0:T(8,128)(2,1)S(1)} %get-tuple-element.44), channel_id=1, source_target_pairs={{0,4},{4,0},{8,12},{12,8},{16,20},{20,16},{24,28},{28,24},{1,5},{5... | collective-permute-start | bytes 786440 | tf_op jit(solution)/shard_map/ppermute | solution.py:420
  23.5 7.1 %collective-permute-start.7 = (bf16[4,2,32,128]{3,2,1,0:T(8,128)(2,1)S(1)}, bf16[4,2,32,128]{3,2,1,0:T(8,128)(2,1)S(1)}, u32[]{:S(2)}, u32[]{:S(2)}) collective-permute-start(bf16[4,2,32,128]{3,2,1,0:T(8,128)(2,1)S(1)} %get-tuple-element.46), channel_id=1, source_target_pairs={{0,1},{1,0},{2,3},{3,2},{4,5},{5,4},{6,7},{7,6},{8,9},{9,8},{10,11... | collective-permute-start | bytes 196616 | tf_op jit(solution)/shard_map/ppermute | solution.py:420
  27.8 4.3 %collective-permute-start.8 = (bf16[4,2,32,128]{3,2,1,0:T(8,128)(2,1)S(1)}, bf16[4,2,32,128]{3,2,1,0:T(8,128)(2,1)S(1)}, u32[]{:S(2)}, u32[]{:S(2)}) collective-permute-start(bf16[4,2,32,128]{3,2,1,0:T(8,128)(2,1)S(1)} %get-tuple-element.47), channel_id=1, source_target_pairs={{0,2},{1,3},{2,0},{3,1},{4,6},{5,7},{6,4},{7,5},{8,10},{9,11},{10,... | collective-permute-start | bytes 196616 | tf_op jit(solution)/shard_map/ppermute | solution.py:420
  29.2 5.2 %collective-permute-start.9 = (bf16[4,2,32,128]{3,2,1,0:T(8,128)(2,1)S(1)}, bf16[4,2,32,128]{3,2,1,0:T(8,128)(2,1)S(1)}, u32[]{:S(2)}, u32[]{:S(2)}) collective-permute-start(bf16[4,2,32,128]{3,2,1,0:T(8,128)(2,1)S(1)} %get-tuple-element.48), channel_id=1, source_target_pairs={{0,3},{1,2},{2,1},{3,0},{4,7},{5,6},{6,5},{7,4},{8,11},{9,10},{10,... | collective-permute-start | bytes 196616 | tf_op jit(solution)/shard_map/ppermute | solution.py:420
  34.4 6.7 %collective-permute-start.10 = (f32[2,32,128]{2,1,0:T(8,128)S(1)}, f32[2,32,128]{2,1,0:T(8,128)S(1)}, u32[]{:S(2)}, u32[]{:S(2)}) collective-permute-start(f32[2,32,128]{2,1,0:T(8,128)S(1)} %get-tuple-element.50), channel_id=1, source_target_pairs={{0,8},{4,12},{8,0},{12,4},{16,24},{20,28},{24,16},{28,20},{1,9},{5... | collective-permute-start | bytes 98312 | tf_op jit(solution)/shard_map/ppermute | solution.py:420
  36.6 5.1 %collective-permute-start.11 = (f32[2,32,128]{2,1,0:T(8,128)S(1)}, f32[2,32,128]{2,1,0:T(8,128)S(1)}, u32[]{:S(2)}, u32[]{:S(2)}) collective-permute-start(f32[2,32,128]{2,1,0:T(8,128)S(1)} %get-tuple-element.51), channel_id=1, source_target_pairs={{0,16},{4,20},{8,24},{12,28},{16,0},{20,4},{24,8},{28,12},{1,17},{... | collective-permute-start | bytes 98312 | tf_op jit(solution)/shard_map/ppermute | solution.py:420
  39.0 5.7 %collective-permute-start.12 = (f32[2,32,128]{2,1,0:T(8,128)S(1)}, f32[2,32,128]{2,1,0:T(8,128)S(1)}, u32[]{:S(2)}, u32[]{:S(2)}) collective-permute-start(f32[2,32,128]{2,1,0:T(8,128)S(1)} %get-tuple-element.52), channel_id=1, source_target_pairs={{0,24},{4,28},{8,16},{12,20},{16,8},{20,12},{24,0},{28,4},{1,25},{... | collective-permute-start | bytes 98312 | tf_op jit(solution)/shard_map/ppermute | solution.py:420

commit v4 on v3

v4 whole, which is shorter than its diff:
```python
import functools

import jax
import jax.numpy as jnp
from jax import lax
from jax.experimental import pallas as pl
from jax.experimental.pallas import tpu as pltpu
from jax.sharding import PartitionSpec as P


CH = 64
PAD = 16

root_half = 0.7071067811865476
inv_root_two_pi = 0.3989422804014327


def pair_exchange(block, axis, first):
    count = lax.axis_size(axis)
    pairs = []
    for low in range(first, count - 1, 2):
        pairs += [(low, low + 1), (low + 1, low)]
    return lax.ppermute(block, axis, pairs)


def in_hbm(block):
    return pltpu.with_memory_space_constraint(block, pltpu.HBM)


def pack_kernel(
    x_hbm, g_hbm, one_hbm, two_hbm, x_ref, g_ref, one_ref, two_ref, to_a, to_b, own_a, own_b, sems
):
    rows, cols, _ = x_ref.shape
    pairs = ((x_hbm, x_ref), (g_hbm, g_ref), (one_hbm, one_ref), (two_hbm, two_ref))
    copies = [
        pltpu.make_async_copy(source, target, sems.at[k])
        for k, (source, target) in enumerate(pairs)
    ]
    for copy in copies:
        copy.start()
    ha_even = lax.rem(lax.axis_index("ha"), 2) == 0
    wa_even = lax.rem(lax.axis_index("wa"), 2) == 0
    a_start = jnp.where(ha_even, rows - 2, 0)
    b_start = jnp.where(ha_even, 0, rows - 2)
    for which, ref in enumerate((x_ref, g_ref)):
        copies[which].wait()
        to_a[which] = ref[pl.ds(a_start, 2)]
        to_b[which] = ref[pl.ds(b_start, 2)]
        for r in range(rows):
            left, right = ref[r, 0:2, :], ref[r, cols - 2 : cols, :]
            own_a[which, r] = jnp.where(wa_even, right, left)
            own_b[which, r] = jnp.where(wa_even, left, right)
    for copy in copies[2:]:
        copy.wait()


def pack(x, g, one, two):
    rows, cols, lanes = x.shape
    vmem = pl.BlockSpec(memory_space=pltpu.VMEM)
    hbm = pl.BlockSpec(memory_space=pltpu.HBM)
    shapes = [x.shape] * 2 + [one.shape] * 2
    shapes += [(2, 2, cols, lanes)] * 2 + [(2, rows, 2, lanes)] * 2
    return pl.pallas_call(
        pack_kernel,
        out_shape=tuple(jax.ShapeDtypeStruct(shape, x.dtype) for shape in shapes),
        in_specs=[hbm] * 4,
        out_specs=(vmem,) * 8,
        scratch_shapes=[pltpu.SemaphoreType.DMA((4,))],
        compiler_params=pltpu.CompilerParams(vmem_limit_bytes=4 << 20),
        cost_estimate=pl.CostEstimate(flops=0, bytes_accessed=1_100_000, transcendentals=0),
    )(*(in_hbm(block) for block in (x, g, one, two)))


def corners_kernel(wa_ref, wb_ref, to_a, to_b):
    rows = wa_ref.shape[1]
    ha_even = lax.rem(lax.axis_index("ha"), 2) == 0
    a_start = jnp.where(ha_even, rows - 2, 0)
    b_start = jnp.where(ha_even, 0, rows - 2)
    for side, ref in enumerate((wa_ref, wb_ref)):
        for which in range(2):
            for r in range(2):
                to_a[side, which, r] = ref[which, a_start + r]
                to_b[side, which, r] = ref[which, b_start + r]


def small_call(kernel, out_shape, *operands):
    vmem = pl.BlockSpec(memory_space=pltpu.VMEM)
    return pl.pallas_call(
        kernel,
        out_shape=out_shape,
        in_specs=[vmem] * len(operands),
        out_specs=(vmem,) * len(out_shape),
        compiler_params=pltpu.CompilerParams(vmem_limit_bytes=2 << 20),
        cost_estimate=pl.CostEstimate(flops=0, bytes_accessed=300_000, transcendentals=0),
    )(*operands)


def corners(wa, wb):
    shape = jax.ShapeDtypeStruct((2, 2, 2) + wa.shape[2:], wa.dtype)
    return small_call(corners_kernel, (shape, shape), wa, wb)


def halo_selection(lines, shape):
    ha_odd = lax.rem(lax.axis_index("ha"), 2)
    wa_odd = lax.rem(lax.axis_index("wa"), 2)
    halo = 2 * lines
    gap_rows = (lines + 1) * PAD
    side_rows = 2 * lines
    q = lax.broadcasted_iota(jnp.int32, shape, 0)
    col = lax.broadcasted_iota(jnp.int32, shape, 1)

    def order(line):
        swapped = jnp.where(
            line < 2, line + lines - 2, jnp.where(line >= lines - 2, line - lines + 2, line)
        )
        return jnp.where(ha_odd == 0, swapped, line)

    left_base = jnp.where(wa_odd == 0, halo, 0)
    right_base = jnp.where(wa_odd == 0, 0, halo)
    gap = lax.div(q, PAD)
    w = lax.rem(q, PAD)
    left_hit = (w == PAD - 1) & (gap < lines) & (col == left_base + 2 * order(gap) + 1)
    right_hit = (w == 0) & (gap >= 1) & (col == right_base + 2 * order(gap - 1))
    in_gaps = (q < gap_rows) & (left_hit | right_hit)
    q = q - gap_rows
    tap = lax.div(q, side_rows)
    b = lax.rem(tap, 3)
    right = lax.div(lax.rem(q, side_rows), lines)
    line = lax.rem(q, lines) + lax.div(tap, 3) - 1
    at = order(line)
    left_source = jnp.where(b == 2, 2 * halo + at, left_base + 2 * at + b)
    right_source = jnp.where(b == 0, 2 * halo + lines + at, right_base + 2 * at + b - 1)
    source = jnp.where(right == 0, left_source, right_source)
    in_sides = (q >= 0) & (line >= 0) & (line < lines) & (col == source)
    return jnp.where(in_gaps | in_sides, 1.0, 0.0).astype(jnp.bfloat16)


def transposed(value, turned):
    flat = jnp.transpose(value)
    halves = []
    for side in range(flat.shape[1] // 128):
        turned[side] = flat[:, 128 * side : 128 * side + 128]
        pieces = [
            turned[side, pl.ds(64 * j + odd, 32, stride=2), :] for j in range(4) for odd in range(2)
        ]
        halves.append(jnp.concatenate(pieces, axis=0))
    return jnp.concatenate(halves, axis=1).astype(jnp.bfloat16)


def prepare_kernel(
    x_ref, one_ref, two_ref, one_out, two_flip_out, one_flip_out, select_out, x_t_out, turned
):
    rows = x_ref.shape[0]
    select_out[...] = halo_selection(rows + 4, select_out.shape)
    for group in range(2):
        lane = slice(256 * group, 256 * group + 256)
        own = jnp.concatenate([x_ref[r, :, lane] for r in range(rows)], axis=0)
        x_t_out[group] = transposed(own.astype(jnp.float32), turned)
    zero = jnp.zeros((CH, CH), jnp.bfloat16)

    def banded(tiles):
        padded = [zero] + tiles + [zero]
        return [jnp.concatenate([padded[c + 1], padded[c]], axis=1) for c in range(4)]

    def flipped(ref, tap):
        return jnp.transpose(ref[26 - tap].astype(jnp.float32)).astype(jnp.bfloat16)

    for ab in range(9):
        taps = [3 * ab + c for c in range(3)]
        for c, tile in enumerate(banded([one_ref[t] for t in taps])):
            one_out[ab, c] = tile
        for c, tile in enumerate(banded([flipped(two_ref, t) for t in taps])):
            two_flip_out[ab, c] = tile
        for c, tile in enumerate(banded([flipped(one_ref, t) for t in taps])):
            one_flip_out[ab, c] = tile


def prepare(x, kernel_one, kernel_two):
    rows, cols, _ = x.shape
    lines = rows + 4
    bands = jax.ShapeDtypeStruct((9, 4, CH, 2 * CH), jnp.bfloat16)
    select = ((lines + 1) * PAD + 18 * lines, 6 * lines)
    vmem = pl.BlockSpec(memory_space=pltpu.VMEM)
    return pl.pallas_call(
        prepare_kernel,
        out_shape=(
            bands,
            bands,
            bands,
            jax.ShapeDtypeStruct(select, jnp.bfloat16),
            jax.ShapeDtypeStruct((2, 256, rows * cols), jnp.bfloat16),
        ),
        in_specs=[vmem] * 3,
        out_specs=(vmem,) * 5,
        scratch_shapes=[pltpu.VMEM((rows * cols // 128, 256, 128), jnp.float32)],
        compiler_params=pltpu.CompilerParams(vmem_limit_bytes=8 << 20),
        cost_estimate=pl.CostEstimate(
            flops=4_000_000, bytes_accessed=4_000_000, transcendentals=0
        ),
    )(x, kernel_one, kernel_two)


def banded_weights(band_ref, group):
    zero = jnp.zeros((CH, 2 * CH), jnp.bfloat16)
    rows = []
    for ab in range(9):
        for i in range(5):
            halves = []
            for m in range(2):
                c = i - 2 * m + 1 - group
                halves.append(band_ref[ab, c] if 0 <= c < 4 else zero)
            rows.append(jnp.concatenate(halves, axis=1))
        if ab % 3 == 2:
            rows.append(jnp.concatenate([zero, zero], axis=1))
    return jnp.concatenate(rows, axis=0)


def gather_depths(plain, turned_lanes):
    zero = jnp.zeros_like(plain[0][0])
    low = lax.broadcasted_iota(jnp.int32, zero.shape, 1) < CH

    def part(tiles, k):
        return tiles[k]

    (p0, p1, p2), (t0, t1, t2) = plain, turned_lanes
    first = [
        part(p0, 0),
        part(p0, 1),
        jnp.where(low, part(p0, 2), part(t1, 0)),
        part(t1, 1),
        part(t1, 2),
        part(p2, 0),
        part(p2, 1),
        jnp.where(low, part(p2, 2), zero),
    ]
    second = [
        part(t0, 2),
        part(t0, 3),
        jnp.where(low, part(t0, 0), part(p1, 1)),
        part(p1, 2),
        part(p1, 3),
        part(t2, 2),
        part(t2, 3),
        jnp.where(low, part(t2, 0), zero),
    ]
    return [jnp.concatenate(half, axis=1).astype(jnp.bfloat16) for half in (first, second)]


def correlate(src, side, band_ref, cols, line, count):
    outs = []
    for group in range(2):
        windows = []
        for a in range(3):
            top = (line + a - 1) * cols
            window = src[group, top : top + count * cols, :]
            if side is not None:
                window = jnp.concatenate([window, side[group, a]], axis=0)
            windows.append(window)
        outs.append(
            jnp.dot(
                jnp.concatenate(windows, axis=1),
                banded_weights(band_ref, group),
                preferred_element_type=jnp.float32,
            )
        )
    return outs


def input_grad_kernel(rows, cols, ps, band_ref, out_ref):
    result = correlate(ps, None, band_ref, cols, 2, rows)
    for group in range(2):
        for r in range(rows):
            out_ref[r, :, 256 * group : 256 * group + 256] = result[group][
                r * cols : r * cols + cols
            ].astype(out_ref.dtype)


def main_kernel(
    rows,
    cols,
    x_ref,
    g_ref,
    ra_ref,
    rb_ref,
    wa_ref,
    wb_ref,
    corner_a_ref,
    corner_b_ref,
    one_ref,
    two_flip_ref,
    select_ref,
    x_t_ref,
    ps,
    *rest,
):
    kg_refs, scratch = rest[:-16], rest[-16:]
    xs, gs, x_side, g_side, sums, acc_one, acc_two, turned_refs = *scratch[:7], scratch[7:9]
    wide_refs, wide_turned_refs = scratch[9:12], scratch[12:15]
    edges_ref = scratch[15]
    f32, bf16 = jnp.float32, jnp.bfloat16
    stride = cols + PAD
    lines = rows + 4
    base = 8
    ha = lax.axis_index("ha")
    wa = lax.axis_index("wa")
    ha_odd = lax.rem(ha, 2)
    wa_odd = lax.rem(wa, 2)

    nothing = lax.shift_right_logical(wa, 16)

    halo = 2 * lines
    gap_rows = (lines + 1) * PAD
    side_rows = 2 * lines

    tiles = x_ref.shape[2] // 128

    def split_lanes(value):
        return [value[:, 128 * k : 128 * k + 128] for k in range(tiles)]

    def turn(parts):
        swapped = [pltpu.roll(part, CH, 1) for part in parts]
        low = lax.broadcasted_iota(jnp.int32, parts[0].shape, 1) < CH
        return [jnp.where(low, swapped[k - 1], swapped[k]) for k in range(tiles)]

    def put_wide(wide, start, count, parts, first=0):
        for k, part in enumerate(parts, first):
            wide[k, pl.ds(start, count), :] = part

    def gather_lines(which, first, last, out):
        wide, wide_turned = wide_refs[which], wide_turned_refs[which]
        top, bottom = base + first * stride, base + last * stride + PAD
        for k, value in enumerate(turn([wide[k, top - 8 : bottom + 8, :] for k in range(tiles)])):
            wide_turned[k, top - 8 : bottom + 8, :] = value
        for l in range(first, last):
            start = base + PAD + l * stride - 1
            where = [start + nothing, start + 1, start + 2 + nothing]
            plain, other = (
                [[ref[k, pl.ds(at, cols), :] for k in range(tiles)] for at in where]
                for ref in (wide, wide_turned)
            )
            for group, value in enumerate(gather_depths(plain, other)):
                out[group, l * cols : (l + 1) * cols, :] = value

    def spread(which, own_ref, out, side_out):
        wide, edges = wide_refs[which], edges_ref.at[which]
        for side, ref in enumerate((wa_ref, wb_ref)):
            pieces = (
                [corner_a_ref[side, which, r] for r in range(2)]
                + [ref[which, r] for r in range(rows)]
                + [corner_b_ref[side, which, r] for r in range(2)]
            )
            for k, piece in enumerate(pieces):
                top = side * halo + 2 * k
                edges[top : top + 2, :] = piece.astype(f32)
        owned = (
            [ra_ref[which, r].astype(f32) for r in range(2)]
            + [own_ref[r].astype(f32) for r in range(rows)]
            + [rb_ref[which, r].astype(f32) for r in range(2)]
        )
        for k, value in enumerate(owned):
            edges[2 * halo + k : 2 * halo + k + 1, :] = value[0:1, :]
            edges[2 * halo + lines + k : 2 * halo + lines + k + 1, :] = value[cols - 1 : cols, :]
        placed = jnp.dot(select_ref[...], edges[...].astype(bf16), preferred_element_type=f32)
        for k in range(lines + 1):
            put_wide(wide, base + k * stride, PAD, split_lanes(placed[k * PAD : (k + 1) * PAD]))
        for r in range(rows):
            start = base + PAD + (r + 2) * stride
            put_wide(wide, start, cols, split_lanes(owned[r + 2]))
        above = base + PAD
        below = base + PAD + (rows + 2) * stride
        a_start = jnp.where(ha_odd == 0, below, above)
        b_start = jnp.where(ha_odd == 0, above, below)
        for r in range(2):
            put_wide(wide, pl.multiple_of(a_start + r * stride, 8), cols, split_lanes(owned[r]))
            put_wide(wide, pl.multiple_of(b_start + r * stride, 8), cols, split_lanes(owned[rows + 2 + r]))
        gather_lines(which, 0, lines, out)
        for a in range(3):
            top = gap_rows + 3 * a * side_rows
            plain = [
                split_lanes(placed[top + b * side_rows : top + (b + 1) * side_rows])
                for b in range(3)
            ]
            other = [turn(parts) for parts in plain]
            for group, value in enumerate(gather_depths(plain, other)):
                side_out[group, a] = value

    count = (rows + 2) * cols
    spread(0, x_ref, xs, x_side)
    pre = correlate(xs, x_side, one_ref, cols, 1, rows + 2)
    spread(1, g_ref, gs, g_side)
    grad_active = correlate(gs, g_side, two_flip_ref, cols, 1, rows + 2)

    ha_last = lax.axis_size("ha") - 1
    wa_last = lax.axis_size("wa") - 1
    position = lax.broadcasted_iota(jnp.int32, (side_rows, 256), 0)
    line = lax.rem(position, lines)
    dead = ((line < 2) & (ha == 0)) | ((line >= rows + 2) & (ha == ha_last))
    dead = dead | ((position < lines) & (wa == 0)) | ((position >= lines) & (wa == wa_last))

    active_t, slopes = [], []
    for group in range(2):
        value = pre[group]
        cdf = 0.5 * (1.0 + lax.erf(value * root_half))
        slopes.append(cdf + value * inv_root_two_pi * jnp.exp(-0.5 * value * value))
        active = (value * cdf)[cols : cols + rows * cols]
        active_t.append(transposed(active, turned_refs[group]))

    half, lead = CH // 2, 8
    low_half = lax.broadcasted_iota(jnp.int32, (CH, 2 * CH), 1) < CH
    low = low_half[:half]

    def kernel_grad(k, fixed, src, acc_ref):
        for a in range(3):
            add_taps(k, a, kernel_grad_parts(fixed, src, acc_ref.at[a], a))

    def kernel_grad_parts(fixed, src, acc_ref, a):
        parts = [[None] * 4 for _ in range(3)]

        def put(window, e, tile):
            old = parts[2 - window][e]
            parts[2 - window][e] = tile if old is None else old + tile

        for group in range(2):
            top = (3 - a) * cols
            acc_ref[...] = jnp.dot(
                fixed[group], src[group, top : top + rows * cols, :], preferred_element_type=f32
            )
            for j in range(4):
                for t in range(8):
                    (window, i), (next_window, next_i) = divmod(2 * t, 5), divmod(2 * t + 1, 5)
                    e = j - i + 1 + group
                    c = j - next_i + 1 + group
                    joined = next_window in (window, 3)
                    use_left = 0 <= e < 4 if joined else 0 <= e < 3
                    use_right = not joined and 0 <= c < 3
                    if not (use_left or use_right):
                        continue
                    tile = acc_ref[64 * j : 64 * j + 64, 128 * t : 128 * t + 128]
                    if use_left:
                        whole = joined or e == 0
                        put(window, e, tile if whole else jnp.where(low_half, tile, 0.0))
                    if use_right:
                        whole = c == 2
                        put(next_window, c + 1, tile if whole else jnp.where(low_half, 0.0, tile))
        return parts

    def add_taps(k, a, parts):
        for b in range(3):
            for c in range(3):
                left, right = parts[b][c], parts[b][c + 1]
                tile = jnp.where(
                    low,
                    left[:half] + pltpu.roll(right[:half], CH, 1),
                    pltpu.roll(left[half:], CH, 1) + right[half:],
                )
                tap = 9 * a + 3 * b + c
                sums[k, lead + half * tap : lead + half * tap + half, :] = tile

    kernel_grad(1, active_t, gs, acc_two)

    edges = edges_ref.at[2]
    for group in range(2):
        lane = slice(256 * group, 256 * group + 256)
        grad_pre = grad_active[group] * slopes[group]
        for l in range(1, rows + 3):
            start = base + PAD + l * stride
            own = grad_pre[(l - 1) * cols : l * cols]
            if l == 1:
                own = jnp.where(ha == 0, 0.0, own)
            if l == rows + 2:
                own = jnp.where(ha == ha_last, 0.0, own)
            put_wide(wide_refs[2], start, cols, [own[:, :128], own[:, 128:]], 2 * group)
        edges[:side_rows, lane] = jnp.where(dead, 0.0, grad_pre[count:])
    for l in range(1, rows + 3):
        left, right = base + l * stride + PAD - 1, base + (l + 1) * stride
        put_wide(wide_refs[2], left, 1, split_lanes(edges[l : l + 1, :]))
        put_wide(wide_refs[2], right, 1, split_lanes(edges[lines + l : lines + l + 1, :]))
    gather_lines(2, 1, rows + 3, ps)

    kernel_grad(0, x_t_ref, ps, acc_one)

    if len(kg_refs) == 1:
        for k in range(2):
            kg_refs[0][k] = sums[k, lead : lead + 27 * half, :]
        return
    keep_ref, send_ref = kg_refs
    slabs, width, share, _ = keep_ref.shape
    take = 27 * half // (2 * slabs * width)
    full, left_over = take // 8 * 8, take % 8
    head = lax.broadcasted_iota(jnp.int32, (8, 2 * CH), 0) < left_over

    def chunk(d):
        at = lead + take * d + nothing
        first = sums[0, pl.ds(at, full + 8), :]
        second = sums[1, pl.ds(at - left_over, share - full), :]
        seam = jnp.where(head, first[full:], second[:8])
        return jnp.concatenate([first[:full], seam, second[8:]], axis=0)

    for z in range(slabs):
        for w in range(width):
            even, odd = (chunk((2 * z + c) * width + w) for c in range(2))
            keep_ref[z, w] = jnp.where(ha_odd == 0, even, odd)
            send_ref[z, w] = jnp.where(ha_odd == 0, odd, even).astype(bf16)


def main(x, g, ra, rb, wa, wb, corner_a, corner_b, one, two_flip, select, x_t, split):
    rows, cols, lanes = x.shape
    stride = cols + PAD
    span = (rows + 4) * stride + PAD
    if split:
        slabs, width = split
        take = 27 * CH // 2 // (2 * slabs * width)
        share = -(-2 * take // 8) * 8
        grads = tuple(
            jax.ShapeDtypeStruct((slabs, width, share, 2 * CH), dtype)
            for dtype in (jnp.float32, jnp.bfloat16)
        )
    else:
        grads = (jax.ShapeDtypeStruct((2, 27 * CH // 2, 2 * CH), jnp.float32),)
    vmem = pl.BlockSpec(memory_space=pltpu.VMEM)
    lines = rows + 4
    moving = (2, lines * cols, 1024)
    side = pltpu.VMEM((2, 3, 2 * lines, 1024), jnp.bfloat16)
    wide = pltpu.VMEM((lanes // 128, span + 16, 128), jnp.float32)
    turning = pltpu.VMEM((rows * cols // 128, 256, 128), jnp.float32)
    return pl.pallas_call(
        functools.partial(main_kernel, rows, cols),
        out_shape=(
            jax.ShapeDtypeStruct(moving, jnp.bfloat16),
            *grads,
        ),
        in_specs=[vmem] * 12,
        out_specs=(vmem,) * (1 + len(grads)),
        scratch_shapes=[
            pltpu.VMEM(moving, jnp.bfloat16),
            pltpu.VMEM(moving, jnp.bfloat16),
            side,
            side,
            pltpu.VMEM((2, 27 * CH // 2 + 40, 2 * CH), jnp.float32),
            pltpu.VMEM((3, 256, 1024), jnp.float32),
            pltpu.VMEM((3, 256, 1024), jnp.float32),
            turning,
            turning,
            *[wide] * 6,
            pltpu.VMEM((3, 6 * lines, lanes), jnp.float32),
        ],
        compiler_params=pltpu.CompilerParams(vmem_limit_bytes=32 << 20),
        cost_estimate=pl.CostEstimate(
            flops=14_000_000_000, bytes_accessed=8_000_000, transcendentals=1_000_000
        ),
    )(x, g, ra, rb, wa, wb, corner_a, corner_b, one, two_flip, select, x_t)


def input_grad(ps, band, shape):
    rows, cols, _ = shape
    vmem = pl.BlockSpec(memory_space=pltpu.VMEM)
    return pl.pallas_call(
        functools.partial(input_grad_kernel, rows, cols),
        out_shape=jax.ShapeDtypeStruct(shape, jnp.bfloat16),
        in_specs=[vmem, vmem],
        out_specs=vmem,
        compiler_params=pltpu.CompilerParams(vmem_limit_bytes=8 << 20),
        cost_estimate=pl.CostEstimate(
            flops=2_000_000_000, bytes_accessed=4_000_000, transcendentals=0
        ),
    )(ps, band)


def xor_exchange(block, axis, mask):
    count = lax.axis_size(axis)
    return lax.ppermute(block, axis, [(i, i ^ mask) for i in range(count)])


def total_of(refs):
    total = refs[0].astype(jnp.float32)
    for ref in refs[1:]:
        total = total + ref.astype(jnp.float32)
    return total


def sum_chip_kernel(keep_ref, got_ref, own_ref, *send_refs):
    wa = lax.axis_index("wa")
    for z in range(keep_ref.shape[0]):
        own_ref[z] = total_of([keep_ref[z, wa], got_ref[z, wa]])
        for k, ref in enumerate(send_refs, 1):
            ref[z] = total_of([keep_ref[z, wa ^ k], got_ref[z, wa ^ k]]).astype(ref.dtype)


def sum_wa_kernel(*refs):
    slabs = refs[0].shape[0]
    got_refs, (own_ref, *send_refs) = refs[:-slabs], refs[-slabs:]
    z = lax.div(lax.axis_index("ha"), 2)
    own_ref[...] = total_of([ref[z] for ref in got_refs])
    for k, ref in enumerate(send_refs, 1):
        ref[...] = total_of([got[z ^ k] for got in got_refs]).astype(ref.dtype)


def sum_z_kernel(*refs):
    total = total_of([ref[...] for ref in refs[:-2]])
    take = refs[-1].shape[0]
    for k, ref in enumerate(refs[-2:]):
        ref[...] = total[k * take : (k + 1) * take]


def reduce_chunks(keep, send, take):
    slabs, width = keep.shape[:2]
    f32, bf16 = jnp.float32, jnp.bfloat16
    unit = keep.shape[2:]
    got = xor_exchange(send, "ha", 1)
    shapes = [jax.ShapeDtypeStruct((slabs,) + unit, f32)]
    shapes += [jax.ShapeDtypeStruct((slabs,) + unit, bf16)] * (width - 1)
    own, *sends = small_call(sum_chip_kernel, tuple(shapes), keep, got)
    got = []
    for k, block in enumerate(sends, 1):
        got.append(xor_exchange(block, "wa", k))
    shapes = [jax.ShapeDtypeStruct(unit, f32)]
    shapes += [jax.ShapeDtypeStruct(unit, f32)] * (slabs - 1)
    own, *sends = small_call(sum_wa_kernel, tuple(shapes), own, *got)
    got = []
    for k, block in enumerate(sends, 1):
        got.append(xor_exchange(block, "ha", 2 * k))
    shapes = (jax.ShapeDtypeStruct((take, 2 * CH), f32),) * 2
    return small_call(sum_z_kernel, shapes, own, *got)


def shards(inputs, grad_out, kernel_one, kernel_two):
    height_count = lax.axis_size("ha")
    width_count = lax.axis_size("wa")
    devices = height_count * width_count
    x, g, kernel_one, kernel_two, to_a, to_b, own_a, own_b = pack(
        inputs, grad_out, kernel_one, kernel_two
    )
    wb = pair_exchange(own_b, "wa", 1)
    wa = pair_exchange(own_a, "wa", 0)
    ra = pair_exchange(to_a, "ha", 0)
    rb = pair_exchange(to_b, "ha", 1)
    one, two_flip, one_flip, select, x_t = prepare(x, kernel_one, kernel_two)
    corner_to_a, corner_to_b = corners(wa, wb)
    corner_b = pair_exchange(corner_to_b, "ha", 1)
    corner_a = pair_exchange(corner_to_a, "ha", 0)

    split = None
    if (
        (27 * CH // 2) % devices == 0
        and height_count & (height_count - 1) == 0
        and width_count & (width_count - 1) == 0
        and height_count > 1
    ):
        split = (height_count // 2, width_count)
    ps, *grads = main(x, g, ra, rb, wa, wb, corner_a, corner_b, one, two_flip, select, x_t, split)
    grad_inputs = input_grad(ps, one_flip, inputs.shape)
    if split:
        grads = reduce_chunks(*grads, 27 * CH // 2 // devices)
    else:
        grads = [
            lax.psum_scatter(
                grads[0][k].reshape(devices, -1), ("ha", "wa"), scatter_dimension=0, tiled=True
            )
            for k in range(2)
        ]
    return (grad_inputs, grads[0].reshape(-1), grads[1].reshape(-1))


def solution(mesh):
    return jax.shard_map(
        shards,
        mesh=mesh,
        in_specs=(P("ha", "wa", None), P("ha", "wa", None), P(), P()),
        out_specs=(P("ha", "wa", None), P(("ha", "wa")), P(("ha", "wa"))),
        check_vma=False,
    )
```

time: 45.5 us -> 44.3 us (0.974)
  Pallas kernels: 11.8 us -> 10.7 us
    pallas_call x1, Pallas kernels: 7.08 us -> 6.05 us  [main(): pl.pallas_call(functools.partial(main_kernel, rows, cols), out_shape=(jax...]
where the time goes in v4:
time: 44.3 us; the launch traced here: 44.1 us
  starting transfers between devices  22.9 us (52%)
  Pallas kernels  10.7 us (24%)
  waiting for transfers between devices  9.77 us (22%)
  between operations  0.72 us (2%)
    ppermute x7, starting transfers between devices, xor_exchange(): return lax.ppermute(block, axis, [(i, i ^ mask) for i in range(count)])  15.4 us
    ppermute x7, waiting for transfers between devices, xor_exchange(): return lax.ppermute(block, axis, [(i, i ^ mask) for i in range(count)])  8.7 us
    ppermute x6, starting transfers between devices, pair_exchange(): return lax.ppermute(block, axis, pairs)  7.45 us
    pallas_call x1, Pallas kernels, main(): pl.pallas_call(functools.partial(main_kernel, rows, cols), out_shape=(jax...  6.05 us
    pallas_call x1, Pallas kernels, input_grad(): pl.pallas_call(functools.partial(input_grad_kernel, rows, cols), out_shap...  1.68 us
    pallas_call x1, Pallas kernels, pack(): pl.pallas_call(pack_kernel, out_shape=tuple((jax.ShapeDtypeStruct(shape,...  1.34 us
    ppermute x6, waiting for transfers between devices, pair_exchange(): return lax.ppermute(block, axis, pairs)  1.07 us
    pallas_call x1, Pallas kernels, prepare(): pl.pallas_call(prepare_kernel, out_shape=(bands, bands, bands, jax.ShapeD...  0.94 us
  transfers between devices with their start and end apart: 13, of which 6 were waited for; matrix products, arithmetic and copies ran while one was open for 0% of the time, Pallas kernels for 6%

profile of v4, /device:TPU:0, one launch (start us, length us, event | category | flops | bytes accessed | tf_op | source)
XLA Modules:
  0.0 44.1 jit_solution(2269477451532804194)
XLA Ops:
  0.6 1.3 %shard_map.67 = (bf16[4,64,512]{2,1,0:T(8,128)(2,1)S(1)}, bf16[4,64,512]{2,1,0:T(8,128)(2,1)S(1)}, bf16[27,64,64]{2,1,0:T(8,128)(2,1)S(1)}, bf16[27,64,64]{2,1,0...) custom-call(bf16[4,64,512]{2,1,0:T(8,128)(2,1)} %x_hbm.1, ...), custom_call_target="tpu_custom_call" | custom-call | bytes 1100000 | tf_op jit(solution)/shard_map/pallas_call | solution.py:63
  2.0 0.6 %collective-permute-start = (bf16[2,2,64,512]{3,2,1,0:T(8,128)(2,1)S(1)}, bf16[2,2,64,512]{3,2,1,0:T(8,128)(2,1)S(1)}, u32[]{:S(2)}, u32[]{:S(2)}) collective-permute-start(bf16[2,2,64,512]{3,2,1,0:T(8,128)(2,1)S(1)} %get-tuple-element.33), channel_id=1, source_target_pairs={{0,4},{4,0},{8,12},{12,8},{16,20},{20,16},{24,28},{28,24},{1,5},{5... | collective-permute-start | bytes 786440 | tf_op jit(solution)/shard_map/ppermute | solution.py:23
  2.5 0.7 %collective-permute-start.1 = (bf16[2,2,64,512]{3,2,1,0:T(8,128)(2,1)S(1)}, bf16[2,2,64,512]{3,2,1,0:T(8,128)(2,1)S(1)}, u32[]{:S(2)}, u32[]{:S(2)}) collective-permute-start(bf16[2,2,64,512]{3,2,1,0:T(8,128)(2,1)S(1)} %get-tuple-element.34), channel_id=1, source_target_pairs={{4,8},{8,4},{12,16},{16,12},{20,24},{24,20},{5,9},{9,5},{13,17},{1... | collective-permute-start | bytes 786440 | tf_op jit(solution)/shard_map/ppermute | solution.py:23
  3.2 2.6 %collective-permute-start.2 = (bf16[2,4,2,512]{3,2,1,0:T(2,128)(2,1)S(1)}, bf16[2,4,2,512]{3,2,1,0:T(2,128)(2,1)S(1)}, u32[]{:S(2)}, u32[]{:S(2)}) collective-permute-start(bf16[2,4,2,512]{3,2,1,0:T(2,128)(2,1)S(1)} %get-tuple-element.35), channel_id=1, source_target_pairs={{0,1},{1,0},{2,3},{3,2},{4,5},{5,4},{6,7},{7,6},{8,9},{9,8},{10,11... | collective-permute-start | bytes 49160 | tf_op jit(solution)/shard_map/ppermute | solution.py:23
  5.8 0.7 %collective-permute-start.3 = (bf16[2,4,2,512]{3,2,1,0:T(2,128)(2,1)S(1)}, bf16[2,4,2,512]{3,2,1,0:T(2,128)(2,1)S(1)}, u32[]{:S(2)}, u32[]{:S(2)}) collective-permute-start(bf16[2,4,2,512]{3,2,1,0:T(2,128)(2,1)S(1)} %get-tuple-element.36), channel_id=1, source_target_pairs={{1,2},{2,1},{5,6},{6,5},{9,10},{10,9},{13,14},{14,13},{17,18},{18,... | collective-permute-start | bytes 49160 | tf_op jit(solution)/shard_map/ppermute | solution.py:23
  6.4 1.1 %collective-permute-done.2.wa_ref = bf16[2,4,2,512]{3,2,1,0:T(2,128)(2,1)S(1)} collective-permute-done((bf16[2,4,2,512]{3,2,1,0:T(2,128)(2,1)S(1)}, bf16[2,4,2,512]{3,2,1,0:T(2,128)(2,1)S(1)}, u32[]{:S(2)}, u32[]{:S(2)}) %collective-permute-start.2) | collective-permute-done | bytes 16416 | tf_op jit(solution)/shard_map/ppermute | solution.py:23
  7.5 0.0 collective-permute-done.3.wb_ref
  7.5 2.4 %collective-permute-start.4 = (bf16[2,2,2,2,512]{4,3,2,1,0:T(2,128)(2,1)S(1)}, bf16[2,2,2,2,512]{4,3,2,1,0:T(2,128)(2,1)S(1)}, u32[]{:S(2)}, u32[]{:S(2)}) collective-permute-start(bf16[2,2,2,2,512]{4,3,2,1,0:T(2,128)(2,1)S(1)} %get-tuple-element.37), channel_id=1, source_target_pairs={{0,4},{4,0},{8,12},{12,8},{16,20},{20,16},{24,28},{28,24},{1,5},{5... | collective-permute-start | bytes 49160 | tf_op jit(solution)/shard_map/ppermute | solution.py:23
  9.9 0.7 %collective-permute-start.5 = (bf16[2,2,2,2,512]{4,3,2,1,0:T(2,128)(2,1)S(1)}, bf16[2,2,2,2,512]{4,3,2,1,0:T(2,128)(2,1)S(1)}, u32[]{:S(2)}, u32[]{:S(2)}) collective-permute-start(bf16[2,2,2,2,512]{4,3,2,1,0:T(2,128)(2,1)S(1)} %get-tuple-element.38), channel_id=1, source_target_pairs={{4,8},{8,4},{12,16},{16,12},{20,24},{24,20},{5,9},{9,5},{13,17},{1... | collective-permute-start | bytes 49160 | tf_op jit(solution)/shard_map/ppermute | solution.py:23
  10.5 0.9 %shard_map.69 = (bf16[9,4,64,128]{3,2,1,0:T(8,128)(2,1)S(1)}, bf16[9,4,64,128]{3,2,1,0:T(8,128)(2,1)S(1)}, bf16[9,4,64,128]{3,2,1,0:T(8,128)(2,1)S(1)}, bf16[288...) custom-call(bf16[4,64,512]{2,1,0:T(8,128)(2,1)S(1)} %get-tuple-element.31.x_ref, ...), custom_call_target="tpu_custom_call" | custom-call | flops 4000000 | bytes 4000000 | tf_op jit(solution)/shard_map/pallas_call | solution.py:184
  11.5 0.0 collective-permute-done.4.corner_a_ref
  11.5 0.0 collective-permute-done.5.corner_b_ref
  11.5 0.0 collective-permute-done.ra_ref
  11.5 0.0 collective-permute-done.1.rb_ref
  11.5 6.1 %shard_map.70 = (bf16[2,512,1024]{2,1,0:T(8,128)(2,1)S(1)}, f32[4,4,56,128]{3,2,1,0:T(8,128)S(1)}, bf16[4,4,56,128]{3,2,1,0:T(8,128)(2,1)S(1)}) custom-call(bf16[4,64,512]{2,1,0:T(8,128)(2,1)S(1)} %get-tuple-element.31.x_ref, bf16[4,64,512]{2,1,0:T(8,128)(2,1)S(1)} %get-tuple-element.32.g_ref, bf16[2,2,64,512]{3,2,1,0:T(8,128)(2,1)S(1)} %collective-permute-done.ra_ref, ...), custom_call_target="tpu_custom_call" | custom-call | flops 14000000000 | bytes 8000000 | tf_op jit(solution)/shard_map/pallas_call | solution.py:526
  17.6 3.7 %collective-permute-start.6 = (bf16[4,4,56,128]{3,2,1,0:T(8,128)(2,1)S(1)}, bf16[4,4,56,128]{3,2,1,0:T(8,128)(2,1)S(1)}, u32[]{:S(2)}, u32[]{:S(2)}) collective-permute-start(bf16[4,4,56,128]{3,2,1,0:T(8,128)(2,1)S(1)} %get-tuple-element.48), channel_id=1, source_target_pairs={{0,4},{4,0},{8,12},{12,8},{16,20},{20,16},{24,28},{28,24},{1,5},{5... | collective-permute-start | bytes 688136 | tf_op jit(solution)/shard_map/ppermute | solution.py:571
  21.3 1.1 %collective-permute-done.6.got_ref = bf16[4,4,56,128]{3,2,1,0:T(8,128)(2,1)S(1)} collective-permute-done((bf16[4,4,56,128]{3,2,1,0:T(8,128)(2,1)S(1)}, bf16[4,4,56,128]{3,2,1,0:T(8,128)(2,1)S(1)}, u32[]{:S(2)}, u32[]{:S(2)}) %collective-permute-start.6) | collective-permute-done | bytes 229408 | tf_op jit(solution)/shard_map/ppermute | solution.py:571
  22.4 0.1 shard_map.72
  22.5 4.3 %collective-permute-start.7 = (bf16[4,56,128]{2,1,0:T(8,128)(2,1)S(1)}, bf16[4,56,128]{2,1,0:T(8,128)(2,1)S(1)}, u32[]{:S(2)}, u32[]{:S(2)}) collective-permute-start(bf16[4,56,128]{2,1,0:T(8,128)(2,1)S(1)} %get-tuple-element.50), channel_id=1, source_target_pairs={{0,1},{1,0},{2,3},{3,2},{4,5},{5,4},{6,7},{7,6},{8,9},{9,8},{10,11... | collective-permute-start | bytes 172040 | tf_op jit(solution)/shard_map/ppermute | solution.py:571
  26.8 1.4 %collective-permute-start.8 = (bf16[4,56,128]{2,1,0:T(8,128)(2,1)S(1)}, bf16[4,56,128]{2,1,0:T(8,128)(2,1)S(1)}, u32[]{:S(2)}, u32[]{:S(2)}) collective-permute-start(bf16[4,56,128]{2,1,0:T(8,128)(2,1)S(1)} %get-tuple-element.51), channel_id=1, source_target_pairs={{0,2},{1,3},{2,0},{3,1},{4,6},{5,7},{6,4},{7,5},{8,10},{9,11},{10,... | collective-permute-start | bytes 172040 | tf_op jit(solution)/shard_map/ppermute | solution.py:571
  28.1 1.4 %collective-permute-start.9 = (bf16[4,56,128]{2,1,0:T(8,128)(2,1)S(1)}, bf16[4,56,128]{2,1,0:T(8,128)(2,1)S(1)}, u32[]{:S(2)}, u32[]{:S(2)}) collective-permute-start(bf16[4,56,128]{2,1,0:T(8,128)(2,1)S(1)} %get-tuple-element.52), channel_id=1, source_target_pairs={{0,3},{1,2},{2,1},{3,0},{4,7},{5,6},{6,5},{7,4},{8,11},{9,10},{10,... | collective-permute-start | bytes 172040 | tf_op jit(solution)/shard_map/ppermute | solution.py:571
  29.5 0.0 collective-permute-done.7.refs_1_
  29.5 1.4 %collective-permute-done.8.refs_2_ = bf16[4,56,128]{2,1,0:T(8,128)(2,1)S(1)} collective-permute-done((bf16[4,56,128]{2,1,0:T(8,128)(2,1)S(1)}, bf16[4,56,128]{2,1,0:T(8,128)(2,1)S(1)}, u32[]{:S(2)}, u32[]{:S(2)}) %collective-permute-start.8) | collective-permute-done | bytes 57376 | tf_op jit(solution)/shard_map/ppermute | solution.py:571
  30.9 2.3 %collective-permute-done.9.refs_3_ = bf16[4,56,128]{2,1,0:T(8,128)(2,1)S(1)} collective-permute-done((bf16[4,56,128]{2,1,0:T(8,128)(2,1)S(1)}, bf16[4,56,128]{2,1,0:T(8,128)(2,1)S(1)}, u32[]{:S(2)}, u32[]{:S(2)}) %collective-permute-start.9) | collective-permute-done | bytes 57376 | tf_op jit(solution)/shard_map/ppermute | solution.py:571
  33.3 2.2 %collective-permute-start.10 = (f32[56,128]{1,0:T(8,128)S(1)}, f32[56,128]{1,0:T(8,128)S(1)}, u32[]{:S(2)}, u32[]{:S(2)}) collective-permute-start(f32[56,128]{1,0:T(8,128)S(1)} %get-tuple-element.54), channel_id=1, source_target_pairs={{0,8},{4,12},{8,0},{12,4},{16,24},{20,28},{24,16},{28,20},{1,9},{5... | collective-permute-start | bytes 86024 | tf_op jit(solution)/shard_map/ppermute | solution.py:571
  35.4 2.4 %collective-permute-start.11 = (f32[56,128]{1,0:T(8,128)S(1)}, f32[56,128]{1,0:T(8,128)S(1)}, u32[]{:S(2)}, u32[]{:S(2)}) collective-permute-start(f32[56,128]{1,0:T(8,128)S(1)} %get-tuple-element.55), channel_id=1, source_target_pairs={{0,16},{4,20},{8,24},{12,28},{16,0},{20,4},{24,8},{28,12},{1,17},{... | collective-permute-start | bytes 86024 | tf_op jit(solution)/shard_map/ppermute | solution.py:571
  37.8 0.1 collective-permute-start.12
  37.9 1.7 %shard_map.71 = bf16[4,64,512]{2,1,0:T(8,128)(2,1)} custom-call(bf16[2,512,1024]{2,1,0:T(8,128)(2,1)S(1)} %get-tuple-element.45.ps, bf16[9,4,64,128]{3,2,1,0:T(8,128)(2,1)S(1)} %get-tuple-element.46.band_ref), custom_call_target="tpu_custom_call" | custom-call | flops 2000000000 | bytes 4000000 | tf_op jit(solution)/shard_map/pallas_call | solution.py:557
  39.6 0.0 collective-permute-done.10.refs_1_
  39.6 0.8 %collective-permute-done.11.refs_2_ = f32[56,128]{1,0:T(8,128)S(1)} collective-permute-done((f32[56,128]{1,0:T(8,128)S(1)}, f32[56,128]{1,0:T(8,128)S(1)}, u32[]{:S(2)}, u32[]{:S(2)}) %collective-permute-start.11) | collective-permute-done | bytes 28704 | tf_op jit(solution)/shard_map/ppermute | solution.py:571
  40.4 3.1 %collective-permute-done.12.refs_3_ = f32[56,128]{1,0:T(8,128)S(1)} collective-permute-done((f32[56,128]{1,0:T(8,128)S(1)}, f32[56,128]{1,0:T(8,128)S(1)}, u32[]{:S(2)}, u32[]{:S(2)}) %collective-permute-start.12) | collective-permute-done | bytes 28704 | tf_op jit(solution)/shard_map/ppermute | solution.py:571
  43.5 0.6 %shard_map.74 = (f32[27,128]{1,0:T(8,128)}, f32[27,128]{1,0:T(8,128)}) custom-call(f32[56,128]{1,0:T(8,128)S(1)} %get-tuple-element.53.refs_0_, f32[56,128]{1,0:T(8,128)S(1)} %collective-permute-done.10.refs_1_, f32[56,128]{1,0:T(8,128)S(1)} %collective-permute-done.11.refs_2_, f32[56,128]{1,0:T(8,128)S(1)} %collective-permute-done.12.refs_3_), custom_call_target="tpu_custom_call" | custom-call | bytes 300000 | tf_op jit(solution)/shard_map/pallas_call | solution.py:88
  (2 shorter events, 0.0 us)
Async XLA Ops:
  2.0 9.5 %collective-permute-start = (bf16[2,2,64,512]{3,2,1,0:T(8,128)(2,1)S(1)}, bf16[2,2,64,512]{3,2,1,0:T(8,128)(2,1)S(1)}, u32[]{:S(2)}, u32[]{:S(2)}) collective-permute-start(bf16[2,2,64,512]{3,2,1,0:T(8,128)(2,1)S(1)} %get-tuple-element.33), channel_id=1, source_target_pairs={{0,4},{4,0},{8,12},{12,8},{16,20},{20,16},{24,28},{28,24},{1,5},{5... | collective-permute-start | bytes 786440 | tf_op jit(solution)/shard_map/ppermute | solution.py:23
  2.5 9.0 %collective-permute-start.1 = (bf16[2,2,64,512]{3,2,1,0:T(8,128)(2,1)S(1)}, bf16[2,2,64,512]{3,2,1,0:T(8,128)(2,1)S(1)}, u32[]{:S(2)}, u32[]{:S(2)}) collective-permute-start(bf16[2,2,64,512]{3,2,1,0:T(8,128)(2,1)S(1)} %get-tuple-element.34), channel_id=1, source_target_pairs={{4,8},{8,4},{12,16},{16,12},{20,24},{24,20},{5,9},{9,5},{13,17},{1... | collective-permute-start | bytes 786440 | tf_op jit(solution)/shard_map/ppermute | solution.py:23
  3.2 4.3 %collective-permute-start.2 = (bf16[2,4,2,512]{3,2,1,0:T(2,128)(2,1)S(1)}, bf16[2,4,2,512]{3,2,1,0:T(2,128)(2,1)S(1)}, u32[]{:S(2)}, u32[]{:S(2)}) collective-permute-start(bf16[2,4,2,512]{3,2,1,0:T(2,128)(2,1)S(1)} %get-tuple-element.35), channel_id=1, source_target_pairs={{0,1},{1,0},{2,3},{3,2},{4,5},{5,4},{6,7},{7,6},{8,9},{9,8},{10,11... | collective-permute-start | bytes 49160 | tf_op jit(solution)/shard_map/ppermute | solution.py:23
  5.8 1.7 %collective-permute-start.3 = (bf16[2,4,2,512]{3,2,1,0:T(2,128)(2,1)S(1)}, bf16[2,4,2,512]{3,2,1,0:T(2,128)(2,1)S(1)}, u32[]{:S(2)}, u32[]{:S(2)}) collective-permute-start(bf16[2,4,2,512]{3,2,1,0:T(2,128)(2,1)S(1)} %get-tuple-element.36), channel_id=1, source_target_pairs={{1,2},{2,1},{5,6},{6,5},{9,10},{10,9},{13,14},{14,13},{17,18},{18,... | collective-permute-start | bytes 49160 | tf_op jit(solution)/shard_map/ppermute | solution.py:23
  7.5 4.0 %collective-permute-start.4 = (bf16[2,2,2,2,512]{4,3,2,1,0:T(2,128)(2,1)S(1)}, bf16[2,2,2,2,512]{4,3,2,1,0:T(2,128)(2,1)S(1)}, u32[]{:S(2)}, u32[]{:S(2)}) collective-permute-start(bf16[2,2,2,2,512]{4,3,2,1,0:T(2,128)(2,1)S(1)} %get-tuple-element.37), channel_id=1, source_target_pairs={{0,4},{4,0},{8,12},{12,8},{16,20},{20,16},{24,28},{28,24},{1,5},{5... | collective-permute-start | bytes 49160 | tf_op jit(solution)/shard_map/ppermute | solution.py:23
  9.9 1.6 %collective-permute-start.5 = (bf16[2,2,2,2,512]{4,3,2,1,0:T(2,128)(2,1)S(1)}, bf16[2,2,2,2,512]{4,3,2,1,0:T(2,128)(2,1)S(1)}, u32[]{:S(2)}, u32[]{:S(2)}) collective-permute-start(bf16[2,2,2,2,512]{4,3,2,1,0:T(2,128)(2,1)S(1)} %get-tuple-element.38), channel_id=1, source_target_pairs={{4,8},{8,4},{12,16},{16,12},{20,24},{24,20},{5,9},{9,5},{13,17},{1... | collective-permute-start | bytes 49160 | tf_op jit(solution)/shard_map/ppermute | solution.py:23
  17.6 4.8 %collective-permute-start.6 = (bf16[4,4,56,128]{3,2,1,0:T(8,128)(2,1)S(1)}, bf16[4,4,56,128]{3,2,1,0:T(8,128)(2,1)S(1)}, u32[]{:S(2)}, u32[]{:S(2)}) collective-permute-start(bf16[4,4,56,128]{3,2,1,0:T(8,128)(2,1)S(1)} %get-tuple-element.48), channel_id=1, source_target_pairs={{0,4},{4,0},{8,12},{12,8},{16,20},{20,16},{24,28},{28,24},{1,5},{5... | collective-permute-start | bytes 688136 | tf_op jit(solution)/shard_map/ppermute | solution.py:571
  22.5 7.1 %collective-permute-start.7 = (bf16[4,56,128]{2,1,0:T(8,128)(2,1)S(1)}, bf16[4,56,128]{2,1,0:T(8,128)(2,1)S(1)}, u32[]{:S(2)}, u32[]{:S(2)}) collective-permute-start(bf16[4,56,128]{2,1,0:T(8,128)(2,1)S(1)} %get-tuple-element.50), channel_id=1, source_target_pairs={{0,1},{1,0},{2,3},{3,2},{4,5},{5,4},{6,7},{7,6},{8,9},{9,8},{10,11... | collective-permute-start | bytes 172040 | tf_op jit(solution)/shard_map/ppermute | solution.py:571
  26.8 4.2 %collective-permute-start.8 = (bf16[4,56,128]{2,1,0:T(8,128)(2,1)S(1)}, bf16[4,56,128]{2,1,0:T(8,128)(2,1)S(1)}, u32[]{:S(2)}, u32[]{:S(2)}) collective-permute-start(bf16[4,56,128]{2,1,0:T(8,128)(2,1)S(1)} %get-tuple-element.51), channel_id=1, source_target_pairs={{0,2},{1,3},{2,0},{3,1},{4,6},{5,7},{6,4},{7,5},{8,10},{9,11},{10,... | collective-permute-start | bytes 172040 | tf_op jit(solution)/shard_map/ppermute | solution.py:571
  28.1 5.1 %collective-permute-start.9 = (bf16[4,56,128]{2,1,0:T(8,128)(2,1)S(1)}, bf16[4,56,128]{2,1,0:T(8,128)(2,1)S(1)}, u32[]{:S(2)}, u32[]{:S(2)}) collective-permute-start(bf16[4,56,128]{2,1,0:T(8,128)(2,1)S(1)} %get-tuple-element.52), channel_id=1, source_target_pairs={{0,3},{1,2},{2,1},{3,0},{4,7},{5,6},{6,5},{7,4},{8,11},{9,10},{10,... | collective-permute-start | bytes 172040 | tf_op jit(solution)/shard_map/ppermute | solution.py:571
  33.3 6.3 %collective-permute-start.10 = (f32[56,128]{1,0:T(8,128)S(1)}, f32[56,128]{1,0:T(8,128)S(1)}, u32[]{:S(2)}, u32[]{:S(2)}) collective-permute-start(f32[56,128]{1,0:T(8,128)S(1)} %get-tuple-element.54), channel_id=1, source_target_pairs={{0,8},{4,12},{8,0},{12,4},{16,24},{20,28},{24,16},{28,20},{1,9},{5... | collective-permute-start | bytes 86024 | tf_op jit(solution)/shard_map/ppermute | solution.py:571
  35.4 4.9 %collective-permute-start.11 = (f32[56,128]{1,0:T(8,128)S(1)}, f32[56,128]{1,0:T(8,128)S(1)}, u32[]{:S(2)}, u32[]{:S(2)}) collective-permute-start(f32[56,128]{1,0:T(8,128)S(1)} %get-tuple-element.55), channel_id=1, source_target_pairs={{0,16},{4,20},{8,24},{12,28},{16,0},{20,4},{24,8},{28,12},{1,17},{... | collective-permute-start | bytes 86024 | tf_op jit(solution)/shard_map/ppermute | solution.py:571
  37.8 5.7 %collective-permute-start.12 = (f32[56,128]{1,0:T(8,128)S(1)}, f32[56,128]{1,0:T(8,128)S(1)}, u32[]{:S(2)}, u32[]{:S(2)}) collective-permute-start(f32[56,128]{1,0:T(8,128)S(1)} %get-tuple-element.56), channel_id=1, source_target_pairs={{0,24},{4,28},{8,16},{12,20},{16,8},{20,12},{24,0},{28,4},{1,25},{... | collective-permute-start | bytes 86024 | tf_op jit(solution)/shard_map/ppermute | solution.py:571

commit v5 on v4

--- a/solution.py
+++ b/solution.py
@@ -148,14 +148,9 @@
 
 
 def prepare_kernel(
-    x_ref, one_ref, two_ref, one_out, two_flip_out, one_flip_out, select_out, x_t_out, turned
+    lines, one_ref, two_ref, one_out, two_flip_out, one_flip_out, select_out
 ):
-    rows = x_ref.shape[0]
-    select_out[...] = halo_selection(rows + 4, select_out.shape)
-    for group in range(2):
-        lane = slice(256 * group, 256 * group + 256)
-        own = jnp.concatenate([x_ref[r, :, lane] for r in range(rows)], axis=0)
-        x_t_out[group] = transposed(own.astype(jnp.float32), turned)
+    select_out[...] = halo_selection(lines, select_out.shape)
     zero = jnp.zeros((CH, CH), jnp.bfloat16)
 
     def banded(tiles):
@@ -175,29 +170,20 @@
             one_flip_out[ab, c] = tile
 
 
-def prepare(x, kernel_one, kernel_two):
-    rows, cols, _ = x.shape
-    lines = rows + 4
+def prepare(lines, kernel_one, kernel_two):
     bands = jax.ShapeDtypeStruct((9, 4, CH, 2 * CH), jnp.bfloat16)
     select = ((lines + 1) * PAD + 18 * lines, 6 * lines)
     vmem = pl.BlockSpec(memory_space=pltpu.VMEM)
     return pl.pallas_call(
-        prepare_kernel,
-        out_shape=(
-            bands,
-            bands,
-            bands,
-            jax.ShapeDtypeStruct(select, jnp.bfloat16),
-            jax.ShapeDtypeStruct((2, 256, rows * cols), jnp.bfloat16),
-        ),
-        in_specs=[vmem] * 3,
-        out_specs=(vmem,) * 5,
-        scratch_shapes=[pltpu.VMEM((rows * cols // 128, 256, 128), jnp.float32)],
+        functools.partial(prepare_kernel, lines),
+        out_shape=(bands, bands, bands, jax.ShapeDtypeStruct(select, jnp.bfloat16)),
+        in_specs=[vmem] * 2,
+        out_specs=(vmem,) * 4,
         compiler_params=pltpu.CompilerParams(vmem_limit_bytes=8 << 20),
         cost_estimate=pl.CostEstimate(
             flops=4_000_000, bytes_accessed=4_000_000, transcendentals=0
         ),
-    )(x, kernel_one, kernel_two)
+    )(kernel_one, kernel_two)
 
 
 def banded_weights(band_ref, group):
@@ -246,16 +232,18 @@
     return [jnp.concatenate(half, axis=1).astype(jnp.bfloat16) for half in (first, second)]
 
 
-def correlate(src, side, band_ref, cols, line, count):
+def correlate(src, side, band_ref, cols, runs):
     outs = []
     for group in range(2):
         windows = []
         for a in range(3):
-            top = (line + a - 1) * cols
-            window = src[group, top : top + count * cols, :]
+            parts = [
+                src[group, (line + a - 1) * cols : (line + a - 1 + count) * cols, :]
+                for line, count in runs
+            ]
             if side is not None:
-                window = jnp.concatenate([window, side[group, a]], axis=0)
-            windows.append(window)
+                parts.append(side[group, a])
+            windows.append(parts[0] if len(parts) == 1 else jnp.concatenate(parts, axis=0))
         outs.append(
             jnp.dot(
                 jnp.concatenate(windows, axis=1),
@@ -267,7 +255,7 @@
 
 
 def input_grad_kernel(rows, cols, ps, band_ref, out_ref):
-    result = correlate(ps, None, band_ref, cols, 2, rows)
+    result = correlate(ps, None, band_ref, cols, [(2, rows)])
     for group in range(2):
         for r in range(rows):
             out_ref[r, :, 256 * group : 256 * group + 256] = result[group][
@@ -275,28 +263,10 @@
             ].astype(out_ref.dtype)
 
 
-def main_kernel(
-    rows,
-    cols,
-    x_ref,
-    g_ref,
-    ra_ref,
-    rb_ref,
-    wa_ref,
-    wb_ref,
-    corner_a_ref,
-    corner_b_ref,
-    one_ref,
-    two_flip_ref,
-    select_ref,
-    x_t_ref,
-    ps,
-    *rest,
+def field_tools(
+    rows, cols, ra_ref, rb_ref, wa_ref, wb_ref, corner_a_ref, corner_b_ref, select_ref, scratch
 ):
-    kg_refs, scratch = rest[:-16], rest[-16:]
-    xs, gs, x_side, g_side, sums, acc_one, acc_two, turned_refs = *scratch[:7], scratch[7:9]
-    wide_refs, wide_turned_refs = scratch[9:12], scratch[12:15]
-    edges_ref = scratch[15]
+    wide_refs, wide_turned_refs, edges_ref = scratch
     f32, bf16 = jnp.float32, jnp.bfloat16
     stride = cols + PAD
     lines = rows + 4
@@ -312,7 +282,7 @@
     gap_rows = (lines + 1) * PAD
     side_rows = 2 * lines
 
-    tiles = x_ref.shape[2] // 128
+    tiles = ra_ref.shape[3] // 128
 
     def split_lanes(value):
         return [value[:, 128 * k : 128 * k + 128] for k in range(tiles)]
@@ -341,7 +311,7 @@
             for group, value in enumerate(gather_depths(plain, other)):
                 out[group, l * cols : (l + 1) * cols, :] = value
 
-    def spread(which, own_ref, out, side_out):
+    def spread(which, own_ref, out, side_out, gathered):
         wide, edges = wide_refs[which], edges_ref.at[which]
         for side, ref in enumerate((wa_ref, wb_ref)):
             pieces = (
@@ -360,7 +330,8 @@
         for k, value in enumerate(owned):
             edges[2 * halo + k : 2 * halo + k + 1, :] = value[0:1, :]
             edges[2 * halo + lines + k : 2 * halo + lines + k + 1, :] = value[cols - 1 : cols, :]
-        placed = jnp.dot(select_ref[...], edges[...].astype(bf16), preferred_element_type=f32)
+        used = gap_rows if side_out is None else select_ref.shape[0]
+        placed = jnp.dot(select_ref[:used], edges[...].astype(bf16), preferred_element_type=f32)
         for k in range(lines + 1):
             put_wide(wide, base + k * stride, PAD, split_lanes(placed[k * PAD : (k + 1) * PAD]))
         for r in range(rows):
@@ -373,8 +344,9 @@
         for r in range(2):
             put_wide(wide, pl.multiple_of(a_start + r * stride, 8), cols, split_lanes(owned[r]))
             put_wide(wide, pl.multiple_of(b_start + r * stride, 8), cols, split_lanes(owned[rows + 2 + r]))
-        gather_lines(which, 0, lines, out)
-        for a in range(3):
+        for first, last in gathered:
+            gather_lines(which, first, last, out)
+        for a in range(0 if side_out is None else 3):
             top = gap_rows + 3 * a * side_rows
             plain = [
                 split_lanes(placed[top + b * side_rows : top + (b + 1) * side_rows])
@@ -384,34 +356,61 @@
             for group, value in enumerate(gather_depths(plain, other)):
                 side_out[group, a] = value
 
-    count = (rows + 2) * cols
-    spread(0, x_ref, xs, x_side)
-    pre = correlate(xs, x_side, one_ref, cols, 1, rows + 2)
-    spread(1, g_ref, gs, g_side)
-    grad_active = correlate(gs, g_side, two_flip_ref, cols, 1, rows + 2)
-
-    ha_last = lax.axis_size("ha") - 1
-    wa_last = lax.axis_size("wa") - 1
-    position = lax.broadcasted_iota(jnp.int32, (side_rows, 256), 0)
-    line = lax.rem(position, lines)
-    dead = ((line < 2) & (ha == 0)) | ((line >= rows + 2) & (ha == ha_last))
-    dead = dead | ((position < lines) & (wa == 0)) | ((position >= lines) & (wa == wa_last))
+    return spread, gather_lines, put_wide, split_lanes
+
+
+def main_kernel(
+    rows,
+    cols,
+    x_ref,
+    g_ref,
+    ra_ref,
+    rb_ref,
+    wa_ref,
+    wb_ref,
+    corner_a_ref,
+    corner_b_ref,
+    select_ref,
+    one_ref,
+    two_flip_ref,
+    grad_pre_ref,
+    *rest,
+):
+    f32, bf16 = jnp.float32, jnp.bfloat16
+    kg_refs, scratch = rest[:-13], rest[-13:]
+    xs, gs, sums, acc_one, acc_two, turned_refs = *scratch[:5], scratch[5:7]
+    swap = scratch[7]
+    spread, _, _, _ = field_tools(
+        rows,
+        cols,
+        ra_ref,
+        rb_ref,
+        wa_ref,
+        wb_ref,
+        corner_a_ref,
+        corner_b_ref,
+        select_ref,
+        (scratch[8:10], scratch[10:12], scratch[12]),
+    )
+    lines = rows + 4
+    ha_odd = lax.rem(lax.axis_index("ha"), 2)
+    nothing = lax.shift_right_logical(lax.axis_index("wa"), 16)
+
+    spread(0, x_ref, xs, None, [(1, lines - 1)])
+    pre = correlate(xs, None, one_ref, cols, [(2, rows)])
+    spread(1, g_ref, gs, None, [(1, lines - 1)])
+    grad_active = correlate(gs, None, two_flip_ref, cols, [(2, rows)])
 
     active_t, slopes = [], []
     for group in range(2):
         value = pre[group]
         cdf = 0.5 * (1.0 + lax.erf(value * root_half))
         slopes.append(cdf + value * inv_root_two_pi * jnp.exp(-0.5 * value * value))
-        active = (value * cdf)[cols : cols + rows * cols]
-        active_t.append(transposed(active, turned_refs[group]))
+        active_t.append(transposed(value * cdf, turned_refs[group]))
 
     half, lead = CH // 2, 8
     low_half = lax.broadcasted_iota(jnp.int32, (CH, 2 * CH), 1) < CH
     low = low_half[:half]
-
-    def kernel_grad(k, fixed, src, acc_ref):
-        for a in range(3):
-            add_taps(k, a, kernel_grad_parts(fixed, src, acc_ref.at[a], a))
 
     def kernel_grad_parts(fixed, src, acc_ref, a):
         parts = [[None] * 4 for _ in range(3)]
@@ -444,40 +443,75 @@
                         put(next_window, c + 1, tile if whole else jnp.where(low_half, 0.0, tile))
         return parts
 
-    def add_taps(k, a, parts):
+    def put_tile(k, tap, left, right):
+        sums[k, lead + half * tap : lead + half * tap + half, :] = jnp.where(low, left, right)
+
+    def add_taps(a, parts):
         for b in range(3):
             for c in range(3):
                 left, right = parts[b][c], parts[b][c + 1]
-                tile = jnp.where(
-                    low,
+                put_tile(
+                    1,
+                    9 * a + 3 * b + c,
                     left[:half] + pltpu.roll(right[:half], CH, 1),
                     pltpu.roll(left[half:], CH, 1) + right[half:],
                 )
-                tap = 9 * a + 3 * b + c
-                sums[k, lead + half * tap : lead + half * tap + half, :] = tile
-
-    kernel_grad(1, active_t, gs, acc_two)
-
-    edges = edges_ref.at[2]
+
+    def first_grad(fixed, src, a):
+        parts = [[None] * 4 for _ in range(3)]
+
+        def put(window, e, tile):
+            old = parts[window][e + 1]
+            parts[window][e + 1] = tile if old is None else old + tile
+
+        for group in range(2):
+            top = (a + 1) * cols
+            acc_ref = acc_one.at[2 * a + group]
+            acc_ref[...] = jnp.dot(
+                fixed[group], src[group, top : top + rows * cols, :], preferred_element_type=f32
+            )
+            for j in range(4):
+                for t in range(8):
+                    (window, i), (next_window, next_i) = divmod(2 * t, 5), divmod(2 * t + 1, 5)
+                    e = i - j + 1 - group
+                    c = next_i - j + 1 - group
+                    joined = next_window in (window, 3)
+                    use_left = -1 <= e < 3 if joined else 0 <= e < 3
+                    use_right = not joined and 0 <= c < 3
+                    if not (use_left or use_right):
+                        continue
+                    tile = acc_ref[64 * j : 64 * j + 64, 128 * t : 128 * t + 128]
+                    if use_left:
+                        whole = joined or e == 2
+                        put(window, e, tile if whole else jnp.where(low_half, tile, 0.0))
+                    if use_right:
+                        whole = c == 0
+                        put(next_window, c - 1, tile if whole else jnp.where(low_half, 0.0, tile))
+
+        def joined_halves(b, c, d):
+            first = parts[b][c + 1] + pltpu.roll(parts[b][c], CH, 1)
+            second = pltpu.roll(parts[b][d + 1], CH, 1) + parts[b][d]
+            return jnp.where(low_half, first, second)
+
+        for b in range(3):
+            for k, (c, d) in enumerate(((0, 1), (2, 2))):
+                slot = swap.at[2 * (3 * a + b) + k]
+                slot[:, :CH] = jnp.transpose(joined_halves(b, c, d))
+                for tap, at in ((c, 0), (d, CH))[: 1 + (c != d)]:
+                    even = slot[pl.ds(at, half, stride=2), :]
+                    odd = slot[pl.ds(at + 1, half, stride=2), :]
+                    put_tile(0, 9 * a + 3 * b + tap, even, pltpu.roll(odd, CH, 1))
+
+    for a in range(2):
+        add_taps(a, kernel_grad_parts(active_t, gs, acc_two.at[a], a))
+    grad_pre_t = []
     for group in range(2):
-        lane = slice(256 * group, 256 * group + 256)
         grad_pre = grad_active[group] * slopes[group]
-        for l in range(1, rows + 3):
-            start = base + PAD + l * stride
-            own = grad_pre[(l - 1) * cols : l * cols]
-            if l == 1:
-                own = jnp.where(ha == 0, 0.0, own)
-            if l == rows + 2:
-                own = jnp.where(ha == ha_last, 0.0, own)
-            put_wide(wide_refs[2], start, cols, [own[:, :128], own[:, 128:]], 2 * group)
-        edges[:side_rows, lane] = jnp.where(dead, 0.0, grad_pre[count:])
-    for l in range(1, rows + 3):
-        left, right = base + l * stride + PAD - 1, base + (l + 1) * stride
-        put_wide(wide_refs[2], left, 1, split_lanes(edges[l : l + 1, :]))
-        put_wide(wide_refs[2], right, 1, split_lanes(edges[lines + l : lines + l + 1, :]))
-    gather_lines(2, 1, rows + 3, ps)
-
-    kernel_grad(0, x_t_ref, ps, acc_one)
+        grad_pre_ref[:, 256 * group : 256 * group + 256] = grad_pre.astype(bf16)
+        grad_pre_t.append(jnp.transpose(grad_pre).astype(bf16))
+    for a in range(3):
+        first_grad(grad_pre_t, xs, a)
+    add_taps(2, kernel_grad_parts(active_t, gs, acc_two.at[2], 2))
 
     if len(kg_refs) == 1:
         for k in range(2):
@@ -503,10 +537,86 @@
             send_ref[z, w] = jnp.where(ha_odd == 0, odd, even).astype(bf16)
 
 
-def main(x, g, ra, rb, wa, wb, corner_a, corner_b, one, two_flip, select, x_t, split):
-    rows, cols, lanes = x.shape
-    stride = cols + PAD
-    span = (rows + 4) * stride + PAD
+def ring_kernel(
+    rows,
+    cols,
+    x_ref,
+    g_ref,
+    ra_ref,
+    rb_ref,
+    wa_ref,
+    wb_ref,
+    corner_a_ref,
+    corner_b_ref,
+    select_ref,
+    one_ref,
+    two_flip_ref,
+    grad_pre_ref,
+    ps,
+    *scratch,
+):
+    f32 = jnp.float32
+    xs, gs, x_side, g_side = scratch[:4]
+    wide_refs, edges_ref = scratch[4:7], scratch[10]
+    spread, gather_lines, put_wide, split_lanes = field_tools(
+        rows,
+        cols,
+        ra_ref,
+        rb_ref,
+        wa_ref,
+        wb_ref,
+        corner_a_ref,
+        corner_b_ref,
+        select_ref,
+        (wide_refs, scratch[7:10], edges_ref),
+    )
+    lines, stride, base = rows + 4, cols + PAD, 8
+    side_rows = 2 * lines
+    ha, wa = lax.axis_index("ha"), lax.axis_index("wa")
+    ha_last = lax.axis_size("ha") - 1
+    wa_last = lax.axis_size("wa") - 1
+    runs = [(1, 1), (rows + 2, 1)]
+    gathered = [(0, 3), (lines - 3, lines)]
+    spread(0, x_ref, xs, x_side, gathered)
+    pre = correlate(xs, x_side, one_ref, cols, runs)
+    spread(1, g_ref, gs, g_side, gathered)
+    grad_active = correlate(gs, g_side, two_flip_ref, cols, runs)
+    position = lax.broadcasted_iota(jnp.int32, (side_rows, 256), 0)
+    line = lax.rem(position, lines)
+    dead = ((line < 2) & (ha == 0)) | ((line >= rows + 2) & (ha == ha_last))
+    dead = dead | ((position < lines) & (wa == 0)) | ((position >= lines) & (wa == wa_last))
+    wide, edges = wide_refs[2], edges_ref.at[2]
+    for r in range(rows):
+        own = grad_pre_ref[r * cols : r * cols + cols, :].astype(f32)
+        put_wide(wide, base + PAD + (r + 2) * stride, cols, split_lanes(own))
+    for group in range(2):
+        value = pre[group]
+        cdf = 0.5 * (1.0 + lax.erf(value * root_half))
+        slope = cdf + value * inv_root_two_pi * jnp.exp(-0.5 * value * value)
+        grad_pre = grad_active[group] * slope
+        above = jnp.where(ha == 0, 0.0, grad_pre[:cols])
+        below = jnp.where(ha == ha_last, 0.0, grad_pre[cols : 2 * cols])
+        for l, part in ((1, above), (rows + 2, below)):
+            start = base + PAD + l * stride
+            put_wide(wide, start, cols, [part[:, :128], part[:, 128:]], 2 * group)
+        edges[:side_rows, 256 * group : 256 * group + 256] = jnp.where(
+            dead, 0.0, grad_pre[2 * cols :]
+        )
+    for l in range(1, rows + 3):
+        left, right = base + l * stride + PAD - 1, base + (l + 1) * stride
+        put_wide(wide, left, 1, split_lanes(edges[l : l + 1, :]))
+        put_wide(wide, right, 1, split_lanes(edges[lines + l : lines + l + 1, :]))
+    gather_lines(2, 1, rows + 3, ps)
+
+
+def scratch_shapes(rows, cols, lanes, fields):
+    span = (rows + 4) * (cols + PAD) + PAD
+    wide = pltpu.VMEM((lanes // 128, span + 16, 128), jnp.float32)
+    return [*[wide] * (2 * fields), pltpu.VMEM((fields, 6 * (rows + 4), lanes), jnp.float32)]
+
+
+def main(fields, bands, split):
+    rows, cols, lanes = fields[0].shape
     if split:
         slabs, width = split
         take = 27 * CH // 2 // (2 * slabs * width)
@@ -518,37 +628,53 @@
     else:
         grads = (jax.ShapeDtypeStruct((2, 27 * CH // 2, 2 * CH), jnp.float32),)
     vmem = pl.BlockSpec(memory_space=pltpu.VMEM)
-    lines = rows + 4
-    moving = (2, lines * cols, 1024)
-    side = pltpu.VMEM((2, 3, 2 * lines, 1024), jnp.bfloat16)
-    wide = pltpu.VMEM((lanes // 128, span + 16, 128), jnp.float32)
+    moving = pltpu.VMEM((2, (rows + 4) * cols, 1024), jnp.bfloat16)
     turning = pltpu.VMEM((rows * cols // 128, 256, 128), jnp.float32)
     return pl.pallas_call(
         functools.partial(main_kernel, rows, cols),
-        out_shape=(
-            jax.ShapeDtypeStruct(moving, jnp.bfloat16),
-            *grads,
-        ),
-        in_specs=[vmem] * 12,
+        out_shape=(jax.ShapeDtypeStruct((rows * cols, lanes), jnp.bfloat16), *grads),
+        in_specs=[vmem] * 11,
         out_specs=(vmem,) * (1 + len(grads)),
         scratch_shapes=[
-            pltpu.VMEM(moving, jnp.bfloat16),
-            pltpu.VMEM(moving, jnp.bfloat16),
-            side,
-            side,
+            moving,
+            moving,
             pltpu.VMEM((2, 27 * CH // 2 + 40, 2 * CH), jnp.float32),
-            pltpu.VMEM((3, 256, 1024), jnp.float32),
+            pltpu.VMEM((6, 256, 1024), jnp.float32),
             pltpu.VMEM((3, 256, 1024), jnp.float32),
             turning,
             turning,
-            *[wide] * 6,
-            pltpu.VMEM((3, 6 * lines, lanes), jnp.float32),
+            pltpu.VMEM((18, 2 * CH, 2 * CH), jnp.float32),
+            *scratch_shapes(rows, cols, lanes, 2),
         ],
         compiler_params=pltpu.CompilerParams(vmem_limit_bytes=32 << 20),
         cost_estimate=pl.CostEstimate(
-            flops=14_000_000_000, bytes_accessed=8_000_000, transcendentals=1_000_000
+            flops=10_000_000_000, bytes_accessed=8_000_000, transcendentals=1_000_000
         ),
-    )(x, g, ra, rb, wa, wb, corner_a, corner_b, one, two_flip, select, x_t)
+    )(*fields, *bands)
+
+
+def ring(fields, bands, grad_pre):
+    rows, cols, lanes = fields[0].shape
+    vmem = pl.BlockSpec(memory_space=pltpu.VMEM)
+    moving = ((2, (rows + 4) * cols, 1024), jnp.bfloat16)
+    side = pltpu.VMEM((2, 3, 2 * (rows + 4), 1024), jnp.bfloat16)
+    return pl.pallas_call(
+        functools.partial(ring_kernel, rows, cols),
+        out_shape=jax.ShapeDtypeStruct(*moving),
+        in_specs=[vmem] * 12,
+        out_specs=vmem,
+        scratch_shapes=[
+            pltpu.VMEM(*moving),
+            pltpu.VMEM(*moving),
+            side,
+            side,
+            *scratch_shapes(rows, cols, lanes, 3),
+        ],
+        compiler_params=pltpu.CompilerParams(vmem_limit_bytes=20 << 20),
+        cost_estimate=pl.CostEstimate(
+            flops=3_000_000_000, bytes_accessed=8_000_000, transcendentals=500_000
+        ),
+    )(*fields, *bands, grad_pre)
 
 
 def input_grad(ps, band, shape):
@@ -624,6 +750,7 @@
 
 
 def shards(inputs, grad_out, kernel_one, kernel_two):
+    rows, _, _ = inputs.shape
     height_count = lax.axis_size("ha")
     width_count = lax.axis_size("wa")
     devices = height_count * width_count
@@ -634,7 +761,7 @@
     wa = pair_exchange(own_a, "wa", 0)
     ra = pair_exchange(to_a, "ha", 0)
     rb = pair_exchange(to_b, "ha", 1)
-    one, two_flip, one_flip, select, x_t = prepare(x, kernel_one, kernel_two)
+    one, two_flip, one_flip, select = prepare(rows + 4, kernel_one, kernel_two)
     corner_to_a, corner_to_b = corners(wa, wb)
     corner_b = pair_exchange(corner_to_b, "ha", 1)
     corner_a = pair_exchange(corner_to_a, "ha", 0)
@@ -647,7 +774,10 @@
         and height_count > 1
     ):
         split = (height_count // 2, width_count)
-    ps, *grads = main(x, g, ra, rb, wa, wb, corner_a, corner_b, one, two_flip, select, x_t, split)
+    fields = (x, g, ra, rb, wa, wb, corner_a, corner_b)
+    bands = (select, one, two_flip)
+    grad_pre, *grads = main(fields, bands, split)
+    ps = ring(fields, bands, grad_pre)
     grad_inputs = input_grad(ps, one_flip, inputs.shape)
     if split:
         grads = reduce_chunks(*grads, 27 * CH // 2 // devices)

time: 44.3 us -> 43.2 us (0.975)
  waiting for transfers between devices: 9.77 us -> 7.31 us
  Pallas kernels: 10.7 us -> 12 us
    ppermute x7, waiting for transfers between devices: 8.7 us -> 6.23 us  [xor_exchange(): return lax.ppermute(block, axis, [(i, i ^ mask) for i in range(count)])]
    pallas_call x1 -> x2, Pallas kernels: 0.94 us -> 3.31 us  [the longest x1 2.44 us: ring(): pl.pallas_call(functools.partial(ring_kernel, rows, cols), out_shape=jax....]
    pallas_call x1, Pallas kernels: 6.05 us -> 4.98 us  [main(): pl.pallas_call(functools.partial(main_kernel, rows, cols), out_shape=(jax...]
  transfers between devices with their start and end apart: 13 -> 13, of which waited for: 6 -> 5; matrix products, arithmetic and copies ran while one was open for 0% -> 0% of each run, Pallas kernels for 6% -> 12%
where the time goes in v5:
time: 43.2 us; the launch traced here: 43 us
  starting transfers between devices  23 us (53%)
  Pallas kernels  12 us (28%)
  waiting for transfers between devices  7.31 us (17%)
  between operations  0.75 us (2%)
    ppermute x7, starting transfers between devices, xor_exchange(): return lax.ppermute(block, axis, [(i, i ^ mask) for i in range(count)])  15.5 us
    ppermute x6, starting transfers between devices, pair_exchange(): return lax.ppermute(block, axis, pairs)  7.45 us
    ppermute x7, waiting for transfers between devices, xor_exchange(): return lax.ppermute(block, axis, [(i, i ^ mask) for i in range(count)])  6.23 us
    pallas_call x1, Pallas kernels, main(): pl.pallas_call(functools.partial(main_kernel, rows, cols), out_shape=(jax...  4.98 us
    pallas_call x1, Pallas kernels, ring(): pl.pallas_call(functools.partial(ring_kernel, rows, cols), out_shape=jax....  2.44 us
    pallas_call x1, Pallas kernels, input_grad(): pl.pallas_call(functools.partial(input_grad_kernel, rows, cols), out_shap...  1.68 us
    pallas_call x1, Pallas kernels, pack(): pl.pallas_call(pack_kernel, out_shape=tuple((jax.ShapeDtypeStruct(shape,...  1.34 us
    ppermute x6, waiting for transfers between devices, pair_exchange(): return lax.ppermute(block, axis, pairs)  1.07 us
  transfers between devices with their start and end apart: 13, of which 5 were waited for; matrix products, arithmetic and copies ran while one was open for 0% of the time, Pallas kernels for 12%

profile of v5, /device:TPU:0, one launch (start us, length us, event | category | flops | bytes accessed | tf_op | source)
XLA Modules:
  0.0 43.0 jit_solution(5910965803774249072)
XLA Ops:
  0.6 1.3 %shard_map.67 = (bf16[4,64,512]{2,1,0:T(8,128)(2,1)S(1)}, bf16[4,64,512]{2,1,0:T(8,128)(2,1)S(1)}, bf16[27,64,64]{2,1,0:T(8,128)(2,1)S(1)}, bf16[27,64,64]{2,1,0...) custom-call(bf16[4,64,512]{2,1,0:T(8,128)(2,1)} %x_hbm.1, ...), custom_call_target="tpu_custom_call" | custom-call | bytes 1100000 | tf_op jit(solution)/shard_map/pallas_call | solution.py:63
  2.0 0.6 %collective-permute-start = (bf16[2,2,64,512]{3,2,1,0:T(8,128)(2,1)S(1)}, bf16[2,2,64,512]{3,2,1,0:T(8,128)(2,1)S(1)}, u32[]{:S(2)}, u32[]{:S(2)}) collective-permute-start(bf16[2,2,64,512]{3,2,1,0:T(8,128)(2,1)S(1)} %get-tuple-element.32), channel_id=1, source_target_pairs={{0,4},{4,0},{8,12},{12,8},{16,20},{20,16},{24,28},{28,24},{1,5},{5... | collective-permute-start | bytes 786440 | tf_op jit(solution)/shard_map/ppermute | solution.py:23
  2.5 0.7 %collective-permute-start.1 = (bf16[2,2,64,512]{3,2,1,0:T(8,128)(2,1)S(1)}, bf16[2,2,64,512]{3,2,1,0:T(8,128)(2,1)S(1)}, u32[]{:S(2)}, u32[]{:S(2)}) collective-permute-start(bf16[2,2,64,512]{3,2,1,0:T(8,128)(2,1)S(1)} %get-tuple-element.33), channel_id=1, source_target_pairs={{4,8},{8,4},{12,16},{16,12},{20,24},{24,20},{5,9},{9,5},{13,17},{1... | collective-permute-start | bytes 786440 | tf_op jit(solution)/shard_map/ppermute | solution.py:23
  3.2 2.6 %collective-permute-start.2 = (bf16[2,4,2,512]{3,2,1,0:T(2,128)(2,1)S(1)}, bf16[2,4,2,512]{3,2,1,0:T(2,128)(2,1)S(1)}, u32[]{:S(2)}, u32[]{:S(2)}) collective-permute-start(bf16[2,4,2,512]{3,2,1,0:T(2,128)(2,1)S(1)} %get-tuple-element.34), channel_id=1, source_target_pairs={{0,1},{1,0},{2,3},{3,2},{4,5},{5,4},{6,7},{7,6},{8,9},{9,8},{10,11... | collective-permute-start | bytes 49160 | tf_op jit(solution)/shard_map/ppermute | solution.py:23
  5.8 0.7 %collective-permute-start.3 = (bf16[2,4,2,512]{3,2,1,0:T(2,128)(2,1)S(1)}, bf16[2,4,2,512]{3,2,1,0:T(2,128)(2,1)S(1)}, u32[]{:S(2)}, u32[]{:S(2)}) collective-permute-start(bf16[2,4,2,512]{3,2,1,0:T(2,128)(2,1)S(1)} %get-tuple-element.35), channel_id=1, source_target_pairs={{1,2},{2,1},{5,6},{6,5},{9,10},{10,9},{13,14},{14,13},{17,18},{18,... | collective-permute-start | bytes 49160 | tf_op jit(solution)/shard_map/ppermute | solution.py:23
  6.4 1.1 %collective-permute-done.2.wa_ref = bf16[2,4,2,512]{3,2,1,0:T(2,128)(2,1)S(1)} collective-permute-done((bf16[2,4,2,512]{3,2,1,0:T(2,128)(2,1)S(1)}, bf16[2,4,2,512]{3,2,1,0:T(2,128)(2,1)S(1)}, u32[]{:S(2)}, u32[]{:S(2)}) %collective-permute-start.2) | collective-permute-done | bytes 16416 | tf_op jit(solution)/shard_map/ppermute | solution.py:23
  7.5 0.0 collective-permute-done.3.wb_ref
  7.5 2.4 %collective-permute-start.4 = (bf16[2,2,2,2,512]{4,3,2,1,0:T(2,128)(2,1)S(1)}, bf16[2,2,2,2,512]{4,3,2,1,0:T(2,128)(2,1)S(1)}, u32[]{:S(2)}, u32[]{:S(2)}) collective-permute-start(bf16[2,2,2,2,512]{4,3,2,1,0:T(2,128)(2,1)S(1)} %get-tuple-element.36), channel_id=1, source_target_pairs={{0,4},{4,0},{8,12},{12,8},{16,20},{20,16},{24,28},{28,24},{1,5},{5... | collective-permute-start | bytes 49160 | tf_op jit(solution)/shard_map/ppermute | solution.py:23
  9.9 0.7 %collective-permute-start.5 = (bf16[2,2,2,2,512]{4,3,2,1,0:T(2,128)(2,1)S(1)}, bf16[2,2,2,2,512]{4,3,2,1,0:T(2,128)(2,1)S(1)}, u32[]{:S(2)}, u32[]{:S(2)}) collective-permute-start(bf16[2,2,2,2,512]{4,3,2,1,0:T(2,128)(2,1)S(1)} %get-tuple-element.37), channel_id=1, source_target_pairs={{4,8},{8,4},{12,16},{16,12},{20,24},{24,20},{5,9},{9,5},{13,17},{1... | collective-permute-start | bytes 49160 | tf_op jit(solution)/shard_map/ppermute | solution.py:23
  10.5 0.9 %shard_map.69 = (bf16[9,4,64,128]{3,2,1,0:T(8,128)(2,1)S(1)}, bf16[9,4,64,128]{3,2,1,0:T(8,128)(2,1)S(1)}, bf16[9,4,64,128]{3,2,1,0:T(8,128)(2,1)S(1)}, bf16[288,48]{1,0:T(8,128)(2,1)S(1)}) custom-call(bf16[27,64,64]{2,1,0:T(8,128)(2,1)S(1)} %get-tuple-element.38.one_ref, bf16[27,64,64]{2,1,0:T(8,128)(2,1)S(1)} %get-tuple-element.39.two_ref), custom_call_target="tpu_custom_call" | custom-call | flops 4000000 | bytes 4000000 | tf_op jit(solution)/shard_map/pallas_call | solution.py:177
  11.4 0.0 collective-permute-done.4.corner_a_ref
  11.4 0.0 collective-permute-done.5.corner_b_ref
  11.4 0.0 collective-permute-done.ra_ref
  11.4 0.0 collective-permute-done.1.rb_ref
  11.4 5.0 %shard_map.70 = (bf16[256,512]{1,0:T(8,128)(2,1)S(1)}, f32[4,4,56,128]{3,2,1,0:T(8,128)S(1)}, bf16[4,4,56,128]{3,2,1,0:T(8,128)(2,1)S(1)}) custom-call(bf16[4,64,512]{2,1,0:T(8,128)(2,1)S(1)} %get-tuple-element.30.x_ref, bf16[4,64,512]{2,1,0:T(8,128)(2,1)S(1)} %get-tuple-element.31.g_ref, bf16[2,2,64,512]{3,2,1,0:T(8,128)(2,1)S(1)} %collective-permute-done.ra_ref, ...), custom_call_target="tpu_custom_call" | custom-call | flops 10000000000 | bytes 8000000 | tf_op jit(solution)/shard_map/pallas_call | solution.py:633
  16.4 3.8 %collective-permute-start.6 = (bf16[4,4,56,128]{3,2,1,0:T(8,128)(2,1)S(1)}, bf16[4,4,56,128]{3,2,1,0:T(8,128)(2,1)S(1)}, u32[]{:S(2)}, u32[]{:S(2)}) collective-permute-start(bf16[4,4,56,128]{3,2,1,0:T(8,128)(2,1)S(1)} %get-tuple-element.46), channel_id=1, source_target_pairs={{0,4},{4,0},{8,12},{12,8},{16,20},{20,16},{24,28},{28,24},{1,5},{5... | collective-permute-start | bytes 688136 | tf_op jit(solution)/shard_map/ppermute | solution.py:697
  20.2 1.1 %collective-permute-done.6.got_ref = bf16[4,4,56,128]{3,2,1,0:T(8,128)(2,1)S(1)} collective-permute-done((bf16[4,4,56,128]{3,2,1,0:T(8,128)(2,1)S(1)}, bf16[4,4,56,128]{3,2,1,0:T(8,128)(2,1)S(1)}, u32[]{:S(2)}, u32[]{:S(2)}) %collective-permute-start.6) | collective-permute-done | bytes 229408 | tf_op jit(solution)/shard_map/ppermute | solution.py:697
  21.3 0.1 shard_map.73
  21.4 4.3 %collective-permute-start.7 = (bf16[4,56,128]{2,1,0:T(8,128)(2,1)S(1)}, bf16[4,56,128]{2,1,0:T(8,128)(2,1)S(1)}, u32[]{:S(2)}, u32[]{:S(2)}) collective-permute-start(bf16[4,56,128]{2,1,0:T(8,128)(2,1)S(1)} %get-tuple-element.48), channel_id=1, source_target_pairs={{0,1},{1,0},{2,3},{3,2},{4,5},{5,4},{6,7},{7,6},{8,9},{9,8},{10,11... | collective-permute-start | bytes 172040 | tf_op jit(solution)/shard_map/ppermute | solution.py:697
  25.7 1.4 %collective-permute-start.8 = (bf16[4,56,128]{2,1,0:T(8,128)(2,1)S(1)}, bf16[4,56,128]{2,1,0:T(8,128)(2,1)S(1)}, u32[]{:S(2)}, u32[]{:S(2)}) collective-permute-start(bf16[4,56,128]{2,1,0:T(8,128)(2,1)S(1)} %get-tuple-element.49), channel_id=1, source_target_pairs={{0,2},{1,3},{2,0},{3,1},{4,6},{5,7},{6,4},{7,5},{8,10},{9,11},{10,... | collective-permute-start | bytes 172040 | tf_op jit(solution)/shard_map/ppermute | solution.py:697
  27.1 1.4 %collective-permute-start.9 = (bf16[4,56,128]{2,1,0:T(8,128)(2,1)S(1)}, bf16[4,56,128]{2,1,0:T(8,128)(2,1)S(1)}, u32[]{:S(2)}, u32[]{:S(2)}) collective-permute-start(bf16[4,56,128]{2,1,0:T(8,128)(2,1)S(1)} %get-tuple-element.50), channel_id=1, source_target_pairs={{0,3},{1,2},{2,1},{3,0},{4,7},{5,6},{6,5},{7,4},{8,11},{9,10},{10,... | collective-permute-start | bytes 172040 | tf_op jit(solution)/shard_map/ppermute | solution.py:697
  28.5 2.4 %shard_map.71.ps = bf16[2,512,1024]{2,1,0:T(8,128)(2,1)S(1)} custom-call(bf16[4,64,512]{2,1,0:T(8,128)(2,1)S(1)} %get-tuple-element.30.x_ref, bf16[4,64,512]{2,1,0:T(8,128)(2,1)S(1)} %get-tuple-element.31.g_ref, bf16[2,2,64,512]{3,2,1,0:T(8,128)(2,1)S(1)} %collective-permute-done.ra_ref, bf16[2,2,64,512]{3,2,1,0:T(8,128)(2,1)S(1)} %collective-permute-done.1.rb_ref, ...), custom_call_target="tpu_custom_call" | custom-call | flops 3000000000 | bytes 8000000 | tf_op jit(solution)/shard_map/pallas_call | solution.py:661
  30.9 0.0 collective-permute-done.7.refs_1_
  30.9 0.0 collective-permute-done.8.refs_2_
  30.9 1.2 %collective-permute-done.9.refs_3_ = bf16[4,56,128]{2,1,0:T(8,128)(2,1)S(1)} collective-permute-done((bf16[4,56,128]{2,1,0:T(8,128)(2,1)S(1)}, bf16[4,56,128]{2,1,0:T(8,128)(2,1)S(1)}, u32[]{:S(2)}, u32[]{:S(2)}) %collective-permute-start.9) | collective-permute-done | bytes 57376 | tf_op jit(solution)/shard_map/ppermute | solution.py:697
  32.2 2.2 %collective-permute-start.10 = (f32[56,128]{1,0:T(8,128)S(1)}, f32[56,128]{1,0:T(8,128)S(1)}, u32[]{:S(2)}, u32[]{:S(2)}) collective-permute-start(f32[56,128]{1,0:T(8,128)S(1)} %get-tuple-element.52), channel_id=1, source_target_pairs={{0,8},{4,12},{8,0},{12,4},{16,24},{20,28},{24,16},{28,20},{1,9},{5... | collective-permute-start | bytes 86024 | tf_op jit(solution)/shard_map/ppermute | solution.py:697
  34.4 2.4 %collective-permute-start.11 = (f32[56,128]{1,0:T(8,128)S(1)}, f32[56,128]{1,0:T(8,128)S(1)}, u32[]{:S(2)}, u32[]{:S(2)}) collective-permute-start(f32[56,128]{1,0:T(8,128)S(1)} %get-tuple-element.53), channel_id=1, source_target_pairs={{0,16},{4,20},{8,24},{12,28},{16,0},{20,4},{24,8},{28,12},{1,17},{... | collective-permute-start | bytes 86024 | tf_op jit(solution)/shard_map/ppermute | solution.py:697
  36.8 0.1 collective-permute-start.12
  36.8 1.7 %shard_map.72 = bf16[4,64,512]{2,1,0:T(8,128)(2,1)} custom-call(bf16[2,512,1024]{2,1,0:T(8,128)(2,1)S(1)} %shard_map.71.ps, bf16[9,4,64,128]{3,2,1,0:T(8,128)(2,1)S(1)} %get-tuple-element.44.band_ref), custom_call_target="tpu_custom_call" | custom-call | flops 2000000000 | bytes 4000000 | tf_op jit(solution)/shard_map/pallas_call | solution.py:683
  38.5 0.0 collective-permute-done.10.refs_1_
  38.5 0.8 %collective-permute-done.11.refs_2_ = f32[56,128]{1,0:T(8,128)S(1)} collective-permute-done((f32[56,128]{1,0:T(8,128)S(1)}, f32[56,128]{1,0:T(8,128)S(1)}, u32[]{:S(2)}, u32[]{:S(2)}) %collective-permute-start.11) | collective-permute-done | bytes 28704 | tf_op jit(solution)/shard_map/ppermute | solution.py:697
  39.3 3.1 %collective-permute-done.12.refs_3_ = f32[56,128]{1,0:T(8,128)S(1)} collective-permute-done((f32[56,128]{1,0:T(8,128)S(1)}, f32[56,128]{1,0:T(8,128)S(1)}, u32[]{:S(2)}, u32[]{:S(2)}) %collective-permute-start.12) | collective-permute-done | bytes 28704 | tf_op jit(solution)/shard_map/ppermute | solution.py:697
  42.4 0.6 %shard_map.75 = (f32[27,128]{1,0:T(8,128)}, f32[27,128]{1,0:T(8,128)}) custom-call(f32[56,128]{1,0:T(8,128)S(1)} %get-tuple-element.51.refs_0_, f32[56,128]{1,0:T(8,128)S(1)} %collective-permute-done.10.refs_1_, f32[56,128]{1,0:T(8,128)S(1)} %collective-permute-done.11.refs_2_, f32[56,128]{1,0:T(8,128)S(1)} %collective-permute-done.12.refs_3_), custom_call_target="tpu_custom_call" | custom-call | bytes 300000 | tf_op jit(solution)/shard_map/pallas_call | solution.py:88
  (2 shorter events, 0.0 us)
Async XLA Ops:
  2.0 9.4 %collective-permute-start = (bf16[2,2,64,512]{3,2,1,0:T(8,128)(2,1)S(1)}, bf16[2,2,64,512]{3,2,1,0:T(8,128)(2,1)S(1)}, u32[]{:S(2)}, u32[]{:S(2)}) collective-permute-start(bf16[2,2,64,512]{3,2,1,0:T(8,128)(2,1)S(1)} %get-tuple-element.32), channel_id=1, source_target_pairs={{0,4},{4,0},{8,12},{12,8},{16,20},{20,16},{24,28},{28,24},{1,5},{5... | collective-permute-start | bytes 786440 | tf_op jit(solution)/shard_map/ppermute | solution.py:23
  2.5 8.9 %collective-permute-start.1 = (bf16[2,2,64,512]{3,2,1,0:T(8,128)(2,1)S(1)}, bf16[2,2,64,512]{3,2,1,0:T(8,128)(2,1)S(1)}, u32[]{:S(2)}, u32[]{:S(2)}) collective-permute-start(bf16[2,2,64,512]{3,2,1,0:T(8,128)(2,1)S(1)} %get-tuple-element.33), channel_id=1, source_target_pairs={{4,8},{8,4},{12,16},{16,12},{20,24},{24,20},{5,9},{9,5},{13,17},{1... | collective-permute-start | bytes 786440 | tf_op jit(solution)/shard_map/ppermute | solution.py:23
  3.2 4.3 %collective-permute-start.2 = (bf16[2,4,2,512]{3,2,1,0:T(2,128)(2,1)S(1)}, bf16[2,4,2,512]{3,2,1,0:T(2,128)(2,1)S(1)}, u32[]{:S(2)}, u32[]{:S(2)}) collective-permute-start(bf16[2,4,2,512]{3,2,1,0:T(2,128)(2,1)S(1)} %get-tuple-element.34), channel_id=1, source_target_pairs={{0,1},{1,0},{2,3},{3,2},{4,5},{5,4},{6,7},{7,6},{8,9},{9,8},{10,11... | collective-permute-start | bytes 49160 | tf_op jit(solution)/shard_map/ppermute | solution.py:23
  5.8 1.7 %collective-permute-start.3 = (bf16[2,4,2,512]{3,2,1,0:T(2,128)(2,1)S(1)}, bf16[2,4,2,512]{3,2,1,0:T(2,128)(2,1)S(1)}, u32[]{:S(2)}, u32[]{:S(2)}) collective-permute-start(bf16[2,4,2,512]{3,2,1,0:T(2,128)(2,1)S(1)} %get-tuple-element.35), channel_id=1, source_target_pairs={{1,2},{2,1},{5,6},{6,5},{9,10},{10,9},{13,14},{14,13},{17,18},{18,... | collective-permute-start | bytes 49160 | tf_op jit(solution)/shard_map/ppermute | solution.py:23
  7.5 3.9 %collective-permute-start.4 = (bf16[2,2,2,2,512]{4,3,2,1,0:T(2,128)(2,1)S(1)}, bf16[2,2,2,2,512]{4,3,2,1,0:T(2,128)(2,1)S(1)}, u32[]{:S(2)}, u32[]{:S(2)}) collective-permute-start(bf16[2,2,2,2,512]{4,3,2,1,0:T(2,128)(2,1)S(1)} %get-tuple-element.36), channel_id=1, source_target_pairs={{0,4},{4,0},{8,12},{12,8},{16,20},{20,16},{24,28},{28,24},{1,5},{5... | collective-permute-start | bytes 49160 | tf_op jit(solution)/shard_map/ppermute | solution.py:23
  9.9 1.5 %collective-permute-start.5 = (bf16[2,2,2,2,512]{4,3,2,1,0:T(2,128)(2,1)S(1)}, bf16[2,2,2,2,512]{4,3,2,1,0:T(2,128)(2,1)S(1)}, u32[]{:S(2)}, u32[]{:S(2)}) collective-permute-start(bf16[2,2,2,2,512]{4,3,2,1,0:T(2,128)(2,1)S(1)} %get-tuple-element.37), channel_id=1, source_target_pairs={{4,8},{8,4},{12,16},{16,12},{20,24},{24,20},{5,9},{9,5},{13,17},{1... | collective-permute-start | bytes 49160 | tf_op jit(solution)/shard_map/ppermute | solution.py:23
  16.4 4.9 %collective-permute-start.6 = (bf16[4,4,56,128]{3,2,1,0:T(8,128)(2,1)S(1)}, bf16[4,4,56,128]{3,2,1,0:T(8,128)(2,1)S(1)}, u32[]{:S(2)}, u32[]{:S(2)}) collective-permute-start(bf16[4,4,56,128]{3,2,1,0:T(8,128)(2,1)S(1)} %get-tuple-element.46), channel_id=1, source_target_pairs={{0,4},{4,0},{8,12},{12,8},{16,20},{20,16},{24,28},{28,24},{1,5},{5... | collective-permute-start | bytes 688136 | tf_op jit(solution)/shard_map/ppermute | solution.py:697
  21.4 9.5 %collective-permute-start.7 = (bf16[4,56,128]{2,1,0:T(8,128)(2,1)S(1)}, bf16[4,56,128]{2,1,0:T(8,128)(2,1)S(1)}, u32[]{:S(2)}, u32[]{:S(2)}) collective-permute-start(bf16[4,56,128]{2,1,0:T(8,128)(2,1)S(1)} %get-tuple-element.48), channel_id=1, source_target_pairs={{0,1},{1,0},{2,3},{3,2},{4,5},{5,4},{6,7},{7,6},{8,9},{9,8},{10,11... | collective-permute-start | bytes 172040 | tf_op jit(solution)/shard_map/ppermute | solution.py:697
  25.7 5.2 %collective-permute-start.8 = (bf16[4,56,128]{2,1,0:T(8,128)(2,1)S(1)}, bf16[4,56,128]{2,1,0:T(8,128)(2,1)S(1)}, u32[]{:S(2)}, u32[]{:S(2)}) collective-permute-start(bf16[4,56,128]{2,1,0:T(8,128)(2,1)S(1)} %get-tuple-element.49), channel_id=1, source_target_pairs={{0,2},{1,3},{2,0},{3,1},{4,6},{5,7},{6,4},{7,5},{8,10},{9,11},{10,... | collective-permute-start | bytes 172040 | tf_op jit(solution)/shard_map/ppermute | solution.py:697
  27.1 5.1 %collective-permute-start.9 = (bf16[4,56,128]{2,1,0:T(8,128)(2,1)S(1)}, bf16[4,56,128]{2,1,0:T(8,128)(2,1)S(1)}, u32[]{:S(2)}, u32[]{:S(2)}) collective-permute-start(bf16[4,56,128]{2,1,0:T(8,128)(2,1)S(1)} %get-tuple-element.50), channel_id=1, source_target_pairs={{0,3},{1,2},{2,1},{3,0},{4,7},{5,6},{6,5},{7,4},{8,11},{9,10},{10,... | collective-permute-start | bytes 172040 | tf_op jit(solution)/shard_map/ppermute | solution.py:697
  32.2 6.3 %collective-permute-start.10 = (f32[56,128]{1,0:T(8,128)S(1)}, f32[56,128]{1,0:T(8,128)S(1)}, u32[]{:S(2)}, u32[]{:S(2)}) collective-permute-start(f32[56,128]{1,0:T(8,128)S(1)} %get-tuple-element.52), channel_id=1, source_target_pairs={{0,8},{4,12},{8,0},{12,4},{16,24},{20,28},{24,16},{28,20},{1,9},{5... | collective-permute-start | bytes 86024 | tf_op jit(solution)/shard_map/ppermute | solution.py:697
  34.4 4.9 %collective-permute-start.11 = (f32[56,128]{1,0:T(8,128)S(1)}, f32[56,128]{1,0:T(8,128)S(1)}, u32[]{:S(2)}, u32[]{:S(2)}) collective-permute-start(f32[56,128]{1,0:T(8,128)S(1)} %get-tuple-element.53), channel_id=1, source_target_pairs={{0,16},{4,20},{8,24},{12,28},{16,0},{20,4},{24,8},{28,12},{1,17},{... | collective-permute-start | bytes 86024 | tf_op jit(solution)/shard_map/ppermute | solution.py:697
  36.8 5.7 %collective-permute-start.12 = (f32[56,128]{1,0:T(8,128)S(1)}, f32[56,128]{1,0:T(8,128)S(1)}, u32[]{:S(2)}, u32[]{:S(2)}) collective-permute-start(f32[56,128]{1,0:T(8,128)S(1)} %get-tuple-element.54), channel_id=1, source_target_pairs={{0,24},{4,28},{8,16},{12,20},{16,8},{20,12},{24,0},{28,4},{1,25},{... | collective-permute-start | bytes 86024 | tf_op jit(solution)/shard_map/ppermute | solution.py:697

commit v6 on v5

--- a/solution.py
+++ b/solution.py
@@ -147,10 +147,53 @@
     return jnp.concatenate(halves, axis=1).astype(jnp.bfloat16)
 
 
+def turn_lanes(parts):
+    swapped = [pltpu.roll(part, CH, 1) for part in parts]
+    low = lax.broadcasted_iota(jnp.int32, parts[0].shape, 1) < CH
+    return [jnp.where(low, swapped[k - 1], swapped[k]) for k in range(len(parts))]
+
+
+def gather_line(wide, wide_turned, slot, own, left, right, out, row):
+    cols, lanes = own.shape
+    tiles = lanes // 128
+    nothing = lax.shift_right_logical(lax.axis_index("wa"), 16)
+    base = slot * (cols + 2 * PAD)
+    pieces = ((PAD - 1, 1, left), (PAD, cols, own), (PAD + cols, 1, right))
+    for at, count, value in pieces:
+        for k in range(tiles):
+            wide[k, base + at : base + at + count, :] = value[:, 128 * k : 128 * k + 128]
+    around = slice(base + PAD - 8, base + PAD + cols + 8)
+    for k, value in enumerate(turn_lanes([wide[k, around, :] for k in range(tiles)])):
+        wide_turned[k, around, :] = value
+    start = base + PAD - 1
+    plain, other = (
+        [
+            [ref[k, pl.ds(at, cols), :] for k in range(tiles)]
+            for at in (start + nothing, start + 1, start + 2 + nothing)
+        ]
+        for ref in (wide, wide_turned)
+    )
+    for group, value in enumerate(gather_depths(plain, other)):
+        out[group, row : row + cols, :] = value
+
+
+def line_scratch(slots, cols, lanes):
+    return [pltpu.VMEM((lanes // 128, slots * (cols + 2 * PAD), 128), jnp.float32)] * 2
+
+
 def prepare_kernel(
-    lines, one_ref, two_ref, one_out, two_flip_out, one_flip_out, select_out
+    lines, x_ref, g_ref, wa_ref, wb_ref, one_ref, two_ref, one_out, two_flip_out, one_flip_out, select_out, xs_out, gs_out, wide, wide_turned
 ):
     select_out[...] = halo_selection(lines, select_out.shape)
+    rows, cols, _ = x_ref.shape
+    wa_even = lax.rem(lax.axis_index("wa"), 2) == 0
+    for which, (ref, out) in enumerate(((x_ref, xs_out), (g_ref, gs_out))):
+        for r in range(rows):
+            near, far = (side[which, r].astype(jnp.float32) for side in (wa_ref, wb_ref))
+            left, right = jnp.where(wa_even, far, near), jnp.where(wa_even, near, far)
+            own = ref[r].astype(jnp.float32)
+            slot = which * rows + r
+            gather_line(wide, wide_turned, slot, own, left[1:2], right[:1], out, r * cols)
     zero = jnp.zeros((CH, CH), jnp.bfloat16)
 
     def banded(tiles):
@@ -170,20 +213,24 @@
             one_flip_out[ab, c] = tile
 
 
-def prepare(lines, kernel_one, kernel_two):
+def prepare(x, g, wa, wb, kernel_one, kernel_two):
+    rows, cols, lanes = x.shape
+    lines = rows + 4
     bands = jax.ShapeDtypeStruct((9, 4, CH, 2 * CH), jnp.bfloat16)
     select = ((lines + 1) * PAD + 18 * lines, 6 * lines)
+    windows = jax.ShapeDtypeStruct((2, rows * cols, 1024), jnp.bfloat16)
     vmem = pl.BlockSpec(memory_space=pltpu.VMEM)
     return pl.pallas_call(
         functools.partial(prepare_kernel, lines),
-        out_shape=(bands, bands, bands, jax.ShapeDtypeStruct(select, jnp.bfloat16)),
-        in_specs=[vmem] * 2,
-        out_specs=(vmem,) * 4,
-        compiler_params=pltpu.CompilerParams(vmem_limit_bytes=8 << 20),
+        out_shape=(*[bands] * 3, jax.ShapeDtypeStruct(select, jnp.bfloat16), windows, windows),
+        in_specs=[vmem] * 6,
+        out_specs=(vmem,) * 6,
+        scratch_shapes=line_scratch(2 * rows, cols, lanes),
+        compiler_params=pltpu.CompilerParams(vmem_limit_bytes=12 << 20),
         cost_estimate=pl.CostEstimate(
             flops=4_000_000, bytes_accessed=4_000_000, transcendentals=0
         ),
-    )(kernel_one, kernel_two)
+    )(x, g, wa, wb, kernel_one, kernel_two)
 
 
 def banded_weights(band_ref, group):
@@ -359,47 +406,69 @@
     return spread, gather_lines, put_wide, split_lanes
 
 
+def own_windows(own, ends, group, cols, shift):
+    if shift == 0:
+        return own[group]
+    count = own.shape[1]
+    if shift < 0:
+        return jnp.concatenate([ends[group, :cols, :], own[group, : count - cols, :]], axis=0)
+    return jnp.concatenate([own[group, cols:, :], ends[group, cols:, :]], axis=0)
+
+
+def correlate_own(own, ends, band_ref, cols, group):
+    windows = [own_windows(own, ends, group, cols, a - 1) for a in range(3)]
+    return jnp.dot(
+        jnp.concatenate(windows, axis=1),
+        banded_weights(band_ref, group),
+        preferred_element_type=jnp.float32,
+    )
+
+
 def main_kernel(
-    rows,
     cols,
-    x_ref,
-    g_ref,
     ra_ref,
     rb_ref,
-    wa_ref,
-    wb_ref,
     corner_a_ref,
     corner_b_ref,
-    select_ref,
+    xs,
+    gs,
     one_ref,
     two_flip_ref,
     grad_pre_ref,
     *rest,
 ):
     f32, bf16 = jnp.float32, jnp.bfloat16
-    kg_refs, scratch = rest[:-13], rest[-13:]
-    xs, gs, sums, acc_one, acc_two, turned_refs = *scratch[:5], scratch[5:7]
-    swap = scratch[7]
-    spread, _, _, _ = field_tools(
-        rows,
-        cols,
-        ra_ref,
-        rb_ref,
-        wa_ref,
-        wb_ref,
-        corner_a_ref,
-        corner_b_ref,
-        select_ref,
-        (scratch[8:10], scratch[10:12], scratch[12]),
-    )
-    lines = rows + 4
+    kg_refs, scratch = rest[:-10], rest[-10:]
+    x_ends, g_ends, sums, acc_one, acc_two, turned_refs = *scratch[:5], scratch[5:7]
+    swap, wide, wide_turned = scratch[7:]
     ha_odd = lax.rem(lax.axis_index("ha"), 2)
+    wa_odd = lax.rem(lax.axis_index("wa"), 2)
     nothing = lax.shift_right_logical(lax.axis_index("wa"), 16)
 
-    spread(0, x_ref, xs, None, [(1, lines - 1)])
-    pre = correlate(xs, None, one_ref, cols, [(2, rows)])
-    spread(1, g_ref, gs, None, [(1, lines - 1)])
-    grad_active = correlate(gs, None, two_flip_ref, cols, [(2, rows)])
+    def spread(which, out):
+        for slot, (odd_refs, even_refs, r) in enumerate(
+            (
+                ((ra_ref, corner_a_ref), (rb_ref, corner_b_ref), 1),
+                ((rb_ref, corner_b_ref), (ra_ref, corner_a_ref), 0),
+            )
+        ):
+            own, left, right = (
+                jnp.where(ha_odd == 1, odd.astype(f32), even.astype(f32))
+                for odd, even in (
+                    (odd_refs[0][which, r], even_refs[0][which, r]),
+                    *(
+                        (odd_refs[1][side, which, r], even_refs[1][side, which, r])
+                        for side in (1 - wa_odd, wa_odd)
+                    ),
+                )
+            )
+            at = 2 * which + slot
+            gather_line(wide, wide_turned, at, own, left[1:2], right[:1], out, slot * cols)
+
+    spread(0, x_ends)
+    spread(1, g_ends)
+    pre = [correlate_own(xs, x_ends, one_ref, cols, group) for group in range(2)]
+    grad_active = [correlate_own(gs, g_ends, two_flip_ref, cols, group) for group in range(2)]
 
     active_t, slopes = [], []
     for group in range(2):
@@ -412,7 +481,7 @@
     low_half = lax.broadcasted_iota(jnp.int32, (CH, 2 * CH), 1) < CH
     low = low_half[:half]
 
-    def kernel_grad_parts(fixed, src, acc_ref, a):
+    def kernel_grad_parts(fixed, acc_ref, a):
         parts = [[None] * 4 for _ in range(3)]
 
         def put(window, e, tile):
@@ -420,10 +489,9 @@
             parts[2 - window][e] = tile if old is None else old + tile
 
         for group in range(2):
-            top = (3 - a) * cols
-            acc_ref[...] = jnp.dot(
-                fixed[group], src[group, top : top + rows * cols, :], preferred_element_type=f32
-            )
+            window = own_windows(gs, g_ends, group, cols, 1 - a)
+            acc = acc_ref.at[group]
+            acc[...] = jnp.dot(fixed[group], window, preferred_element_type=f32)
             for j in range(4):
                 for t in range(8):
                     (window, i), (next_window, next_i) = divmod(2 * t, 5), divmod(2 * t + 1, 5)
@@ -434,7 +502,7 @@
                     use_right = not joined and 0 <= c < 3
                     if not (use_left or use_right):
                         continue
-                    tile = acc_ref[64 * j : 64 * j + 64, 128 * t : 128 * t + 128]
+                    tile = acc[64 * j : 64 * j + 64, 128 * t : 128 * t + 128]
                     if use_left:
                         whole = joined or e == 0
                         put(window, e, tile if whole else jnp.where(low_half, tile, 0.0))
@@ -457,7 +525,7 @@
                     pltpu.roll(left[half:], CH, 1) + right[half:],
                 )
 
-    def first_grad(fixed, src, a):
+    def first_grad(fixed, a):
         parts = [[None] * 4 for _ in range(3)]
 
         def put(window, e, tile):
@@ -465,11 +533,9 @@
             parts[window][e + 1] = tile if old is None else old + tile
 
         for group in range(2):
-            top = (a + 1) * cols
+            window = own_windows(xs, x_ends, group, cols, a - 1)
             acc_ref = acc_one.at[2 * a + group]
-            acc_ref[...] = jnp.dot(
-                fixed[group], src[group, top : top + rows * cols, :], preferred_element_type=f32
-            )
+            acc_ref[...] = jnp.dot(fixed[group], window, preferred_element_type=f32)
             for j in range(4):
                 for t in range(8):
                     (window, i), (next_window, next_i) = divmod(2 * t, 5), divmod(2 * t + 1, 5)
@@ -502,16 +568,16 @@
                     odd = slot[pl.ds(at + 1, half, stride=2), :]
                     put_tile(0, 9 * a + 3 * b + tap, even, pltpu.roll(odd, CH, 1))
 
-    for a in range(2):
-        add_taps(a, kernel_grad_parts(active_t, gs, acc_two.at[a], a))
+    add_taps(0, kernel_grad_parts(active_t, acc_two.at[0], 0))
     grad_pre_t = []
     for group in range(2):
         grad_pre = grad_active[group] * slopes[group]
         grad_pre_ref[:, 256 * group : 256 * group + 256] = grad_pre.astype(bf16)
         grad_pre_t.append(jnp.transpose(grad_pre).astype(bf16))
     for a in range(3):
-        first_grad(grad_pre_t, xs, a)
-    add_taps(2, kernel_grad_parts(active_t, gs, acc_two.at[2], 2))
+        first_grad(grad_pre_t, a)
+    for a in (1, 2):
+        add_taps(a, kernel_grad_parts(active_t, acc_two.at[a], a))
 
     if len(kg_refs) == 1:
         for k in range(2):
@@ -615,8 +681,8 @@
     return [*[wide] * (2 * fields), pltpu.VMEM((fields, 6 * (rows + 4), lanes), jnp.float32)]
 
 
-def main(fields, bands, split):
-    rows, cols, lanes = fields[0].shape
+def main(shape, operands, split):
+    rows, cols, lanes = shape
     if split:
         slabs, width = split
         take = 27 * CH // 2 // (2 * slabs * width)
@@ -628,29 +694,29 @@
     else:
         grads = (jax.ShapeDtypeStruct((2, 27 * CH // 2, 2 * CH), jnp.float32),)
     vmem = pl.BlockSpec(memory_space=pltpu.VMEM)
-    moving = pltpu.VMEM((2, (rows + 4) * cols, 1024), jnp.bfloat16)
+    ends = pltpu.VMEM((2, 2 * cols, 1024), jnp.bfloat16)
     turning = pltpu.VMEM((rows * cols // 128, 256, 128), jnp.float32)
     return pl.pallas_call(
-        functools.partial(main_kernel, rows, cols),
+        functools.partial(main_kernel, cols),
         out_shape=(jax.ShapeDtypeStruct((rows * cols, lanes), jnp.bfloat16), *grads),
-        in_specs=[vmem] * 11,
+        in_specs=[vmem] * 8,
         out_specs=(vmem,) * (1 + len(grads)),
         scratch_shapes=[
-            moving,
-            moving,
+            ends,
+            ends,
             pltpu.VMEM((2, 27 * CH // 2 + 40, 2 * CH), jnp.float32),
             pltpu.VMEM((6, 256, 1024), jnp.float32),
-            pltpu.VMEM((3, 256, 1024), jnp.float32),
+            pltpu.VMEM((3, 2, 256, 1024), jnp.float32),
             turning,
             turning,
             pltpu.VMEM((18, 2 * CH, 2 * CH), jnp.float32),
-            *scratch_shapes(rows, cols, lanes, 2),
+            *line_scratch(4, cols, lanes),
         ],
         compiler_params=pltpu.CompilerParams(vmem_limit_bytes=32 << 20),
         cost_estimate=pl.CostEstimate(
             flops=10_000_000_000, bytes_accessed=8_000_000, transcendentals=1_000_000
         ),
-    )(*fields, *bands)
+    )(*operands)
 
 
 def ring(fields, bands, grad_pre):
@@ -750,7 +816,6 @@
 
 
 def shards(inputs, grad_out, kernel_one, kernel_two):
-    rows, _, _ = inputs.shape
     height_count = lax.axis_size("ha")
     width_count = lax.axis_size("wa")
     devices = height_count * width_count
@@ -761,7 +826,7 @@
     wa = pair_exchange(own_a, "wa", 0)
     ra = pair_exchange(to_a, "ha", 0)
     rb = pair_exchange(to_b, "ha", 1)
-    one, two_flip, one_flip, select = prepare(rows + 4, kernel_one, kernel_two)
+    one, two_flip, one_flip, select, xs, gs = prepare(x, g, wa, wb, kernel_one, kernel_two)
     corner_to_a, corner_to_b = corners(wa, wb)
     corner_b = pair_exchange(corner_to_b, "ha", 1)
     corner_a = pair_exchange(corner_to_a, "ha", 0)
@@ -776,7 +841,8 @@
         split = (height_count // 2, width_count)
     fields = (x, g, ra, rb, wa, wb, corner_a, corner_b)
     bands = (select, one, two_flip)
-    grad_pre, *grads = main(fields, bands, split)
+    operands = (ra, rb, corner_a, corner_b, xs, gs, one, two_flip)
+    grad_pre, *grads = main(inputs.shape, operands, split)
     ps = ring(fields, bands, grad_pre)
     grad_inputs = input_grad(ps, one_flip, inputs.shape)
     if split:

time: 43.2 us -> 42.2 us (0.977)
  starting transfers between devices: 23 us -> 22.3 us
    ppermute x7, starting transfers between devices: 15.5 us -> 14.9 us  [xor_exchange(): return lax.ppermute(block, axis, [(i, i ^ mask) for i in range(count)])]
  transfers between devices with their start and end apart: 13 -> 13, of which waited for: 5 -> 5; matrix products, arithmetic and copies ran while one was open for 0% -> 0% of each run, Pallas kernels for 12% -> 13%
where the time goes in v6:
time: 42.2 us; the launch traced here: 42.1 us
  starting transfers between devices  22.3 us (53%)
  Pallas kernels  11.7 us (28%)
  waiting for transfers between devices  7.31 us (17%)
  between operations  0.74 us (2%)
    ppermute x7, starting transfers between devices, xor_exchange(): return lax.ppermute(block, axis, [(i, i ^ mask) for i in range(count)])  14.9 us
    ppermute x6, starting transfers between devices, pair_exchange(): return lax.ppermute(block, axis, pairs)  7.45 us
    ppermute x7, waiting for transfers between devices, xor_exchange(): return lax.ppermute(block, axis, [(i, i ^ mask) for i in range(count)])  6.23 us
    pallas_call x1, Pallas kernels, main(): pl.pallas_call(functools.partial(main_kernel, cols), out_shape=(jax.Shape...  4.02 us
    pallas_call x1, Pallas kernels, ring(): pl.pallas_call(functools.partial(ring_kernel, rows, cols), out_shape=jax....  2.43 us
    pallas_call x1, Pallas kernels, input_grad(): pl.pallas_call(functools.partial(input_grad_kernel, rows, cols), out_shap...  1.68 us
    pallas_call x1, Pallas kernels, prepare(): pl.pallas_call(functools.partial(prepare_kernel, lines), out_shape=(*[ban...  1.53 us
    pallas_call x1, Pallas kernels, pack(): pl.pallas_call(pack_kernel, out_shape=tuple((jax.ShapeDtypeStruct(shape,...  1.34 us
  transfers between devices with their start and end apart: 13, of which 5 were waited for; matrix products, arithmetic and copies ran while one was open for 0% of the time, Pallas kernels for 13%

profile of v6, /device:TPU:0, one launch (start us, length us, event | category | flops | bytes accessed | tf_op | source)
XLA Modules:
  0.0 42.1 jit_solution(8112632698717313845)
XLA Ops:
  0.6 1.3 %shard_map.67 = (bf16[4,64,512]{2,1,0:T(8,128)(2,1)S(1)}, bf16[4,64,512]{2,1,0:T(8,128)(2,1)S(1)}, bf16[27,64,64]{2,1,0:T(8,128)(2,1)S(1)}, bf16[27,64,64]{2,1,0...) custom-call(bf16[4,64,512]{2,1,0:T(8,128)(2,1)} %x_hbm.1, ...), custom_call_target="tpu_custom_call" | custom-call | bytes 1100000 | tf_op jit(solution)/shard_map/pallas_call | solution.py:63
  2.0 0.6 %collective-permute-start = (bf16[2,2,64,512]{3,2,1,0:T(8,128)(2,1)S(1)}, bf16[2,2,64,512]{3,2,1,0:T(8,128)(2,1)S(1)}, u32[]{:S(2)}, u32[]{:S(2)}) collective-permute-start(bf16[2,2,64,512]{3,2,1,0:T(8,128)(2,1)S(1)} %get-tuple-element.34), channel_id=1, source_target_pairs={{0,4},{4,0},{8,12},{12,8},{16,20},{20,16},{24,28},{28,24},{1,5},{5... | collective-permute-start | bytes 786440 | tf_op jit(solution)/shard_map/ppermute | solution.py:23
  2.5 0.7 %collective-permute-start.1 = (bf16[2,2,64,512]{3,2,1,0:T(8,128)(2,1)S(1)}, bf16[2,2,64,512]{3,2,1,0:T(8,128)(2,1)S(1)}, u32[]{:S(2)}, u32[]{:S(2)}) collective-permute-start(bf16[2,2,64,512]{3,2,1,0:T(8,128)(2,1)S(1)} %get-tuple-element.35), channel_id=1, source_target_pairs={{4,8},{8,4},{12,16},{16,12},{20,24},{24,20},{5,9},{9,5},{13,17},{1... | collective-permute-start | bytes 786440 | tf_op jit(solution)/shard_map/ppermute | solution.py:23
  3.2 2.6 %collective-permute-start.2 = (bf16[2,4,2,512]{3,2,1,0:T(2,128)(2,1)S(1)}, bf16[2,4,2,512]{3,2,1,0:T(2,128)(2,1)S(1)}, u32[]{:S(2)}, u32[]{:S(2)}) collective-permute-start(bf16[2,4,2,512]{3,2,1,0:T(2,128)(2,1)S(1)} %get-tuple-element.36), channel_id=1, source_target_pairs={{0,1},{1,0},{2,3},{3,2},{4,5},{5,4},{6,7},{7,6},{8,9},{9,8},{10,11... | collective-permute-start | bytes 49160 | tf_op jit(solution)/shard_map/ppermute | solution.py:23
  5.8 0.7 %collective-permute-start.3 = (bf16[2,4,2,512]{3,2,1,0:T(2,128)(2,1)S(1)}, bf16[2,4,2,512]{3,2,1,0:T(2,128)(2,1)S(1)}, u32[]{:S(2)}, u32[]{:S(2)}) collective-permute-start(bf16[2,4,2,512]{3,2,1,0:T(2,128)(2,1)S(1)} %get-tuple-element.37), channel_id=1, source_target_pairs={{1,2},{2,1},{5,6},{6,5},{9,10},{10,9},{13,14},{14,13},{17,18},{18,... | collective-permute-start | bytes 49160 | tf_op jit(solution)/shard_map/ppermute | solution.py:23
  6.4 1.1 %collective-permute-done.2.wa_ref = bf16[2,4,2,512]{3,2,1,0:T(2,128)(2,1)S(1)} collective-permute-done((bf16[2,4,2,512]{3,2,1,0:T(2,128)(2,1)S(1)}, bf16[2,4,2,512]{3,2,1,0:T(2,128)(2,1)S(1)}, u32[]{:S(2)}, u32[]{:S(2)}) %collective-permute-start.2) | collective-permute-done | bytes 16416 | tf_op jit(solution)/shard_map/ppermute | solution.py:23
  7.5 0.0 collective-permute-done.3.wb_ref
  7.5 2.4 %collective-permute-start.4 = (bf16[2,2,2,2,512]{4,3,2,1,0:T(2,128)(2,1)S(1)}, bf16[2,2,2,2,512]{4,3,2,1,0:T(2,128)(2,1)S(1)}, u32[]{:S(2)}, u32[]{:S(2)}) collective-permute-start(bf16[2,2,2,2,512]{4,3,2,1,0:T(2,128)(2,1)S(1)} %get-tuple-element.38), channel_id=1, source_target_pairs={{0,4},{4,0},{8,12},{12,8},{16,20},{20,16},{24,28},{28,24},{1,5},{5... | collective-permute-start | bytes 49160 | tf_op jit(solution)/shard_map/ppermute | solution.py:23
  9.9 0.7 %collective-permute-start.5 = (bf16[2,2,2,2,512]{4,3,2,1,0:T(2,128)(2,1)S(1)}, bf16[2,2,2,2,512]{4,3,2,1,0:T(2,128)(2,1)S(1)}, u32[]{:S(2)}, u32[]{:S(2)}) collective-permute-start(bf16[2,2,2,2,512]{4,3,2,1,0:T(2,128)(2,1)S(1)} %get-tuple-element.39), channel_id=1, source_target_pairs={{4,8},{8,4},{12,16},{16,12},{20,24},{24,20},{5,9},{9,5},{13,17},{1... | collective-permute-start | bytes 49160 | tf_op jit(solution)/shard_map/ppermute | solution.py:23
  10.5 1.5 %shard_map.69 = (bf16[9,4,64,128]{3,2,1,0:T(8,128)(2,1)S(1)}, bf16[9,4,64,128]{3,2,1,0:T(8,128)(2,1)S(1)}, bf16[9,4,64,128]{3,2,1,0:T(8,128)(2,1)S(1)}, bf16[288...) custom-call(bf16[4,64,512]{2,1,0:T(8,128)(2,1)S(1)} %get-tuple-element.32.x_ref, ...), custom_call_target="tpu_custom_call" | custom-call | flops 4000000 | bytes 4000000 | tf_op jit(solution)/shard_map/pallas_call | solution.py:223
  12.1 0.0 collective-permute-done.4.corner_a_ref
  12.1 0.0 collective-permute-done.5.corner_b_ref
  12.1 0.0 collective-permute-done.ra_ref
  12.1 0.0 collective-permute-done.1.rb_ref
  12.1 4.0 %shard_map.70 = (bf16[256,512]{1,0:T(8,128)(2,1)S(1)}, f32[4,4,56,128]{3,2,1,0:T(8,128)S(1)}, bf16[4,4,56,128]{3,2,1,0:T(8,128)(2,1)S(1)}) custom-call(bf16[2,2,64,512]{3,2,1,0:T(8,128)(2,1)S(1)} %collective-permute-done.ra_ref, bf16[2,2,64,512]{3,2,1,0:T(8,128)(2,1)S(1)} %collective-permute-done.1.rb_ref, ...), custom_call_target="tpu_custom_call" | custom-call | flops 10000000000 | bytes 8000000 | tf_op jit(solution)/shard_map/pallas_call | solution.py:699
  16.1 3.3 %collective-permute-start.6 = (bf16[4,4,56,128]{3,2,1,0:T(8,128)(2,1)S(1)}, bf16[4,4,56,128]{3,2,1,0:T(8,128)(2,1)S(1)}, u32[]{:S(2)}, u32[]{:S(2)}) collective-permute-start(bf16[4,4,56,128]{3,2,1,0:T(8,128)(2,1)S(1)} %get-tuple-element.50), channel_id=1, source_target_pairs={{0,4},{4,0},{8,12},{12,8},{16,20},{20,16},{24,28},{28,24},{1,5},{5... | collective-permute-start | bytes 688136 | tf_op jit(solution)/shard_map/ppermute | solution.py:763
  19.4 1.1 %collective-permute-done.6.got_ref = bf16[4,4,56,128]{3,2,1,0:T(8,128)(2,1)S(1)} collective-permute-done((bf16[4,4,56,128]{3,2,1,0:T(8,128)(2,1)S(1)}, bf16[4,4,56,128]{3,2,1,0:T(8,128)(2,1)S(1)}, u32[]{:S(2)}, u32[]{:S(2)}) %collective-permute-start.6) | collective-permute-done | bytes 229408 | tf_op jit(solution)/shard_map/ppermute | solution.py:763
  20.5 0.1 shard_map.73
  20.6 4.2 %collective-permute-start.7 = (bf16[4,56,128]{2,1,0:T(8,128)(2,1)S(1)}, bf16[4,56,128]{2,1,0:T(8,128)(2,1)S(1)}, u32[]{:S(2)}, u32[]{:S(2)}) collective-permute-start(bf16[4,56,128]{2,1,0:T(8,128)(2,1)S(1)} %get-tuple-element.52), channel_id=1, source_target_pairs={{0,1},{1,0},{2,3},{3,2},{4,5},{5,4},{6,7},{7,6},{8,9},{9,8},{10,11... | collective-permute-start | bytes 172040 | tf_op jit(solution)/shard_map/ppermute | solution.py:763
  24.8 1.4 %collective-permute-start.8 = (bf16[4,56,128]{2,1,0:T(8,128)(2,1)S(1)}, bf16[4,56,128]{2,1,0:T(8,128)(2,1)S(1)}, u32[]{:S(2)}, u32[]{:S(2)}) collective-permute-start(bf16[4,56,128]{2,1,0:T(8,128)(2,1)S(1)} %get-tuple-element.53), channel_id=1, source_target_pairs={{0,2},{1,3},{2,0},{3,1},{4,6},{5,7},{6,4},{7,5},{8,10},{9,11},{10,... | collective-permute-start | bytes 172040 | tf_op jit(solution)/shard_map/ppermute | solution.py:763
  26.3 1.4 %collective-permute-start.9 = (bf16[4,56,128]{2,1,0:T(8,128)(2,1)S(1)}, bf16[4,56,128]{2,1,0:T(8,128)(2,1)S(1)}, u32[]{:S(2)}, u32[]{:S(2)}) collective-permute-start(bf16[4,56,128]{2,1,0:T(8,128)(2,1)S(1)} %get-tuple-element.54), channel_id=1, source_target_pairs={{0,3},{1,2},{2,1},{3,0},{4,7},{5,6},{6,5},{7,4},{8,11},{9,10},{10,... | collective-permute-start | bytes 172040 | tf_op jit(solution)/shard_map/ppermute | solution.py:763
  27.7 2.4 %shard_map.71.ps = bf16[2,512,1024]{2,1,0:T(8,128)(2,1)S(1)} custom-call(bf16[4,64,512]{2,1,0:T(8,128)(2,1)S(1)} %get-tuple-element.32.x_ref, bf16[4,64,512]{2,1,0:T(8,128)(2,1)S(1)} %get-tuple-element.33.g_ref, bf16[2,2,64,512]{3,2,1,0:T(8,128)(2,1)S(1)} %collective-permute-done.ra_ref, bf16[2,2,64,512]{3,2,1,0:T(8,128)(2,1)S(1)} %collective-permute-done.1.rb_ref, ...), custom_call_target="tpu_custom_call" | custom-call | flops 3000000000 | bytes 8000000 | tf_op jit(solution)/shard_map/pallas_call | solution.py:727
  30.1 0.0 collective-permute-done.7.refs_1_
  30.1 0.0 collective-permute-done.8.refs_2_
  30.1 1.2 %collective-permute-done.9.refs_3_ = bf16[4,56,128]{2,1,0:T(8,128)(2,1)S(1)} collective-permute-done((bf16[4,56,128]{2,1,0:T(8,128)(2,1)S(1)}, bf16[4,56,128]{2,1,0:T(8,128)(2,1)S(1)}, u32[]{:S(2)}, u32[]{:S(2)}) %collective-permute-start.9) | collective-permute-done | bytes 57376 | tf_op jit(solution)/shard_map/ppermute | solution.py:763
  31.4 2.0 %collective-permute-start.10 = (f32[56,128]{1,0:T(8,128)S(1)}, f32[56,128]{1,0:T(8,128)S(1)}, u32[]{:S(2)}, u32[]{:S(2)}) collective-permute-start(f32[56,128]{1,0:T(8,128)S(1)} %get-tuple-element.56), channel_id=1, source_target_pairs={{0,8},{4,12},{8,0},{12,4},{16,24},{20,28},{24,16},{28,20},{1,9},{5... | collective-permute-start | bytes 86024 | tf_op jit(solution)/shard_map/ppermute | solution.py:763
  33.4 2.4 %collective-permute-start.11 = (f32[56,128]{1,0:T(8,128)S(1)}, f32[56,128]{1,0:T(8,128)S(1)}, u32[]{:S(2)}, u32[]{:S(2)}) collective-permute-start(f32[56,128]{1,0:T(8,128)S(1)} %get-tuple-element.57), channel_id=1, source_target_pairs={{0,16},{4,20},{8,24},{12,28},{16,0},{20,4},{24,8},{28,12},{1,17},{... | collective-permute-start | bytes 86024 | tf_op jit(solution)/shard_map/ppermute | solution.py:763
  35.8 0.1 collective-permute-start.12
  35.9 1.7 %shard_map.72 = bf16[4,64,512]{2,1,0:T(8,128)(2,1)} custom-call(bf16[2,512,1024]{2,1,0:T(8,128)(2,1)S(1)} %shard_map.71.ps, bf16[9,4,64,128]{3,2,1,0:T(8,128)(2,1)S(1)} %get-tuple-element.48.band_ref), custom_call_target="tpu_custom_call" | custom-call | flops 2000000000 | bytes 4000000 | tf_op jit(solution)/shard_map/pallas_call | solution.py:749
  37.6 0.0 collective-permute-done.10.refs_1_
  37.6 0.8 %collective-permute-done.11.refs_2_ = f32[56,128]{1,0:T(8,128)S(1)} collective-permute-done((f32[56,128]{1,0:T(8,128)S(1)}, f32[56,128]{1,0:T(8,128)S(1)}, u32[]{:S(2)}, u32[]{:S(2)}) %collective-permute-start.11) | collective-permute-done | bytes 28704 | tf_op jit(solution)/shard_map/ppermute | solution.py:763
  38.3 3.1 %collective-permute-done.12.refs_3_ = f32[56,128]{1,0:T(8,128)S(1)} collective-permute-done((f32[56,128]{1,0:T(8,128)S(1)}, f32[56,128]{1,0:T(8,128)S(1)}, u32[]{:S(2)}, u32[]{:S(2)}) %collective-permute-start.12) | collective-permute-done | bytes 28704 | tf_op jit(solution)/shard_map/ppermute | solution.py:763
  41.4 0.6 %shard_map.75 = (f32[27,128]{1,0:T(8,128)}, f32[27,128]{1,0:T(8,128)}) custom-call(f32[56,128]{1,0:T(8,128)S(1)} %get-tuple-element.55.refs_0_, f32[56,128]{1,0:T(8,128)S(1)} %collective-permute-done.10.refs_1_, f32[56,128]{1,0:T(8,128)S(1)} %collective-permute-done.11.refs_2_, f32[56,128]{1,0:T(8,128)S(1)} %collective-permute-done.12.refs_3_), custom_call_target="tpu_custom_call" | custom-call | bytes 300000 | tf_op jit(solution)/shard_map/pallas_call | solution.py:88
  (2 shorter events, 0.0 us)
Async XLA Ops:
  2.0 10.1 %collective-permute-start = (bf16[2,2,64,512]{3,2,1,0:T(8,128)(2,1)S(1)}, bf16[2,2,64,512]{3,2,1,0:T(8,128)(2,1)S(1)}, u32[]{:S(2)}, u32[]{:S(2)}) collective-permute-start(bf16[2,2,64,512]{3,2,1,0:T(8,128)(2,1)S(1)} %get-tuple-element.34), channel_id=1, source_target_pairs={{0,4},{4,0},{8,12},{12,8},{16,20},{20,16},{24,28},{28,24},{1,5},{5... | collective-permute-start | bytes 786440 | tf_op jit(solution)/shard_map/ppermute | solution.py:23
  2.5 9.6 %collective-permute-start.1 = (bf16[2,2,64,512]{3,2,1,0:T(8,128)(2,1)S(1)}, bf16[2,2,64,512]{3,2,1,0:T(8,128)(2,1)S(1)}, u32[]{:S(2)}, u32[]{:S(2)}) collective-permute-start(bf16[2,2,64,512]{3,2,1,0:T(8,128)(2,1)S(1)} %get-tuple-element.35), channel_id=1, source_target_pairs={{4,8},{8,4},{12,16},{16,12},{20,24},{24,20},{5,9},{9,5},{13,17},{1... | collective-permute-start | bytes 786440 | tf_op jit(solution)/shard_map/ppermute | solution.py:23
  3.2 4.3 %collective-permute-start.2 = (bf16[2,4,2,512]{3,2,1,0:T(2,128)(2,1)S(1)}, bf16[2,4,2,512]{3,2,1,0:T(2,128)(2,1)S(1)}, u32[]{:S(2)}, u32[]{:S(2)}) collective-permute-start(bf16[2,4,2,512]{3,2,1,0:T(2,128)(2,1)S(1)} %get-tuple-element.36), channel_id=1, source_target_pairs={{0,1},{1,0},{2,3},{3,2},{4,5},{5,4},{6,7},{7,6},{8,9},{9,8},{10,11... | collective-permute-start | bytes 49160 | tf_op jit(solution)/shard_map/ppermute | solution.py:23
  5.8 1.7 %collective-permute-start.3 = (bf16[2,4,2,512]{3,2,1,0:T(2,128)(2,1)S(1)}, bf16[2,4,2,512]{3,2,1,0:T(2,128)(2,1)S(1)}, u32[]{:S(2)}, u32[]{:S(2)}) collective-permute-start(bf16[2,4,2,512]{3,2,1,0:T(2,128)(2,1)S(1)} %get-tuple-element.37), channel_id=1, source_target_pairs={{1,2},{2,1},{5,6},{6,5},{9,10},{10,9},{13,14},{14,13},{17,18},{18,... | collective-permute-start | bytes 49160 | tf_op jit(solution)/shard_map/ppermute | solution.py:23
  7.5 4.6 %collective-permute-start.4 = (bf16[2,2,2,2,512]{4,3,2,1,0:T(2,128)(2,1)S(1)}, bf16[2,2,2,2,512]{4,3,2,1,0:T(2,128)(2,1)S(1)}, u32[]{:S(2)}, u32[]{:S(2)}) collective-permute-start(bf16[2,2,2,2,512]{4,3,2,1,0:T(2,128)(2,1)S(1)} %get-tuple-element.38), channel_id=1, source_target_pairs={{0,4},{4,0},{8,12},{12,8},{16,20},{20,16},{24,28},{28,24},{1,5},{5... | collective-permute-start | bytes 49160 | tf_op jit(solution)/shard_map/ppermute | solution.py:23
  9.9 2.2 %collective-permute-start.5 = (bf16[2,2,2,2,512]{4,3,2,1,0:T(2,128)(2,1)S(1)}, bf16[2,2,2,2,512]{4,3,2,1,0:T(2,128)(2,1)S(1)}, u32[]{:S(2)}, u32[]{:S(2)}) collective-permute-start(bf16[2,2,2,2,512]{4,3,2,1,0:T(2,128)(2,1)S(1)} %get-tuple-element.39), channel_id=1, source_target_pairs={{4,8},{8,4},{12,16},{16,12},{20,24},{24,20},{5,9},{9,5},{13,17},{1... | collective-permute-start | bytes 49160 | tf_op jit(solution)/shard_map/ppermute | solution.py:23
  16.1 4.4 %collective-permute-start.6 = (bf16[4,4,56,128]{3,2,1,0:T(8,128)(2,1)S(1)}, bf16[4,4,56,128]{3,2,1,0:T(8,128)(2,1)S(1)}, u32[]{:S(2)}, u32[]{:S(2)}) collective-permute-start(bf16[4,4,56,128]{3,2,1,0:T(8,128)(2,1)S(1)} %get-tuple-element.50), channel_id=1, source_target_pairs={{0,4},{4,0},{8,12},{12,8},{16,20},{20,16},{24,28},{28,24},{1,5},{5... | collective-permute-start | bytes 688136 | tf_op jit(solution)/shard_map/ppermute | solution.py:763
  20.6 9.5 %collective-permute-start.7 = (bf16[4,56,128]{2,1,0:T(8,128)(2,1)S(1)}, bf16[4,56,128]{2,1,0:T(8,128)(2,1)S(1)}, u32[]{:S(2)}, u32[]{:S(2)}) collective-permute-start(bf16[4,56,128]{2,1,0:T(8,128)(2,1)S(1)} %get-tuple-element.52), channel_id=1, source_target_pairs={{0,1},{1,0},{2,3},{3,2},{4,5},{5,4},{6,7},{7,6},{8,9},{9,8},{10,11... | collective-permute-start | bytes 172040 | tf_op jit(solution)/shard_map/ppermute | solution.py:763
  24.8 5.3 %collective-permute-start.8 = (bf16[4,56,128]{2,1,0:T(8,128)(2,1)S(1)}, bf16[4,56,128]{2,1,0:T(8,128)(2,1)S(1)}, u32[]{:S(2)}, u32[]{:S(2)}) collective-permute-start(bf16[4,56,128]{2,1,0:T(8,128)(2,1)S(1)} %get-tuple-element.53), channel_id=1, source_target_pairs={{0,2},{1,3},{2,0},{3,1},{4,6},{5,7},{6,4},{7,5},{8,10},{9,11},{10,... | collective-permute-start | bytes 172040 | tf_op jit(solution)/shard_map/ppermute | solution.py:763
  26.3 5.1 %collective-permute-start.9 = (bf16[4,56,128]{2,1,0:T(8,128)(2,1)S(1)}, bf16[4,56,128]{2,1,0:T(8,128)(2,1)S(1)}, u32[]{:S(2)}, u32[]{:S(2)}) collective-permute-start(bf16[4,56,128]{2,1,0:T(8,128)(2,1)S(1)} %get-tuple-element.54), channel_id=1, source_target_pairs={{0,3},{1,2},{2,1},{3,0},{4,7},{5,6},{6,5},{7,4},{8,11},{9,10},{10,... | collective-permute-start | bytes 172040 | tf_op jit(solution)/shard_map/ppermute | solution.py:763
  31.4 6.2 %collective-permute-start.10 = (f32[56,128]{1,0:T(8,128)S(1)}, f32[56,128]{1,0:T(8,128)S(1)}, u32[]{:S(2)}, u32[]{:S(2)}) collective-permute-start(f32[56,128]{1,0:T(8,128)S(1)} %get-tuple-element.56), channel_id=1, source_target_pairs={{0,8},{4,12},{8,0},{12,4},{16,24},{20,28},{24,16},{28,20},{1,9},{5... | collective-permute-start | bytes 86024 | tf_op jit(solution)/shard_map/ppermute | solution.py:763
  33.4 4.9 %collective-permute-start.11 = (f32[56,128]{1,0:T(8,128)S(1)}, f32[56,128]{1,0:T(8,128)S(1)}, u32[]{:S(2)}, u32[]{:S(2)}) collective-permute-start(f32[56,128]{1,0:T(8,128)S(1)} %get-tuple-element.57), channel_id=1, source_target_pairs={{0,16},{4,20},{8,24},{12,28},{16,0},{20,4},{24,8},{28,12},{1,17},{... | collective-permute-start | bytes 86024 | tf_op jit(solution)/shard_map/ppermute | solution.py:763
  35.8 5.7 %collective-permute-start.12 = (f32[56,128]{1,0:T(8,128)S(1)}, f32[56,128]{1,0:T(8,128)S(1)}, u32[]{:S(2)}, u32[]{:S(2)}) collective-permute-start(f32[56,128]{1,0:T(8,128)S(1)} %get-tuple-element.58), channel_id=1, source_target_pairs={{0,24},{4,28},{8,16},{12,20},{16,8},{20,12},{24,0},{28,4},{1,25},{... | collective-permute-start | bytes 86024 | tf_op jit(solution)/shard_map/ppermute | solution.py:763
